TPU v7x, 512 devices: a whole 4x4x16 slice. The times are simulated.
512 devices in a mesh: row: 32 (over z_lo, y), col: 16 (over z_hi, x, core).
Axes of the slice: x: 4, y: 4, z: 16 (z_hi: 2, z_lo: 8; z = z_hi * 8 + z_lo), core: 2. Of those that a mesh axis runs over, the one named last changes fastest.
Arguments:
- tile_values: bfloat16 [32, 16, 4, 256, 256], P('row', 'col'), may hold values from -0.125 to 0.125
- tile_row: int32 [32, 16, 4], P('row', 'col'), may hold values from 0 to 15
- tile_col: int32 [32, 16, 4], P('row', 'col'), may hold values from 0 to 31
- basis_init: bfloat16 [32, 131072], P(None, ('col', 'row')), may hold values from -6 to 6
Outputs:
- ritz_basis: float32 [32, 131072], P(None, ('col', 'row'))
- residual: float32 [32, 131072], P(None, ('col', 'row'))
- projected: float32 [32, 32], replicated
Inputs may be any that keep to these rules, and one draw needn't show every extreme that they name: `tile_row`: coordinates may repeat within a pair of blocks; repeated tiles add. `tile_col`: coordinates may repeat within a pair of blocks; repeated tiles add.
All inputs are finite; a program needn't handle non-finite values.
Results may differ from a plain program's by a relative error of at most 0.013.
Values may be sent and summed in bfloat16 or wider, within the bound.
No kernel may reach another device: no remote copies, remote signals or barrier semaphores. Data moves between devices by JAX's collectives and lax.ppermute only.
A program may use at most 64 MiB of HBM per device.

v0:
```python
import functools

import jax
import jax.numpy as jnp
from jax import lax
from jax.sharding import Mesh
from jax.sharding import PartitionSpec as P

COL = ("col_0", "col_1", "col_2")
ROW = ("row_0", "row_1")
ROW_COL = ("row_0", "row_1", "col_0", "col_1", "col_2")
COL_ROW = ("col_0", "col_1", "col_2", "row_0", "row_1")


def sent_to_all(value, axis):
    length = lax.axis_size(axis)
    return lax.all_to_all(
        jnp.broadcast_to(value[None], (length, *value.shape)), axis, 0, 0, tiled=True
    )


def laid_out(parts, dim):
    parts = jnp.moveaxis(parts, 0, dim)
    lengths = parts.shape
    return parts.reshape(*lengths[:dim], lengths[dim] * lengths[dim + 1], *lengths[dim + 2 :])


def collect(value, axis, dim):
    parts = sent_to_all(value, axis)
    return laid_out(parts, dim)


def split_up(value, dim, length):
    before, after = (value.shape[:dim], value.shape[dim + 1 :])
    return jnp.moveaxis(value.reshape(*before, length, -1, *after), dim, 0)


def summed_on_arrival(value, axis, dim):
    parts = split_up(value, dim, lax.axis_size(axis))
    arrived = lax.all_to_all(parts, axis, split_axis=0, concat_axis=0, tiled=True)
    return arrived.astype(jnp.float32).sum(axis=0)


def by_axis(value, axes):
    return functools.reduce(lax.psum, axes, value)


def exact_dot(left, right):
    return jnp.dot(left, right, precision=lax.Precision.HIGHEST)


def bucket(contrib, index, slots):
    tile_size = contrib.shape[-1]
    onehot_table = (index[:, None] == jnp.arange(slots, dtype=jnp.int32)[None, :]).astype(
        jnp.float32
    )
    summed = jnp.einsum("ktb,tn->knb", contrib, onehot_table, precision=lax.Precision.HIGHEST)
    return summed.reshape(contrib.shape[0], slots * tile_size)


def apply_hamiltonian(tile_block, tile_rows, tile_cols, vectors_bf):
    vector_count = vectors_bf.shape[0]
    local_rows = vectors_bf.shape[1]
    tile_size = tile_block.shape[-1]
    row_tiles = lax.axis_size(COL) * local_rows // tile_size
    col_tiles = lax.axis_size(ROW) * local_rows // tile_size
    column_block = collect(vectors_bf, ROW, 1)
    row_block = collect(vectors_bf, COL, 1)
    picked = column_block.reshape(vector_count, col_tiles, tile_size)[:, tile_cols]
    direct = jnp.einsum("ktj,tij->kti", picked, tile_block, preferred_element_type=jnp.float32)
    mirror_pick = row_block.reshape(vector_count, row_tiles, tile_size)[:, tile_rows]
    mirror = jnp.einsum("kti,tij->ktj", mirror_pick, tile_block, preferred_element_type=jnp.float32)
    direct_part = bucket(direct, tile_rows, row_tiles)
    mirror_part = bucket(mirror, tile_cols, col_tiles)
    own_direct = summed_on_arrival(direct_part.astype(jnp.bfloat16), COL, 1)
    own_mirror = summed_on_arrival(mirror_part.astype(jnp.bfloat16), ROW, 1)
    return own_direct + own_mirror


def shards(tile_values, tile_row, tile_col, basis_init):
    tile_block = tile_values[0, 0]
    tile_rows = tile_row[0, 0]
    tile_cols = tile_col[0, 0]
    total_rows = basis_init.shape[1] * lax.axis_size(ROW) * lax.axis_size(COL)
    current = basis_init
    ritz_basis = basis_init.astype(jnp.float32)
    product_block = apply_hamiltonian(tile_block, tile_rows, tile_cols, current)
    gram_matrix = by_axis(exact_dot(product_block, product_block.T), ROW_COL) / total_rows
    factor = jnp.linalg.cholesky(gram_matrix)
    ritz_basis = lax.linalg.triangular_solve(factor, product_block, left_side=True, lower=True)
    current = ritz_basis.astype(jnp.bfloat16)
    product_block = apply_hamiltonian(tile_block, tile_rows, tile_cols, current)
    projected = by_axis(exact_dot(ritz_basis, product_block.T), ROW_COL) / total_rows
    residual = product_block - exact_dot(projected.T, ritz_basis)
    return (ritz_basis, residual, projected)


def solution(mesh):
    finer = Mesh(mesh.devices.reshape(8, 4, 2, 4, 2), ("row_0", "row_1", "col_0", "col_1", "col_2"))
    placed = (P(ROW, COL, None, None, None), P(ROW, COL, None), P(ROW, COL, None), P(None, COL_ROW))
    return jax.shard_map(
        shards,
        mesh=finer,
        in_specs=placed,
        out_specs=(P(None, COL_ROW), P(None, COL_ROW), P()),
        check_vma=False,
    )
```

profile of v0, /device:TPU:1, one launch (start us, length us, event | category | flops | bytes accessed | tf_op | source)
XLA Modules:
  0.0 490.1 jit_solution(5127178967336358442)
XLA Ops:
  1.5 42.6 %all_to_all.40 = bf16[32,32,256]{2,1,0:T(8,128)(2,1)S(1)} all-to-all(bf16[32,32,256]{2,1,0:T(8,128)(2,1)S(1)} %broadcast_in_dim.9), channel_id=1, replica_groups=mesh['row_0'=8,'row_1'=4,'col_0'=2,'col_1'=4,'col_2'=2] {'row_0','row_1'}, dimensions={0} | all-to-all | bytes 1048576 | tf_op jit(solution)/shard_map/all_to_all | solution.py:17
  44.8 14.0 %all-to-all-start.2 = ((bf16[16,32,256]{2,1,0:T(8,128)(2,1)}), bf16[16,32,256]{2,1,0:T(8,128)(2,1)S(1)}, u32[]{:S(2)}, u32[]{:S(2)}) async-start(bf16[16,32,256]{2,1,0:T(8,128)(2,1)} %broadcast_in_dim.10), calls=%async_computation.2 | async-start | bytes 524288 | tf_op jit(solution)/shard_map/all_to_all | solution.py:17
  61.7 13.2 %all-to-all-done.2 = bf16[16,32,256]{2,1,0:T(8,128)(2,1)S(1)} async-done(((bf16[16,32,256]{2,1,0:T(8,128)(2,1)}), bf16[16,32,256]{2,1,0:T(8,128)(2,1)S(1)}, u32[]{:S(2)}, u32[]{:S(2)}) %all-to-all-start.2) | async-done | bytes 262176 | tf_op jit(solution)/shard_map/all_to_all | solution.py:17
  74.9 4.4 all-to-all-start.1
  81.9 13.5 %all-to-all-done.1 = bf16[16,32,256]{2,1,0:T(8,128)(2,1)S(1)} async-done(((bf16[16,32,256]{2,1,0:T(8,128)(2,1)}), bf16[16,32,256]{2,1,0:T(8,128)(2,1)S(1)}, u32[]{:S(2)}, u32[]{:S(2)}) %all-to-all-start.1) | async-done | bytes 262176 | tf_op jit(solution)/shard_map/all_to_all | solution.py:40
  95.4 18.8 %all-to-all-start.3 = ((bf16[32,32,256]{2,1,0:T(8,128)(2,1)}), bf16[32,32,256]{2,1,0:T(8,128)(2,1)S(1)}, u32[]{:S(2)}, u32[]{:S(2)}) async-start(bf16[32,32,256]{2,1,0:T(8,128)(2,1)} %copy.12), calls=%async_computation.3 | async-start | bytes 1048576 | tf_op jit(solution)/shard_map/all_to_all | solution.py:40
  114.2 26.7 %all-to-all-done.3 = bf16[32,32,256]{2,1,0:T(8,128)(2,1)S(1)} async-done(((bf16[32,32,256]{2,1,0:T(8,128)(2,1)}), bf16[32,32,256]{2,1,0:T(8,128)(2,1)S(1)}, u32[]{:S(2)}, u32[]{:S(2)}) %all-to-all-start.3) | async-done | bytes 524320 | tf_op jit(solution)/shard_map/all_to_all | solution.py:40
  141.2 47.4 %psum.70 = f32[32,32]{0,1:T(8,128)S(1)} all-reduce(f32[32,32]{0,1:T(8,128)S(1)} %fusion.37), channel_id=1, replica_groups=mesh['row_0'=8,'row_1'=4,'col_0'=2,'col_1'=4,'col_2'=2] {'row_0'}, use_global_device_ids=true, to_apply=%region_2.0 | all-reduce | flops 1024 | bytes 8192 | tf_op jit(solution)/shard_map/psum | solution.py:45
  188.7 12.6 %psum.71 = f32[32,32]{0,1:T(8,128)S(1)} all-reduce(f32[32,32]{0,1:T(8,128)S(1)} %psum.70), channel_id=1, replica_groups=mesh['row_0'=8,'row_1'=4,'col_0'=2,'col_1'=4,'col_2'=2] {'row_1'}, use_global_device_ids=true, to_apply=%region_3.0 | all-reduce | flops 1024 | bytes 8192 | tf_op jit(solution)/shard_map/psum | solution.py:45
  201.3 13.8 %psum.72 = f32[32,32]{0,1:T(8,128)S(1)} all-reduce(f32[32,32]{0,1:T(8,128)S(1)} %psum.71), channel_id=1, replica_groups=mesh['row_0'=8,'row_1'=4,'col_0'=2,'col_1'=4,'col_2'=2] {'col_0'}, use_global_device_ids=true, to_apply=%region_4.0 | all-reduce | flops 1024 | bytes 8192 | tf_op jit(solution)/shard_map/psum | solution.py:45
  215.1 12.8 %psum.73 = f32[32,32]{0,1:T(8,128)S(1)} all-reduce(f32[32,32]{0,1:T(8,128)S(1)} %psum.72), channel_id=1, replica_groups=mesh['row_0'=8,'row_1'=4,'col_0'=2,'col_1'=4,'col_2'=2] {'col_1'}, use_global_device_ids=true, to_apply=%region_5.0 | all-reduce | flops 1024 | bytes 8192 | tf_op jit(solution)/shard_map/psum | solution.py:45
  227.9 19.3 %psum.74 = f32[32,32]{0,1:T(8,128)S(1)} all-reduce(f32[32,32]{0,1:T(8,128)S(1)} %psum.73), channel_id=1, replica_groups=mesh['row_0'=8,'row_1'=4,'col_0'=2,'col_1'=4,'col_2'=2] {'col_2'}, use_global_device_ids=true, to_apply=%region_6.0 | all-reduce | flops 1024 | bytes 8192 | tf_op jit(solution)/shard_map/psum | solution.py:45
  254.2 30.8 %all_to_all.41 = bf16[32,32,256]{2,1,0:T(8,128)(2,1)S(1)} all-to-all(bf16[32,32,256]{2,1,0:T(8,128)(2,1)S(1)} %broadcast_in_dim.11), channel_id=1, replica_groups=mesh['row_0'=8,'row_1'=4,'col_0'=2,'col_1'=4,'col_2'=2] {'row_0','row_1'}, dimensions={0} | all-to-all | bytes 1048576 | tf_op jit(solution)/shard_map/all_to_all | solution.py:17
  285.8 14.5 %all-to-all-start.6 = ((bf16[16,32,256]{2,1,0:T(8,128)(2,1)}), bf16[16,32,256]{2,1,0:T(8,128)(2,1)S(1)}, u32[]{:S(2)}, u32[]{:S(2)}) async-start(bf16[16,32,256]{2,1,0:T(8,128)(2,1)} %broadcast_in_dim.12), calls=%async_computation.6 | async-start | bytes 524288 | tf_op jit(solution)/shard_map/all_to_all | solution.py:17
  302.5 13.9 %all-to-all-done.6 = bf16[16,32,256]{2,1,0:T(8,128)(2,1)S(1)} async-done(((bf16[16,32,256]{2,1,0:T(8,128)(2,1)}), bf16[16,32,256]{2,1,0:T(8,128)(2,1)S(1)}, u32[]{:S(2)}, u32[]{:S(2)}) %all-to-all-start.6) | async-done | bytes 262176 | tf_op jit(solution)/shard_map/all_to_all | solution.py:17
  316.4 4.4 all-to-all-start.5
  323.3 13.5 %all-to-all-done.5 = bf16[16,32,256]{2,1,0:T(8,128)(2,1)S(1)} async-done(((bf16[16,32,256]{2,1,0:T(8,128)(2,1)}), bf16[16,32,256]{2,1,0:T(8,128)(2,1)S(1)}, u32[]{:S(2)}, u32[]{:S(2)}) %all-to-all-start.5) | async-done | bytes 262176 | tf_op jit(solution)/shard_map/all_to_all | solution.py:40
  336.9 18.7 %all-to-all-start.7 = ((bf16[32,32,256]{2,1,0:T(8,128)(2,1)}), bf16[32,32,256]{2,1,0:T(8,128)(2,1)S(1)}, u32[]{:S(2)}, u32[]{:S(2)}) async-start(bf16[32,32,256]{2,1,0:T(8,128)(2,1)} %copy.16), calls=%async_computation.7 | async-start | bytes 1048576 | tf_op jit(solution)/shard_map/all_to_all | solution.py:40
  355.7 26.7 %all-to-all-done.7 = bf16[32,32,256]{2,1,0:T(8,128)(2,1)S(1)} async-done(((bf16[32,32,256]{2,1,0:T(8,128)(2,1)}), bf16[32,32,256]{2,1,0:T(8,128)(2,1)S(1)}, u32[]{:S(2)}, u32[]{:S(2)}) %all-to-all-start.7) | async-done | bytes 524320 | tf_op jit(solution)/shard_map/all_to_all | solution.py:40
  382.6 47.4 %psum.75 = f32[32,32]{0,1:T(8,128)S(1)} all-reduce(f32[32,32]{0,1:T(8,128)S(1)} %fusion.38), channel_id=1, replica_groups=mesh['row_0'=8,'row_1'=4,'col_0'=2,'col_1'=4,'col_2'=2] {'row_0'}, use_global_device_ids=true, to_apply=%region_11.12 | all-reduce | flops 1024 | bytes 8192 | tf_op jit(solution)/shard_map/psum | solution.py:45
  430.1 12.6 %psum.76 = f32[32,32]{0,1:T(8,128)S(1)} all-reduce(f32[32,32]{0,1:T(8,128)S(1)} %psum.75), channel_id=1, replica_groups=mesh['row_0'=8,'row_1'=4,'col_0'=2,'col_1'=4,'col_2'=2] {'row_1'}, use_global_device_ids=true, to_apply=%region_12.13 | all-reduce | flops 1024 | bytes 8192 | tf_op jit(solution)/shard_map/psum | solution.py:45
  442.7 13.9 %psum.77 = f32[32,32]{0,1:T(8,128)S(1)} all-reduce(f32[32,32]{0,1:T(8,128)S(1)} %psum.76), channel_id=1, replica_groups=mesh['row_0'=8,'row_1'=4,'col_0'=2,'col_1'=4,'col_2'=2] {'col_0'}, use_global_device_ids=true, to_apply=%region_13.14 | all-reduce | flops 1024 | bytes 8192 | tf_op jit(solution)/shard_map/psum | solution.py:45
  456.6 12.7 %psum.78 = f32[32,32]{0,1:T(8,128)S(1)} all-reduce(f32[32,32]{0,1:T(8,128)S(1)} %psum.77), channel_id=1, replica_groups=mesh['row_0'=8,'row_1'=4,'col_0'=2,'col_1'=4,'col_2'=2] {'col_1'}, use_global_device_ids=true, to_apply=%region_14.15 | all-reduce | flops 1024 | bytes 8192 | tf_op jit(solution)/shard_map/psum | solution.py:45
  469.3 19.3 %psum.79 = f32[32,32]{0,1:T(8,128)S(1)} all-reduce(f32[32,32]{0,1:T(8,128)S(1)} %psum.78), channel_id=1, replica_groups=mesh['row_0'=8,'row_1'=4,'col_0'=2,'col_1'=4,'col_2'=2] {'col_2'}, use_global_device_ids=true, to_apply=%region_15.16 | all-reduce | flops 1024 | bytes 8192 | tf_op jit(solution)/shard_map/psum | solution.py:45
  (54 shorter events, 21.4 us)
Async XLA Ops:
  0.6 58.8 %copy-start = (bf16[1,1,4,256,256]{4,3,2,1,0:T(8,128)(2,1)S(1)}, bf16[1,1,4,256,256]{4,3,2,1,0:T(8,128)(2,1)}, u32[]{:S(2)}) copy-start(bf16[1,1,4,256,256]{4,3,2,1,0:T(8,128)(2,1)} %param.4) | copy-start | bytes 1572868
  1.5 42.6 %copy-start.2 = (bf16[32,256]{1,0:T(8,128)(2,1)S(1)}, bf16[32,256]{1,0:T(8,128)(2,1)}, u32[]{:S(2)}) copy-start(bf16[32,256]{1,0:T(8,128)(2,1)} %param.7) | copy-start | bytes 49156
  44.8 14.0 %copy-start.4 = (s32[1,1,4]{2,1,0:T(1,128)S(1)}, s32[1,1,4]{2,1,0:T(1,128)}, u32[]{:S(2)}) copy-start(s32[1,1,4]{2,1,0:T(1,128)} %param.6) | copy-start | bytes 52
  44.8 30.1 %all-to-all-start.2 = ((bf16[16,32,256]{2,1,0:T(8,128)(2,1)}), bf16[16,32,256]{2,1,0:T(8,128)(2,1)S(1)}, u32[]{:S(2)}, u32[]{:S(2)}) async-start(bf16[16,32,256]{2,1,0:T(8,128)(2,1)} %broadcast_in_dim.10), calls=%async_computation.2 | async-start | bytes 524288 | tf_op jit(solution)/shard_map/all_to_all | solution.py:17
  59.7 0.7 copy-start.3
  74.9 20.5 %all-to-all-start.1 = ((bf16[16,32,256]{2,1,0:T(8,128)(2,1)}), bf16[16,32,256]{2,1,0:T(8,128)(2,1)S(1)}, u32[]{:S(2)}, u32[]{:S(2)}) async-start(bf16[16,32,256]{2,1,0:T(8,128)(2,1)} %copy.11), calls=%async_computation.1 | async-start | bytes 524288 | tf_op jit(solution)/shard_map/all_to_all | solution.py:40
  95.4 45.5 %all-to-all-start.3 = ((bf16[32,32,256]{2,1,0:T(8,128)(2,1)}), bf16[32,32,256]{2,1,0:T(8,128)(2,1)S(1)}, u32[]{:S(2)}, u32[]{:S(2)}) async-start(bf16[32,32,256]{2,1,0:T(8,128)(2,1)} %copy.12), calls=%async_computation.3 | async-start | bytes 1048576 | tf_op jit(solution)/shard_map/all_to_all | solution.py:40
  254.2 234.4 %copy-start.1 = (f32[32,256]{1,0:T(8,128)}, f32[32,256]{1,0:T(8,128)S(1)}, u32[]{:S(2)}) copy-start(f32[32,256]{1,0:T(8,128)S(1)} %get-tuple-element.10) | copy-start | bytes 98308
  285.8 30.6 %all-to-all-start.6 = ((bf16[16,32,256]{2,1,0:T(8,128)(2,1)}), bf16[16,32,256]{2,1,0:T(8,128)(2,1)S(1)}, u32[]{:S(2)}, u32[]{:S(2)}) async-start(bf16[16,32,256]{2,1,0:T(8,128)(2,1)} %broadcast_in_dim.12), calls=%async_computation.6 | async-start | bytes 524288 | tf_op jit(solution)/shard_map/all_to_all | solution.py:17
  316.4 20.5 %all-to-all-start.5 = ((bf16[16,32,256]{2,1,0:T(8,128)(2,1)}), bf16[16,32,256]{2,1,0:T(8,128)(2,1)S(1)}, u32[]{:S(2)}, u32[]{:S(2)}) async-start(bf16[16,32,256]{2,1,0:T(8,128)(2,1)} %copy.15), calls=%async_computation.5 | async-start | bytes 524288 | tf_op jit(solution)/shard_map/all_to_all | solution.py:40
  336.9 45.5 %all-to-all-start.7 = ((bf16[32,32,256]{2,1,0:T(8,128)(2,1)}), bf16[32,32,256]{2,1,0:T(8,128)(2,1)S(1)}, u32[]{:S(2)}, u32[]{:S(2)}) async-start(bf16[32,32,256]{2,1,0:T(8,128)(2,1)} %copy.16), calls=%async_computation.7 | async-start | bytes 1048576 | tf_op jit(solution)/shard_map/all_to_all | solution.py:40
where the time goes:
time: 491 us; the launch traced here: 490 us
  blocking collectives  285 us (58%)
  waiting for transfers between devices  108 us (22%)
  starting transfers between devices  74.8 us (15%)
  local copies, waits for them, and re-layouts  9.7 us (2%)
  other arithmetic  6.98 us (1%)
    psum x10, blocking collectives, by_axis(): return functools.reduce(lax.psum, axes, value)  212 us
    all_to_all x4, waiting for transfers between devices, summed_on_arrival(): lax.all_to_all(parts, axis, split_axis=0, concat_axis=0, tiled=True)  80.5 us
    all_to_all x2, blocking collectives, sent_to_all(): lax.all_to_all(jnp.broadcast_to(value[None], (length, *value.shape)), axi...  73.5 us
    all_to_all x4, starting transfers between devices, summed_on_arrival(): lax.all_to_all(parts, axis, split_axis=0, concat_axis=0, tiled=True)  46.3 us
    all_to_all x2, starting transfers between devices, sent_to_all(): lax.all_to_all(jnp.broadcast_to(value[None], (length, *value.shape)), axi...  28.6 us
    all_to_all x2, waiting for transfers between devices, sent_to_all(): lax.all_to_all(jnp.broadcast_to(value[None], (length, *value.shape)), axi...  27.2 us
  transfers between devices with their start and end apart: 6, of which 6 were waited for; matrix products, arithmetic and copies ran while one was open for 2% of the time, Pallas kernels for 0%

commit v1 on v0

v1 whole, which is shorter than its diff:
```python
import functools

import jax
import jax.numpy as jnp
from jax import lax
from jax.experimental import pallas as pl
from jax.experimental.pallas import tpu as pltpu
from jax.sharding import Mesh
from jax.sharding import PartitionSpec as P

Z_HI, X_CORE = ("col_0", ("col_1", "col_2"))
Z_LO, Y = ("row_0", "row_1")
COL = ("col_0", "col_1", "col_2")
ROW = ("row_0", "row_1")
COL_ROW = ("col_0", "col_1", "col_2", "row_0", "row_1")
HIGHEST = lax.Precision.HIGHEST
INTERPRET = False


def exchange(parts, axis):
    return lax.all_to_all(parts, axis, 0, 0, tiled=True)


def spread(value, axis):
    length = lax.axis_size(axis)
    return exchange(jnp.broadcast_to(value[None], (length, *value.shape)), axis)


def partner(value):
    return lax.ppermute(value, Z_HI, [(0, 1), (1, 0)])


def split_bits(small, width):
    pieces = []
    rest = small
    for _ in range(3):
        piece = lax.reduce_precision(rest, 8, 7)
        pieces.append(piece)
        rest = rest - piece
    joined = jnp.concatenate(pieces, axis=-1).astype(jnp.bfloat16)
    return jnp.pad(joined, [(0, 0), (0, width - joined.shape[-1])])


def summed_bits(blocks):
    count = blocks.shape[-2]
    wide = blocks[..., : 3 * count].astype(jnp.float32)
    total = (wide[..., 2 * count :] + wide[..., count : 2 * count]) + wide[..., :count]
    return total.sum(axis=0)


def tile_kernel(
    pair_ref, column_ref, row_ref, tile_ref, direct_ref, mirror_ref, form_ref, sums_ref,
    *, tiles, y_count, xc_count,
):
    side = pair_ref[2 * tiles]
    direct_slots, mirror_slots = ([], [])
    form = jnp.zeros(form_ref.shape, jnp.float32)
    for t in range(tiles):
        i = pair_ref[t]
        j = pair_ref[tiles + t]
        from_column = column_ref[lax.rem(j, y_count), lax.div(j, y_count)]
        half = lax.rem(lax.div(i, xc_count) + side, 2)
        from_row = row_ref[lax.rem(i, xc_count), half]
        direct = lax.dot_general(
            from_column, tile_ref[t], (((1,), (1,)), ((), ())), preferred_element_type=jnp.float32
        )
        sums_ref[t] = direct
        sums_ref[tiles + t] = jnp.dot(from_row, tile_ref[t], preferred_element_type=jnp.float32)
        form += lax.dot_general(
            from_row.astype(jnp.float32), direct, (((1,), (1,)), ((), ())),
            precision=HIGHEST, preferred_element_type=jnp.float32,
        )
        direct_slots.append((i, lax.rem(i, xc_count), half))
        mirror_slots.append((j, lax.rem(j, y_count), lax.div(j, y_count)))
    form_ref[...] = form
    direct_ref[...] = jnp.zeros_like(direct_ref)
    mirror_ref[...] = jnp.zeros_like(mirror_ref)
    for base, slots, out_ref in ((0, direct_slots, direct_ref), (tiles, mirror_slots, mirror_ref)):
        for t in range(tiles):
            total = sums_ref[base + t]
            for other in range(tiles):
                if other != t:
                    same = (slots[other][0] == slots[t][0]).astype(jnp.float32)
                    total = total + same * sums_ref[base + other]
            out_ref[slots[t][1], slots[t][2]] = total.astype(jnp.bfloat16)


def tile_products(pairs, column_block, row_block, tiles):
    vectors, size = column_block.shape[-2:]
    vmem = pl.BlockSpec(memory_space=pltpu.VMEM)
    z_count = lax.axis_size(Z_LO)
    return pl.pallas_call(
        functools.partial(
            tile_kernel,
            tiles=tiles.shape[0],
            y_count=column_block.shape[0],
            xc_count=row_block.shape[0],
        ),
        out_shape=(
            jax.ShapeDtypeStruct((row_block.shape[0], 2, vectors, size), jnp.bfloat16),
            jax.ShapeDtypeStruct((column_block.shape[0], z_count, vectors, size), jnp.bfloat16),
            jax.ShapeDtypeStruct((vectors, vectors), jnp.float32),
        ),
        in_specs=[pl.BlockSpec(memory_space=pltpu.SMEM), vmem, vmem, vmem],
        out_specs=(vmem, vmem, vmem),
        scratch_shapes=[pltpu.VMEM((2 * tiles.shape[0], vectors, size), jnp.float32)],
        interpret=INTERPRET,
        name="tile_products",
    )(pairs, column_block, row_block, tiles)


def shards(tile_values, tile_row, tile_col, basis_init):
    tiles = tile_values[0, 0]
    side = lax.axis_index(Z_HI).astype(jnp.int32)
    pairs = jnp.concatenate([tile_row[0, 0], tile_col[0, 0], side[None]])
    vectors, size = basis_init.shape
    total_rows = size * lax.axis_size(COL_ROW)
    f32 = jnp.float32

    other = partner(basis_init)
    column_block = spread(spread(basis_init, Z_LO), Y)
    row_block = spread(jnp.stack([basis_init, other]), X_CORE)
    direct, mirror, _ = tile_products(pairs, column_block, row_block, tiles)
    direct = exchange(direct, X_CORE).astype(f32).sum(axis=0)
    far = partner(direct[1].astype(jnp.bfloat16))
    mirror = exchange(mirror, Y).astype(f32).sum(axis=0)
    mirror = exchange(mirror.astype(jnp.bfloat16), Z_LO).astype(f32).sum(axis=0)
    image = direct[0] + far.astype(f32) + mirror

    gram = jnp.dot(image, image.T, precision=HIGHEST)
    current = image.astype(jnp.bfloat16)
    other = partner(current)
    by_z = spread(jnp.stack([current, split_bits(gram, size)]), Z_LO)
    gram = summed_bits(by_z[:, 1])
    by_y = spread(jnp.concatenate([by_z[:, 0], split_bits(gram, size)[None]]), Y)
    gram = summed_bits(by_y[:, -1])
    by_xc = spread(jnp.stack([current, other, split_bits(gram, size)]), X_CORE)
    gram = summed_bits(by_xc[:, -1])
    direct, mirror, form = tile_products(pairs, by_y, by_xc, tiles)
    count = direct.shape[0]
    form_block = jnp.broadcast_to(split_bits(form, size)[None, None], (count, 1, vectors, size))
    direct = exchange(jnp.concatenate([direct, form_block], axis=1), X_CORE)
    form = summed_bits(direct[:, -1])
    direct = direct[:, :2].astype(f32).sum(axis=0)
    far = partner(jnp.stack([direct[1].astype(jnp.bfloat16), split_bits(gram, size)]))
    gram = gram + summed_bits(far[1:])
    count = mirror.shape[0]
    form_block = jnp.broadcast_to(split_bits(form, size)[None, None], (count, 1, vectors, size))
    mirror = exchange(jnp.concatenate([mirror, form_block], axis=1), Y)
    form = summed_bits(mirror[:, -1])
    mirror = mirror[:, :-1].astype(f32).sum(axis=0).astype(jnp.bfloat16)
    count = mirror.shape[0]
    form_block = jnp.broadcast_to(split_bits(form, size)[None], (count, vectors, size))
    mirror = exchange(jnp.stack([mirror, form_block], axis=1), Z_LO)
    form = summed_bits(mirror[:, 1])
    mirror = mirror[:, 0].astype(f32).sum(axis=0)
    form = form + summed_bits(partner(split_bits(form, size))[None])
    raw_image = direct[0] + far[0].astype(f32) + mirror

    factor = jnp.linalg.cholesky(gram / total_rows)
    inverse = lax.linalg.triangular_solve(
        factor, jnp.eye(vectors, dtype=f32), left_side=True, lower=True
    )
    ritz_basis = jnp.dot(inverse, image, precision=HIGHEST)
    last_image = jnp.dot(inverse, raw_image, precision=HIGHEST)
    form = (form + form.T) / total_rows
    projected = jnp.dot(
        jnp.dot(inverse, form, precision=HIGHEST), inverse.T, precision=HIGHEST
    )
    residual = last_image - jnp.dot(projected.T, ritz_basis, precision=HIGHEST)
    return (ritz_basis, residual, projected)


def solution(mesh):
    finer = Mesh(mesh.devices.reshape(8, 4, 2, 4, 2), ("row_0", "row_1", "col_0", "col_1", "col_2"))
    placed = (P(ROW, COL, None, None, None), P(ROW, COL, None), P(ROW, COL, None), P(None, COL_ROW))
    return jax.shard_map(
        shards,
        mesh=finer,
        in_specs=placed,
        out_specs=(P(None, COL_ROW), P(None, COL_ROW), P()),
        check_vma=False,
    )
```

time: 491 us -> 246 us (0.50)
  the two profiles are of different devices: /device:TPU:1 before, /device:TPU:8 now
where the time goes in v1:
time: 246 us; the launch traced here: 245 us
  starting transfers between devices  81.4 us (33%)
  blocking collectives  79.6 us (32%)
  waiting for transfers between devices  56.1 us (23%)
  other arithmetic  14.6 us (6%)
  Pallas kernels  5.34 us (2%)
  local copies, waits for them, and re-layouts  4.65 us (2%)
    all_to_all x5, blocking collectives, exchange(): return lax.all_to_all(parts, axis, 0, 0, tiled=True)  79.6 us
    ppermute x5, starting transfers between devices, partner(): return lax.ppermute(value, Z_HI, [(0, 1), (1, 0)])  49.4 us
    all_to_all x7, waiting for transfers between devices, exchange(): return lax.all_to_all(parts, axis, 0, 0, tiled=True)  33.4 us
    all_to_all x7, starting transfers between devices, exchange(): return lax.all_to_all(parts, axis, 0, 0, tiled=True)  32 us
    ppermute x5, waiting for transfers between devices, partner(): return lax.ppermute(value, Z_HI, [(0, 1), (1, 0)])  22.8 us
    pallas_call x2, Pallas kernels, tile_products(): pl.pallas_call(functools.partial(tile_kernel, tiles=tiles.shape[0], y_cou...  5.34 us
  transfers between devices with their start and end apart: 12, of which 11 were waited for; matrix products, arithmetic and copies ran while one was open for 4% of the time, Pallas kernels for 0%

profile of v1, /device:TPU:8, one launch (start us, length us, event | category | flops | bytes accessed | tf_op | source)
XLA Modules:
  0.0 244.8 jit_solution(15035775381739733327)
XLA Ops:
  0.6 15.7 %collective-permute-start = (bf16[32,256]{1,0:T(8,128)(2,1)}, bf16[32,256]{1,0:T(8,128)(2,1)S(1)}, u32[]{:S(2)}, u32[]{:S(2)}) collective-permute-start(bf16[32,256]{1,0:T(8,128)(2,1)} %param.7), channel_id=1, source_target_pairs={{0,8},{8,0},{1,9},{9,1},{2,10},{10,2},{3,11},{11,3},{4,12},{12,4},... | collective-permute-start | bytes 49160 | tf_op jit(solution)/shard_map/ppermute | solution.py:30
  19.0 11.7 %all_to_all.60.row_ref = bf16[8,2,32,256]{3,2,1,0:T(8,128)(2,1)} all-to-all(bf16[8,2,32,256]{3,2,1,0:T(8,128)(2,1)S(1)} %broadcast_in_dim.29), channel_id=1, replica_groups=mesh['row_0'=8,'row_1'=4,'col_0'=2,'col_1'=4,'col_2'=2] {'col_1','col_2'}, dimensions={0} | all-to-all | bytes 524288 | tf_op jit(solution)/shard_map/all_to_all | solution.py:21
  30.8 20.8 %all_to_all.61 = bf16[8,32,256]{2,1,0:T(8,128)(2,1)S(1)} all-to-all(bf16[8,32,256]{2,1,0:T(8,128)(2,1)S(1)} %broadcast_in_dim.26), channel_id=1, replica_groups=mesh['row_0'=8,'row_1'=4,'col_0'=2,'col_1'=4,'col_2'=2] {'row_0'}, dimensions={0} | all-to-all | bytes 262144 | tf_op jit(solution)/shard_map/all_to_all | solution.py:21
  52.4 4.9 %all-to-all-start.1 = ((bf16[4,8,32,256]{3,2,1,0:T(8,128)(2,1)}), bf16[4,8,32,256]{3,2,1,0:T(8,128)(2,1)S(1)}, u32[]{:S(2)}, u32[]{:S(2)}) async-start(bf16[4,8,32,256]{3,2,1,0:T(8,128)(2,1)} %broadcast_in_dim.27), calls=%async_computation.1 | async-start | bytes 1048576 | tf_op jit(solution)/shard_map/all_to_all | solution.py:21
  58.5 5.4 %all-to-all-done.1.column_ref = bf16[4,8,32,256]{3,2,1,0:T(8,128)(2,1)S(1)} async-done(((bf16[4,8,32,256]{3,2,1,0:T(8,128)(2,1)}), bf16[4,8,32,256]{3,2,1,0:T(8,128)(2,1)S(1)}, u32[]{:S(2)}, u32[]{:S(2)}) %all-to-all-start.1) | async-done | bytes 524320 | tf_op jit(solution)/shard_map/all_to_all | solution.py:21
  67.3 11.5 %all_to_all.62 = bf16[4,8,32,256]{3,2,1,0:T(8,128)(2,1)S(1)} all-to-all(bf16[4,8,32,256]{3,2,1,0:T(8,128)(2,1)} %get-tuple-element.9), channel_id=1, replica_groups=mesh['row_0'=8,'row_1'=4,'col_0'=2,'col_1'=4,'col_2'=2] {'row_1'}, dimensions={0} | all-to-all | bytes 1048576 | tf_op jit(solution)/shard_map/all_to_all | solution.py:21
  78.8 3.4 %all-to-all-start.3 = ((bf16[8,2,32,256]{3,2,1,0:T(8,128)(2,1)}), bf16[8,2,32,256]{3,2,1,0:T(8,128)(2,1)S(1)}, u32[]{:S(2)}, u32[]{:S(2)}) async-start(bf16[8,2,32,256]{3,2,1,0:T(8,128)(2,1)} %get-tuple-element.8), calls=%async_computation.3 | async-start | bytes 524288 | tf_op jit(solution)/shard_map/all_to_all | solution.py:21
  83.0 6.7 %all-to-all-done.3 = bf16[8,2,32,256]{3,2,1,0:T(8,128)(2,1)S(1)} async-done(((bf16[8,2,32,256]{3,2,1,0:T(8,128)(2,1)}), bf16[8,2,32,256]{3,2,1,0:T(8,128)(2,1)S(1)}, u32[]{:S(2)}, u32[]{:S(2)}) %all-to-all-start.3) | async-done | bytes 262176 | tf_op jit(solution)/shard_map/all_to_all | solution.py:21
  89.7 5.4 %all-to-all-start.5 = ((bf16[8,32,256]{2,1,0:T(8,128)(2,1)}), bf16[8,32,256]{2,1,0:T(8,128)(2,1)S(1)}, u32[]{:S(2)}, u32[]{:S(2)}) async-start(bf16[8,32,256]{2,1,0:T(8,128)(2,1)} %reduce_sum.127), calls=%async_computation.5 | async-start | bytes 262144 | tf_op jit(solution)/shard_map/all_to_all | solution.py:21
  95.1 8.4 %collective-permute-start.1 = (bf16[32,256]{1,0:T(8,128)(2,1)S(1)}, bf16[32,256]{1,0:T(8,128)(2,1)S(1)}, u32[]{:S(2)}, u32[]{:S(2)}) collective-permute-start(bf16[32,256]{1,0:T(8,128)(2,1)S(1)} %fusion.53), channel_id=1, source_target_pairs={{0,8},{8,0},{1,9},{9,1},{2,10},{10,2},{3,11},{11,3},{4,12},{12,4},... | collective-permute-start | bytes 49160 | tf_op jit(solution)/shard_map/ppermute | solution.py:30
  109.8 24.3 %all_to_all.63 = bf16[8,2,32,256]{3,2,1,0:T(8,128)(2,1)S(1)} all-to-all(bf16[8,2,32,256]{3,2,1,0:T(8,128)(2,1)S(1)} %broadcast_in_dim.30), channel_id=1, replica_groups=mesh['row_0'=8,'row_1'=4,'col_0'=2,'col_1'=4,'col_2'=2] {'row_0'}, dimensions={0} | all-to-all | bytes 524288 | tf_op jit(solution)/shard_map/all_to_all | solution.py:21
  135.2 4.9 %all-to-all-start.7 = ((bf16[4,9,32,256]{3,2,1,0:T(8,128)(2,1)}), bf16[4,9,32,256]{3,2,1,0:T(8,128)(2,1)S(1)}, u32[]{:S(2)}, u32[]{:S(2)}) async-start(bf16[4,9,32,256]{3,2,1,0:T(8,128)(2,1)} %broadcast_in_dim.32), calls=%async_computation.7 | async-start | bytes 1179648 | tf_op jit(solution)/shard_map/all_to_all | solution.py:21
  140.1 8.4 %collective-permute-start.2 = (bf16[32,256]{1,0:T(8,128)(2,1)S(1)}, bf16[32,256]{1,0:T(8,128)(2,1)S(1)}, u32[]{:S(2)}, u32[]{:S(2)}) collective-permute-start(bf16[32,256]{1,0:T(8,128)(2,1)S(1)} %get-tuple-element.13), channel_id=1, source_target_pairs={{0,8},{8,0},{1,9},{9,1},{2,10},{10,2},{3,11},{11,3},{4,12},{12,4},... | collective-permute-start | bytes 49160 | tf_op jit(solution)/shard_map/ppermute | solution.py:30
  148.8 5.7 %collective-permute-done.2 = bf16[32,256]{1,0:T(8,128)(2,1)S(1)} collective-permute-done((bf16[32,256]{1,0:T(8,128)(2,1)S(1)}, bf16[32,256]{1,0:T(8,128)(2,1)S(1)}, u32[]{:S(2)}, u32[]{:S(2)}) %collective-permute-start.2) | collective-permute-done | bytes 16416 | tf_op jit(solution)/shard_map/ppermute | solution.py:30
  154.5 11.3 %all_to_all.64.row_ref = bf16[8,3,32,256]{3,2,1,0:T(8,128)(2,1)S(1)} all-to-all(bf16[8,3,32,256]{3,2,1,0:T(8,128)(2,1)S(1)} %broadcast_in_dim.33), channel_id=1, replica_groups=mesh['row_0'=8,'row_1'=4,'col_0'=2,'col_1'=4,'col_2'=2] {'col_1','col_2'}, dimensions={0} | all-to-all | bytes 786432 | tf_op jit(solution)/shard_map/all_to_all | solution.py:21
  171.9 3.5 %all-to-all-start.9 = ((bf16[8,3,32,256]{3,2,1,0:T(8,128)(2,1)}), bf16[8,3,32,256]{3,2,1,0:T(8,128)(2,1)S(1)}, u32[]{:S(2)}, u32[]{:S(2)}) async-start(bf16[8,3,32,256]{3,2,1,0:T(8,128)(2,1)} %pad_maximum_fusion.1), calls=%async_computation.9 | async-start | bytes 786432 | tf_op jit(solution)/shard_map/all_to_all | solution.py:21
  175.6 8.5 %all-to-all-done.9 = bf16[8,3,32,256]{3,2,1,0:T(8,128)(2,1)S(1)} async-done(((bf16[8,3,32,256]{3,2,1,0:T(8,128)(2,1)}), bf16[8,3,32,256]{3,2,1,0:T(8,128)(2,1)S(1)}, u32[]{:S(2)}, u32[]{:S(2)}) %all-to-all-start.9) | async-done | bytes 393248 | tf_op jit(solution)/shard_map/all_to_all | solution.py:21
  184.4 8.5 %collective-permute-start.3 = (bf16[2,32,256]{1,2,0:T(8,128)(2,1)S(1)}, bf16[2,32,256]{1,2,0:T(8,128)(2,1)S(1)}, u32[]{:S(2)}, u32[]{:S(2)}) collective-permute-start(bf16[2,32,256]{1,2,0:T(8,128)(2,1)S(1)} %copy.20), channel_id=1, source_target_pairs={{0,8},{8,0},{1,9},{9,1},{2,10},{10,2},{3,11},{11,3},{4,12},{12,4},... | collective-permute-start | bytes 98312 | tf_op jit(solution)/shard_map/ppermute | solution.py:30
  194.1 4.9 %all-to-all-start.10 = ((bf16[4,9,32,256]{3,2,1,0:T(8,128)(2,1)}), bf16[4,9,32,256]{3,2,1,0:T(8,128)(2,1)S(1)}, u32[]{:S(2)}, u32[]{:S(2)}) async-start(bf16[4,9,32,256]{3,2,1,0:T(8,128)(2,1)} %pad_maximum_fusion), calls=%async_computation.10 | async-start | bytes 1179648 | tf_op jit(solution)/shard_map/all_to_all | solution.py:21
  199.1 6.5 %collective-permute-done.3 = bf16[2,32,256]{1,2,0:T(8,128)(2,1)S(1)} collective-permute-done((bf16[2,32,256]{1,2,0:T(8,128)(2,1)S(1)}, bf16[2,32,256]{1,2,0:T(8,128)(2,1)S(1)}, u32[]{:S(2)}, u32[]{:S(2)}) %collective-permute-start.3) | collective-permute-done | bytes 32800 | tf_op jit(solution)/shard_map/ppermute | solution.py:30
  207.9 5.1 %all-to-all-start.11 = ((bf16[8,2,32,256]{3,2,1,0:T(8,128)(2,1)}), bf16[8,2,32,256]{3,2,1,0:T(8,128)(2,1)S(1)}, u32[]{:S(2)}, u32[]{:S(2)}) async-start(bf16[8,2,32,256]{3,2,1,0:T(8,128)(2,1)} %pad_maximum_fusion.2), calls=%async_computation.11 | async-start | bytes 524288 | tf_op jit(solution)/shard_map/all_to_all | solution.py:21
  220.1 8.4 %all-to-all-done.11 = bf16[8,2,32,256]{3,2,1,0:T(8,128)(2,1)S(1)} async-done(((bf16[8,2,32,256]{3,2,1,0:T(8,128)(2,1)}), bf16[8,2,32,256]{3,2,1,0:T(8,128)(2,1)S(1)}, u32[]{:S(2)}, u32[]{:S(2)}) %all-to-all-start.11) | async-done | bytes 262176 | tf_op jit(solution)/shard_map/all_to_all | solution.py:21
  229.0 8.4 %collective-permute-start.4 = (bf16[32,256]{1,0:T(8,128)(2,1)S(1)}, bf16[32,256]{1,0:T(8,128)(2,1)S(1)}, u32[]{:S(2)}, u32[]{:S(2)}) collective-permute-start(bf16[32,256]{1,0:T(8,128)(2,1)S(1)} %fusion.73), channel_id=1, source_target_pairs={{0,8},{8,0},{1,9},{9,1},{2,10},{10,2},{3,11},{11,3},{4,12},{12,4},... | collective-permute-start | bytes 49160 | tf_op jit(solution)/shard_map/ppermute | solution.py:30
  237.6 5.9 %collective-permute-done.4 = bf16[32,256]{1,0:T(8,128)(2,1)S(1)} collective-permute-done((bf16[32,256]{1,0:T(8,128)(2,1)S(1)}, bf16[32,256]{1,0:T(8,128)(2,1)S(1)}, u32[]{:S(2)}, u32[]{:S(2)}) %collective-permute-start.4) | collective-permute-done | bytes 16416 | tf_op jit(solution)/shard_map/ppermute | solution.py:30
  (112 shorter events, 35.6 us)
Async XLA Ops:
  0.6 17.6 %collective-permute-start = (bf16[32,256]{1,0:T(8,128)(2,1)}, bf16[32,256]{1,0:T(8,128)(2,1)S(1)}, u32[]{:S(2)}, u32[]{:S(2)}) collective-permute-start(bf16[32,256]{1,0:T(8,128)(2,1)} %param.7), channel_id=1, source_target_pairs={{0,8},{8,0},{1,9},{9,1},{2,10},{10,2},{3,11},{11,3},{4,12},{12,4},... | collective-permute-start | bytes 49160 | tf_op jit(solution)/shard_map/ppermute | solution.py:30
  19.0 11.7 %copy-start.7 = (bf16[32,256]{1,0:T(8,128)(2,1)S(1)}, bf16[32,256]{1,0:T(8,128)(2,1)}, u32[]{:S(2)}) copy-start(bf16[32,256]{1,0:T(8,128)(2,1)} %param.7) | copy-start | bytes 49156
  52.4 11.5 %all-to-all-start.1 = ((bf16[4,8,32,256]{3,2,1,0:T(8,128)(2,1)}), bf16[4,8,32,256]{3,2,1,0:T(8,128)(2,1)S(1)}, u32[]{:S(2)}, u32[]{:S(2)}) async-start(bf16[4,8,32,256]{3,2,1,0:T(8,128)(2,1)} %broadcast_in_dim.27), calls=%async_computation.1 | async-start | bytes 1048576 | tf_op jit(solution)/shard_map/all_to_all | solution.py:21
  57.3 0.7 copy-start.8
  57.3 0.7 copy-start.9
  63.9 0.8 copy-start.2
  78.8 10.8 %all-to-all-start.3 = ((bf16[8,2,32,256]{3,2,1,0:T(8,128)(2,1)}), bf16[8,2,32,256]{3,2,1,0:T(8,128)(2,1)S(1)}, u32[]{:S(2)}, u32[]{:S(2)}) async-start(bf16[8,2,32,256]{3,2,1,0:T(8,128)(2,1)} %get-tuple-element.8), calls=%async_computation.3 | async-start | bytes 524288 | tf_op jit(solution)/shard_map/all_to_all | solution.py:21
  89.7 16.9 %all-to-all-start.5 = ((bf16[8,32,256]{2,1,0:T(8,128)(2,1)}), bf16[8,32,256]{2,1,0:T(8,128)(2,1)S(1)}, u32[]{:S(2)}, u32[]{:S(2)}) async-start(bf16[8,32,256]{2,1,0:T(8,128)(2,1)} %reduce_sum.127), calls=%async_computation.5 | async-start | bytes 262144 | tf_op jit(solution)/shard_map/all_to_all | solution.py:21
  95.1 14.3 %collective-permute-start.1 = (bf16[32,256]{1,0:T(8,128)(2,1)S(1)}, bf16[32,256]{1,0:T(8,128)(2,1)S(1)}, u32[]{:S(2)}, u32[]{:S(2)}) collective-permute-start(bf16[32,256]{1,0:T(8,128)(2,1)S(1)} %fusion.53), channel_id=1, source_target_pairs={{0,8},{8,0},{1,9},{9,1},{2,10},{10,2},{3,11},{11,3},{4,12},{12,4},... | collective-permute-start | bytes 49160 | tf_op jit(solution)/shard_map/ppermute | solution.py:30
  135.2 13.3 %all-to-all-start.7 = ((bf16[4,9,32,256]{3,2,1,0:T(8,128)(2,1)}), bf16[4,9,32,256]{3,2,1,0:T(8,128)(2,1)S(1)}, u32[]{:S(2)}, u32[]{:S(2)}) async-start(bf16[4,9,32,256]{3,2,1,0:T(8,128)(2,1)} %broadcast_in_dim.32), calls=%async_computation.7 | async-start | bytes 1179648 | tf_op jit(solution)/shard_map/all_to_all | solution.py:21
  140.1 14.3 %collective-permute-start.2 = (bf16[32,256]{1,0:T(8,128)(2,1)S(1)}, bf16[32,256]{1,0:T(8,128)(2,1)S(1)}, u32[]{:S(2)}, u32[]{:S(2)}) collective-permute-start(bf16[32,256]{1,0:T(8,128)(2,1)S(1)} %get-tuple-element.13), channel_id=1, source_target_pairs={{0,8},{8,0},{1,9},{9,1},{2,10},{10,2},{3,11},{11,3},{4,12},{12,4},... | collective-permute-start | bytes 49160 | tf_op jit(solution)/shard_map/ppermute | solution.py:30
  148.6 17.3 %copy-start = (bf16[4,9,32,256]{3,2,1,0:T(8,128)(2,1)}, bf16[4,9,32,256]{3,2,1,0:T(8,128)(2,1)S(1)}, u32[]{:S(2)}) copy-start(bf16[4,9,32,256]{3,2,1,0:T(8,128)(2,1)S(1)} %all-to-all-done.7.column_ref) | copy-start | bytes 1769476
  165.8 0.8 copy-start.1
  171.9 12.3 %all-to-all-start.9 = ((bf16[8,3,32,256]{3,2,1,0:T(8,128)(2,1)}), bf16[8,3,32,256]{3,2,1,0:T(8,128)(2,1)S(1)}, u32[]{:S(2)}, u32[]{:S(2)}) async-start(bf16[8,3,32,256]{3,2,1,0:T(8,128)(2,1)} %pad_maximum_fusion.1), calls=%async_computation.9 | async-start | bytes 786432 | tf_op jit(solution)/shard_map/all_to_all | solution.py:21
  184.2 9.9 %copy-start.4 = (f32[2,32,256]{2,1,0:T(8,128)}, f32[2,32,256]{2,1,0:T(8,128)S(1)}, u32[]{:S(2)}) copy-start(f32[2,32,256]{2,1,0:T(8,128)S(1)} %convert_reduce_fusion) | copy-start | bytes 196612
  184.4 8.8 %copy-start.3 = (bf16[4,8,32,256]{3,2,1,0:T(8,128)(2,1)S(1)}, bf16[4,8,32,256]{3,2,1,0:T(8,128)(2,1)}, u32[]{:S(2)}) copy-start(bf16[4,8,32,256]{3,2,1,0:T(8,128)(2,1)} %get-tuple-element.12) | copy-start | bytes 1572868
  184.4 21.2 %collective-permute-start.3 = (bf16[2,32,256]{1,2,0:T(8,128)(2,1)S(1)}, bf16[2,32,256]{1,2,0:T(8,128)(2,1)S(1)}, u32[]{:S(2)}, u32[]{:S(2)}) collective-permute-start(bf16[2,32,256]{1,2,0:T(8,128)(2,1)S(1)} %copy.20), channel_id=1, source_target_pairs={{0,8},{8,0},{1,9},{9,1},{2,10},{10,2},{3,11},{11,3},{4,12},{12,4},... | collective-permute-start | bytes 98312 | tf_op jit(solution)/shard_map/ppermute | solution.py:30
  194.1 4.9 %slice-start = ((f32[2,32,256]{2,1,0:T(8,128)}), f32[1,32,256]{2,1,0:T(8,128)S(1)}, s32[]{:S(2)}) async-start(f32[2,32,256]{2,1,0:T(8,128)} %copy-done.4), calls=%async_computation.12 | async-start | bytes 65536 | tf_op jit(solution)/shard_map/slice | solution.py:158
  194.1 12.8 %all-to-all-start.10 = ((bf16[4,9,32,256]{3,2,1,0:T(8,128)(2,1)}), bf16[4,9,32,256]{3,2,1,0:T(8,128)(2,1)S(1)}, u32[]{:S(2)}, u32[]{:S(2)}) async-start(bf16[4,9,32,256]{3,2,1,0:T(8,128)(2,1)} %pad_maximum_fusion), calls=%async_computation.10 | async-start | bytes 1179648 | tf_op jit(solution)/shard_map/all_to_all | solution.py:21
  207.9 20.6 %all-to-all-start.11 = ((bf16[8,2,32,256]{3,2,1,0:T(8,128)(2,1)}), bf16[8,2,32,256]{3,2,1,0:T(8,128)(2,1)S(1)}, u32[]{:S(2)}, u32[]{:S(2)}) async-start(bf16[8,2,32,256]{3,2,1,0:T(8,128)(2,1)} %pad_maximum_fusion.2), calls=%async_computation.11 | async-start | bytes 524288 | tf_op jit(solution)/shard_map/all_to_all | solution.py:21
  220.1 23.8 %copy-start.5 = (f32[32,256]{1,0:T(8,128)}, f32[32,256]{1,0:T(8,128)S(1)}, u32[]{:S(2)}) copy-start(f32[32,256]{1,0:T(8,128)S(1)} %fusion.89) | copy-start | bytes 98308
  229.0 14.5 %collective-permute-start.4 = (bf16[32,256]{1,0:T(8,128)(2,1)S(1)}, bf16[32,256]{1,0:T(8,128)(2,1)S(1)}, u32[]{:S(2)}, u32[]{:S(2)}) collective-permute-start(bf16[32,256]{1,0:T(8,128)(2,1)S(1)} %fusion.73), channel_id=1, source_target_pairs={{0,8},{8,0},{1,9},{9,1},{2,10},{10,2},{3,11},{11,3},{4,12},{12,4},... | collective-permute-start | bytes 49160 | tf_op jit(solution)/shard_map/ppermute | solution.py:30
  243.9 0.9 copy-start.6

commit v2 on v1

v2 whole, which is shorter than its diff:
```python
import functools

import jax
import jax.numpy as jnp
from jax import lax
from jax.experimental import pallas as pl
from jax.experimental.pallas import tpu as pltpu
from jax.sharding import Mesh
from jax.sharding import PartitionSpec as P

Z_HI, X_CORE = ("col_0", ("col_1", "col_2"))
Z_LO, Y = ("row_0", "row_1")
COL = ("col_0", "col_1", "col_2")
ROW = ("row_0", "row_1")
COL_ROW = ("col_0", "col_1", "col_2", "row_0", "row_1")
HIGHEST = lax.Precision.HIGHEST
VMEM = pl.BlockSpec(memory_space=pltpu.VMEM)
SMEM = pl.BlockSpec(memory_space=pltpu.SMEM)
F32, BF16 = (jnp.float32, jnp.bfloat16)
PIECES = 3


def exchange(parts, axis):
    return lax.all_to_all(parts, axis, 0, 0, tiled=True)


def spread(value, axis):
    length = lax.axis_size(axis)
    return exchange(jnp.broadcast_to(value[None], (length, *value.shape)), axis)


def partner(value):
    return lax.ppermute(value, Z_HI, [(0, 1), (1, 0)])


def split_bits(small, width):
    pieces = []
    rest = small
    for _ in range(PIECES):
        piece = lax.reduce_precision(rest, 8, 7)
        pieces.append(piece)
        rest = rest - piece
    joined = jnp.concatenate(pieces, axis=-1).astype(BF16)
    return jnp.pad(joined, [(0, 0), (0, width - joined.shape[-1])])


def summed_bits(blocks):
    count = blocks.shape[-2]
    wide = blocks[..., : PIECES * count].astype(F32)
    total = (wide[..., 2 * count :] + wide[..., count : 2 * count]) + wide[..., :count]
    return total.sum(axis=0)


def store_bits(out_ref, place, small):
    count = small.shape[-1]
    out_ref[place] = jnp.zeros(out_ref.shape[len(place) :], out_ref.dtype)
    rest = small
    for k in range(PIECES):
        piece = rest.astype(BF16)
        out_ref[(*place, slice(None), pl.ds(k * count, count))] = piece
        rest = rest - piece.astype(F32)


def store_sums(out_ref, slots, sums_ref):
    for t, (index, major, minor) in enumerate(slots):
        total = sums_ref[t]
        for other, (other_index, _, _) in enumerate(slots):
            if other != t:
                total = total + (other_index == index).astype(F32) * sums_ref[other]
        out_ref[major, minor] = total.astype(BF16)


def direct_kernel(pair_ref, column_ref, tile_ref, own_ref, out_ref, sums_ref, *, near, extra):
    tiles = tile_ref.shape[0]
    y_count, xc_count = (column_ref.shape[0], out_ref.shape[0])
    side = pair_ref[2 * tiles]
    for t in range(tiles):
        j = pair_ref[tiles + t]
        from_column = column_ref[lax.rem(j, y_count), lax.div(j, y_count)]
        sums_ref[t] = lax.dot_general(
            from_column, tile_ref[t], (((1,), (1,)), ((), ())), preferred_element_type=F32
        )
    for k in range(xc_count):
        for s in range(near + extra):
            out_ref[k, s] = own_ref[s]
        for s in range(near):
            out_ref[k, near + extra + s] = jnp.zeros(out_ref.shape[2:], BF16)
    slots = []
    for t in range(tiles):
        i = pair_ref[t]
        half = lax.rem(lax.div(i, xc_count) + side, near)
        slots.append((i, lax.rem(i, xc_count), near + extra + half))
    store_sums(out_ref, slots, sums_ref)


def mirror_kernel(
    pair_ref, row_ref, tile_ref, direct_ref, out_ref, own_ref, far_ref, sums_ref, *, near, extra
):
    tiles = tile_ref.shape[0]
    y_count, xc_count = (out_ref.shape[0], row_ref.shape[0])
    side = pair_ref[2 * tiles]
    vectors = own_ref.shape[0]
    form = jnp.zeros((vectors, vectors), F32)
    for t in range(tiles):
        i = pair_ref[t]
        half = lax.rem(lax.div(i, xc_count) + side, near)
        from_row = row_ref[lax.rem(i, xc_count), half]
        sums_ref[t] = jnp.dot(from_row, tile_ref[t], preferred_element_type=F32)
        if extra:
            form += lax.dot_general(
                from_row.astype(F32), direct_ref[t], (((1,), (1,)), ((), ())),
                precision=HIGHEST, preferred_element_type=F32,
            )
    for k in range(y_count):
        for s in range(out_ref.shape[1] - extra):
            out_ref[k, s] = jnp.zeros(out_ref.shape[2:], BF16)
    if extra:
        last = out_ref.shape[1] - 1
        store_bits(out_ref, (0, last), form)
        for k in range(1, y_count):
            out_ref[k, last] = out_ref[0, last]
    slots = []
    for t in range(tiles):
        j = pair_ref[tiles + t]
        slots.append((j, lax.rem(j, y_count), lax.div(j, y_count)))
    store_sums(out_ref, slots, sums_ref)
    for s in range(near):
        total = row_ref[0, near + extra + s].astype(F32)
        for k in range(1, xc_count):
            total = total + row_ref[k, near + extra + s].astype(F32)
        if s == 0:
            own_ref[...] = total
        else:
            far_ref[0] = total.astype(BF16)
    if extra:
        wide = row_ref[0, near].astype(F32)
        for k in range(1, xc_count):
            wide = wide + row_ref[k, near].astype(F32)
        total = (wide[:, 2 * vectors : 3 * vectors] + wide[:, vectors : 2 * vectors]) + wide[:, :vectors]
        store_bits(far_ref, (1,), total)


def product(pairs, tiles, current, gram):
    vectors, size = current.shape
    count = tiles.shape[0]
    near = lax.axis_size(Z_HI)
    y_count, z_count, xc_count = (lax.axis_size(Y), lax.axis_size(Z_LO), lax.axis_size(X_CORE))
    extra = 0 if gram is None else 1
    block = (vectors, size)
    if extra:
        by_z = spread(jnp.stack([current, split_bits(gram, size)]), Z_LO)
        gram = summed_bits(by_z[:, 1])
        by_z = jnp.concatenate([by_z[:, 0], split_bits(gram, size)[None]])
    else:
        by_z = spread(current, Z_LO)
    other = partner(current)
    column_block = spread(by_z, Y)
    own = [current, other]
    if extra:
        gram = summed_bits(column_block[:, -1])
        own.append(split_bits(gram, size))
    send, direct = pl.pallas_call(
        functools.partial(direct_kernel, near=near, extra=extra),
        out_shape=(
            jax.ShapeDtypeStruct((xc_count, 2 * near + extra, *block), BF16),
            jax.ShapeDtypeStruct((count, *block), F32),
        ),
        in_specs=[SMEM, VMEM, VMEM, VMEM],
        out_specs=(VMEM, VMEM),
        name="direct_products",
    )(pairs, column_block, tiles, jnp.stack(own))
    arrived = exchange(send, X_CORE)
    send, own_direct, far = pl.pallas_call(
        functools.partial(mirror_kernel, near=near, extra=extra),
        out_shape=(
            jax.ShapeDtypeStruct((y_count, z_count + extra, *block), BF16),
            jax.ShapeDtypeStruct(block, F32),
            jax.ShapeDtypeStruct((1 + extra, *block), BF16),
        ),
        in_specs=[SMEM, VMEM, VMEM, VMEM],
        out_specs=(VMEM, VMEM, VMEM),
        scratch_shapes=[pltpu.VMEM((count, *block), F32)],
        name="mirror_products",
    )(pairs, arrived, tiles, direct)
    mirror = exchange(send, Y)
    sent, far = (far, partner(far))
    own_sum = mirror[:, :z_count].astype(F32).sum(axis=0).astype(BF16)
    if extra:
        form = split_bits(summed_bits(mirror[:, z_count]), size)
        form_block = jnp.broadcast_to(form[None], (z_count, *block))
        by_z = exchange(jnp.stack([own_sum, form_block], axis=1), Z_LO)
        own_sum = by_z[:, 0].astype(F32).sum(axis=0)
        form = summed_bits(by_z[:, 1])
        gram = summed_bits(jnp.stack([sent[1], far[1]]))
    else:
        own_sum = exchange(own_sum, Z_LO).astype(F32).sum(axis=0)
        form = None
    return own_direct + far[0].astype(F32) + own_sum, gram, form


def steps(tile_values, tile_row, tile_col, basis_init):
    tiles = tile_values[0, 0]
    side = lax.axis_index(Z_HI).astype(jnp.int32)
    pairs = jnp.concatenate([tile_row[0, 0], tile_col[0, 0], side[None]])
    vectors, size = basis_init.shape
    total_rows = size * lax.axis_size(COL_ROW)

    image, _, _ = product(pairs, tiles, basis_init, None)
    gram = jnp.dot(image, image.T, precision=HIGHEST)
    raw_image, gram, form = product(pairs, tiles, image.astype(BF16), gram)
    form = summed_bits(spread(split_bits(form, size)[:, : size // 2], COL))

    factor = jnp.linalg.cholesky(gram / total_rows)
    inverse = lax.linalg.triangular_solve(
        factor, jnp.eye(vectors, dtype=F32), left_side=True, lower=True
    )
    ritz_basis = jnp.dot(inverse, image, precision=HIGHEST)
    last_image = jnp.dot(inverse, raw_image, precision=HIGHEST)
    form = (form + form.T) / total_rows
    projected = jnp.dot(
        jnp.dot(inverse, form, precision=HIGHEST), inverse.T, precision=HIGHEST
    )
    residual = last_image - jnp.dot(projected.T, ritz_basis, precision=HIGHEST)
    return (ritz_basis, residual, projected)


def solution(mesh):
    finer = Mesh(mesh.devices.reshape(8, 4, 2, 4, 2), ("row_0", "row_1", "col_0", "col_1", "col_2"))
    placed = (P(ROW, COL, None, None, None), P(ROW, COL, None), P(ROW, COL, None), P(None, COL_ROW))
    return jax.shard_map(
        steps,
        mesh=finer,
        in_specs=placed,
        out_specs=(P(None, COL_ROW), P(None, COL_ROW), P()),
        check_vma=False,
    )
```

time: 246 us -> 235 us (0.955)
  the two profiles are of different devices: /device:TPU:8 before, /device:TPU:1 now
where the time goes in v2:
time: 235 us; the launch traced here: 231 us
  blocking collectives  98 us (42%)
  starting transfers between devices  65.1 us (28%)
  waiting for transfers between devices  38.7 us (16%)
  other arithmetic  11.5 us (5%)
  Pallas kernels  9.41 us (4%)
  local copies, waits for them, and re-layouts  5.57 us (2%)
    all_to_all x5, blocking collectives, exchange(): return lax.all_to_all(parts, axis, 0, 0, tiled=True)  98 us
    all_to_all x6, starting transfers between devices, exchange(): return lax.all_to_all(parts, axis, 0, 0, tiled=True)  33.7 us
    ppermute x4, starting transfers between devices, partner(): return lax.ppermute(value, Z_HI, [(0, 1), (1, 0)])  31.4 us
    all_to_all x6, waiting for transfers between devices, exchange(): return lax.all_to_all(parts, axis, 0, 0, tiled=True)  21 us
    ppermute x4, waiting for transfers between devices, partner(): return lax.ppermute(value, Z_HI, [(0, 1), (1, 0)])  17.6 us
    pallas_call x2, Pallas kernels, product(): pl.pallas_call(functools.partial(mirror_kernel, near=near, extra=extra),...  4.71 us
  transfers between devices with their start and end apart: 10, of which 7 were waited for; matrix products, arithmetic and copies ran while one was open for 4% of the time, Pallas kernels for 0%

profile of v2, /device:TPU:1, one launch (start us, length us, event | category | flops | bytes accessed | tf_op | source)
XLA Modules:
  0.0 231.0 jit_solution(2312803932554462114)
XLA Ops:
  1.4 23.2 %all_to_all.55 = bf16[8,32,256]{2,1,0:T(8,128)(2,1)S(1)} all-to-all(bf16[8,32,256]{2,1,0:T(8,128)(2,1)S(1)} %broadcast_in_dim.18), channel_id=1, replica_groups=mesh['row_0'=8,'row_1'=4,'col_0'=2,'col_1'=4,'col_2'=2] {'row_0'}, dimensions={0} | all-to-all | bytes 262144 | tf_op jit(solution)/shard_map/all_to_all | solution.py:24
  25.4 4.3 %all-to-all-start.1 = ((bf16[4,8,32,256]{3,2,1,0:T(8,128)(2,1)}), bf16[4,8,32,256]{3,2,1,0:T(8,128)(2,1)S(1)}, u32[]{:S(2)}, u32[]{:S(2)}) async-start(bf16[4,8,32,256]{3,2,1,0:T(8,128)(2,1)} %broadcast_in_dim.19), calls=%async_computation.1 | async-start | bytes 1048576 | tf_op jit(solution)/shard_map/all_to_all | solution.py:24
  29.7 7.9 %collective-permute-start = (bf16[32,256]{1,0:T(8,128)(2,1)S(1)}, bf16[32,256]{1,0:T(8,128)(2,1)S(1)}, u32[]{:S(2)}, u32[]{:S(2)}) collective-permute-start(bf16[32,256]{1,0:T(8,128)(2,1)S(1)} %copy-done.4), channel_id=1, source_target_pairs={{0,8},{8,0},{1,9},{9,1},{2,10},{10,2},{3,11},{11,3},{4,12},{12,4},... | collective-permute-start | bytes 49160 | tf_op jit(solution)/shard_map/ppermute | solution.py:33
  39.0 3.9 %collective-permute-done = bf16[32,256]{1,0:T(8,128)(2,1)S(1)} collective-permute-done((bf16[32,256]{1,0:T(8,128)(2,1)S(1)}, bf16[32,256]{1,0:T(8,128)(2,1)S(1)}, u32[]{:S(2)}, u32[]{:S(2)}) %collective-permute-start) | collective-permute-done | bytes 16416 | tf_op jit(solution)/shard_map/ppermute | solution.py:33
  46.6 18.0 %all_to_all.56.row_ref = bf16[8,4,32,256]{3,2,1,0:T(8,128)(2,1)} all-to-all(bf16[8,4,32,256]{3,2,1,0:T(8,128)(2,1)} %get-tuple-element.13), channel_id=1, replica_groups=mesh['row_0'=8,'row_1'=4,'col_0'=2,'col_1'=4,'col_2'=2] {'col_1','col_2'}, dimensions={0} | all-to-all | bytes 1048576 | tf_op jit(solution)/shard_map/all_to_all | solution.py:24
  66.9 12.2 %all_to_all.57 = bf16[4,8,32,256]{3,2,1,0:T(8,128)(2,1)S(1)} all-to-all(bf16[4,8,32,256]{3,2,1,0:T(8,128)(2,1)} %get-tuple-element.17), channel_id=1, replica_groups=mesh['row_0'=8,'row_1'=4,'col_0'=2,'col_1'=4,'col_2'=2] {'row_1'}, dimensions={0} | all-to-all | bytes 1048576 | tf_op jit(solution)/shard_map/all_to_all | solution.py:24
  79.8 4.2 %all-to-all-start.4 = ((bf16[8,32,256]{2,1,0:T(8,128)(2,1)}), bf16[8,32,256]{2,1,0:T(8,128)(2,1)S(1)}, u32[]{:S(2)}, u32[]{:S(2)}) async-start(bf16[8,32,256]{2,1,0:T(8,128)(2,1)} %reduce_sum.98), calls=%async_computation.4 | async-start | bytes 262144 | tf_op jit(solution)/shard_map/all_to_all | solution.py:24
  84.1 7.9 %collective-permute-start.1 = (bf16[1,32,256]{2,1,0:T(8,128)(2,1)S(1)}, bf16[1,32,256]{2,1,0:T(8,128)(2,1)S(1)}, u32[]{:S(2)}, u32[]{:S(2)}) collective-permute-start(bf16[1,32,256]{2,1,0:T(8,128)(2,1)S(1)} %copy-done.10), channel_id=1, source_target_pairs={{0,8},{8,0},{1,9},{9,1},{2,10},{10,2},{3,11},{11,3},{4,12},{12,4},... | collective-permute-start | bytes 49160 | tf_op jit(solution)/shard_map/ppermute | solution.py:33
  94.3 2.9 %collective-permute-done.1 = bf16[1,32,256]{2,1,0:T(8,128)(2,1)S(1)} collective-permute-done((bf16[1,32,256]{2,1,0:T(8,128)(2,1)S(1)}, bf16[1,32,256]{2,1,0:T(8,128)(2,1)S(1)}, u32[]{:S(2)}, u32[]{:S(2)}) %collective-permute-start.1) | collective-permute-done | bytes 16416 | tf_op jit(solution)/shard_map/ppermute | solution.py:33
  97.6 21.2 %all_to_all.58 = bf16[8,2,32,256]{3,2,1,0:T(8,128)(2,1)S(1)} all-to-all(bf16[8,2,32,256]{3,2,1,0:T(8,128)(2,1)S(1)} %broadcast_in_dim.21), channel_id=1, replica_groups=mesh['row_0'=8,'row_1'=4,'col_0'=2,'col_1'=4,'col_2'=2] {'row_0'}, dimensions={0} | all-to-all | bytes 524288 | tf_op jit(solution)/shard_map/all_to_all | solution.py:24
  119.9 3.5 %all-to-all-start.6 = ((bf16[4,9,32,256]{3,2,1,0:T(8,128)(2,1)}), bf16[4,9,32,256]{3,2,1,0:T(8,128)(2,1)S(1)}, u32[]{:S(2)}, u32[]{:S(2)}) async-start(bf16[4,9,32,256]{3,2,1,0:T(8,128)(2,1)} %broadcast_in_dim.23), calls=%async_computation.6 | async-start | bytes 1179648 | tf_op jit(solution)/shard_map/all_to_all | solution.py:24
  123.4 7.9 %collective-permute-start.2 = (bf16[32,256]{1,0:T(8,128)(2,1)S(1)}, bf16[32,256]{1,0:T(8,128)(2,1)S(1)}, u32[]{:S(2)}, u32[]{:S(2)}) collective-permute-start(bf16[32,256]{1,0:T(8,128)(2,1)S(1)} %get-tuple-element.23), channel_id=1, source_target_pairs={{0,8},{8,0},{1,9},{9,1},{2,10},{10,2},{3,11},{11,3},{4,12},{12,4},... | collective-permute-start | bytes 49160 | tf_op jit(solution)/shard_map/ppermute | solution.py:33
  131.5 5.1 %collective-permute-done.2 = bf16[32,256]{1,0:T(8,128)(2,1)S(1)} collective-permute-done((bf16[32,256]{1,0:T(8,128)(2,1)S(1)}, bf16[32,256]{1,0:T(8,128)(2,1)S(1)}, u32[]{:S(2)}, u32[]{:S(2)}) %collective-permute-start.2) | collective-permute-done | bytes 16416 | tf_op jit(solution)/shard_map/ppermute | solution.py:33
  139.6 23.4 %all_to_all.59.row_ref = bf16[8,5,32,256]{3,2,1,0:T(8,128)(2,1)} all-to-all(bf16[8,5,32,256]{3,2,1,0:T(8,128)(2,1)} %get-tuple-element.18), channel_id=1, replica_groups=mesh['row_0'=8,'row_1'=4,'col_0'=2,'col_1'=4,'col_2'=2] {'col_1','col_2'}, dimensions={0} | all-to-all | bytes 1310720 | tf_op jit(solution)/shard_map/all_to_all | solution.py:24
  163.0 2.5 %mirror_products.3 = (bf16[4,9,32,256]{3,2,1,0:T(8,128)(2,1)}, f32[32,256]{1,0:T(8,128)}, bf16[2,32,256]{2,1,0:T(8,128)(2,1)}) custom-call(s32[9]{0:T(128)} %pad_add_fusion.pair_ref, bf16[8,5,32,256]{3,2,1,0:T(8,128)(2,1)} %all_to_all.59.row_ref, bf16[4,256,256]{2,1,0:T(8,128)(2,1)} %bitcast.62, f32[4,32,256]{2,1,0:T(8,128)} %get-tuple-element.19.direct_ref), custom_call_target="tpu_custom_call" | custom-call | tf_op jit(solution)/shard_map/mirror_products/pallas_call | solution.py:173
  165.5 4.6 %all-to-all-start.8 = ((bf16[4,9,32,256]{3,2,1,0:T(8,128)(2,1)}), bf16[4,9,32,256]{3,2,1,0:T(8,128)(2,1)S(1)}, u32[]{:S(2)}, u32[]{:S(2)}) async-start(bf16[4,9,32,256]{3,2,1,0:T(8,128)(2,1)} %get-tuple-element.22), calls=%async_computation.8 | async-start | bytes 1179648 | tf_op jit(solution)/shard_map/all_to_all | solution.py:24
  170.1 7.8 %collective-permute-start.3 = (bf16[2,32,256]{2,1,0:T(8,128)(2,1)S(1)}, bf16[2,32,256]{2,1,0:T(8,128)(2,1)S(1)}, u32[]{:S(2)}, u32[]{:S(2)}) collective-permute-start(bf16[2,32,256]{2,1,0:T(8,128)(2,1)S(1)} %copy-done.7), channel_id=1, source_target_pairs={{0,8},{8,0},{1,9},{9,1},{2,10},{10,2},{3,11},{11,3},{4,12},{12,4},... | collective-permute-start | bytes 98312 | tf_op jit(solution)/shard_map/ppermute | solution.py:33
  177.9 5.7 %collective-permute-done.3 = bf16[2,32,256]{2,1,0:T(8,128)(2,1)S(1)} collective-permute-done((bf16[2,32,256]{2,1,0:T(8,128)(2,1)S(1)}, bf16[2,32,256]{2,1,0:T(8,128)(2,1)S(1)}, u32[]{:S(2)}, u32[]{:S(2)}) %collective-permute-start.3) | collective-permute-done | bytes 32800 | tf_op jit(solution)/shard_map/ppermute | solution.py:33
  184.7 3.4 %all-to-all-start.9 = ((bf16[8,2,32,256]{3,2,1,0:T(8,128)(2,1)}), bf16[8,2,32,256]{3,2,1,0:T(8,128)(2,1)S(1)}, u32[]{:S(2)}, u32[]{:S(2)}) async-start(bf16[8,2,32,256]{3,2,1,0:T(8,128)(2,1)} %pad_maximum_fusion), calls=%async_computation.9 | async-start | bytes 524288 | tf_op jit(solution)/shard_map/all_to_all | solution.py:24
  188.3 2.9 %cholesky.17 = f32[32,32]{1,0:T(8,128)S(1)} custom-call(f32[32,32]{1,0:T(8,128)S(1)} %fusion.53), custom_call_target="Cholesky" | custom-call | tf_op jit(solution)/shard_map/jit(cholesky)/cholesky | solution.py:213
  192.5 2.4 %custom-call.6 = f32[1,32,32]{1,2,0:T(8,128)S(1)} custom-call(f32[1,32,32]{2,1,0:T(8,128)S(1)} %fusion.22), custom_call_target="InvertDiagBlocksLowerTriangular" | custom-call | tf_op jit(solution)/shard_map/triangular_solve | solution.py:214
  195.2 4.8 %all-to-all-done.9 = bf16[8,2,32,256]{3,2,1,0:T(8,128)(2,1)S(1)} async-done(((bf16[8,2,32,256]{3,2,1,0:T(8,128)(2,1)}), bf16[8,2,32,256]{3,2,1,0:T(8,128)(2,1)S(1)}, u32[]{:S(2)}, u32[]{:S(2)}) %all-to-all-start.9) | async-done | bytes 262176 | tf_op jit(solution)/shard_map/all_to_all | solution.py:24
  201.0 13.7 %all-to-all-start.10 = ((bf16[16,32,128]{2,1,0:T(8,128)(2,1)}), bf16[16,32,128]{2,1,0:T(8,128)(2,1)S(1)}, u32[]{:S(2)}, u32[]{:S(2)}) async-start(bf16[16,32,128]{2,1,0:T(8,128)(2,1)} %broadcast_in_dim.48), calls=%async_computation.10 | async-start | bytes 262144 | tf_op jit(solution)/shard_map/all_to_all | solution.py:24
  215.7 13.8 %all-to-all-done.10 = bf16[16,32,128]{2,1,0:T(8,128)(2,1)S(1)} async-done(((bf16[16,32,128]{2,1,0:T(8,128)(2,1)}), bf16[16,32,128]{2,1,0:T(8,128)(2,1)S(1)}, u32[]{:S(2)}, u32[]{:S(2)}) %all-to-all-start.10) | async-done | bytes 131104 | tf_op jit(solution)/shard_map/all_to_all | solution.py:24
  (86 shorter events, 22.8 us)
Async XLA Ops:
  25.4 4.3 %copy-start.4 = (bf16[32,256]{1,0:T(8,128)(2,1)S(1)}, bf16[32,256]{1,0:T(8,128)(2,1)}, u32[]{:S(2)}) copy-start(bf16[32,256]{1,0:T(8,128)(2,1)} %param.7) | copy-start | bytes 49156
  25.4 18.1 %all-to-all-start.1 = ((bf16[4,8,32,256]{3,2,1,0:T(8,128)(2,1)}), bf16[4,8,32,256]{3,2,1,0:T(8,128)(2,1)S(1)}, u32[]{:S(2)}, u32[]{:S(2)}) async-start(bf16[4,8,32,256]{3,2,1,0:T(8,128)(2,1)} %broadcast_in_dim.19), calls=%async_computation.1 | async-start | bytes 1048576 | tf_op jit(solution)/shard_map/all_to_all | solution.py:24
  29.7 13.2 %collective-permute-start = (bf16[32,256]{1,0:T(8,128)(2,1)S(1)}, bf16[32,256]{1,0:T(8,128)(2,1)S(1)}, u32[]{:S(2)}, u32[]{:S(2)}) collective-permute-start(bf16[32,256]{1,0:T(8,128)(2,1)S(1)} %copy-done.4), channel_id=1, source_target_pairs={{0,8},{8,0},{1,9},{9,1},{2,10},{10,2},{3,11},{11,3},{4,12},{12,4},... | collective-permute-start | bytes 49160 | tf_op jit(solution)/shard_map/ppermute | solution.py:33
  37.7 0.7 copy-start.8
  37.7 0.7 copy-start.9
  43.5 0.8 copy-start.1
  79.8 4.2 %copy-start.10 = (bf16[1,32,256]{2,1,0:T(8,128)(2,1)S(1)}, bf16[1,32,256]{2,1,0:T(8,128)(2,1)}, u32[]{:S(2)}) copy-start(bf16[1,32,256]{2,1,0:T(8,128)(2,1)} %get-tuple-element.16) | copy-start | bytes 49156
  79.8 14.5 %all-to-all-start.4 = ((bf16[8,32,256]{2,1,0:T(8,128)(2,1)}), bf16[8,32,256]{2,1,0:T(8,128)(2,1)S(1)}, u32[]{:S(2)}, u32[]{:S(2)}) async-start(bf16[8,32,256]{2,1,0:T(8,128)(2,1)} %reduce_sum.98), calls=%async_computation.4 | async-start | bytes 262144 | tf_op jit(solution)/shard_map/all_to_all | solution.py:24
  84.1 13.2 %copy-start.6 = (f32[32,256]{1,0:T(8,128)S(1)}, f32[32,256]{1,0:T(8,128)}, u32[]{:S(2)}) copy-start(f32[32,256]{1,0:T(8,128)} %get-tuple-element.15) | copy-start | bytes 98308
  84.1 13.2 %collective-permute-start.1 = (bf16[1,32,256]{2,1,0:T(8,128)(2,1)S(1)}, bf16[1,32,256]{2,1,0:T(8,128)(2,1)S(1)}, u32[]{:S(2)}, u32[]{:S(2)}) collective-permute-start(bf16[1,32,256]{2,1,0:T(8,128)(2,1)S(1)} %copy-done.10), channel_id=1, source_target_pairs={{0,8},{8,0},{1,9},{9,1},{2,10},{10,2},{3,11},{11,3},{4,12},{12,4},... | collective-permute-start | bytes 49160 | tf_op jit(solution)/shard_map/ppermute | solution.py:33
  119.9 11.4 %all-to-all-start.6 = ((bf16[4,9,32,256]{3,2,1,0:T(8,128)(2,1)}), bf16[4,9,32,256]{3,2,1,0:T(8,128)(2,1)S(1)}, u32[]{:S(2)}, u32[]{:S(2)}) async-start(bf16[4,9,32,256]{3,2,1,0:T(8,128)(2,1)} %broadcast_in_dim.23), calls=%async_computation.6 | async-start | bytes 1179648 | tf_op jit(solution)/shard_map/all_to_all | solution.py:24
  123.4 13.2 %collective-permute-start.2 = (bf16[32,256]{1,0:T(8,128)(2,1)S(1)}, bf16[32,256]{1,0:T(8,128)(2,1)S(1)}, u32[]{:S(2)}, u32[]{:S(2)}) collective-permute-start(bf16[32,256]{1,0:T(8,128)(2,1)S(1)} %get-tuple-element.23), channel_id=1, source_target_pairs={{0,8},{8,0},{1,9},{9,1},{2,10},{10,2},{3,11},{11,3},{4,12},{12,4},... | collective-permute-start | bytes 49160 | tf_op jit(solution)/shard_map/ppermute | solution.py:33
  131.3 5.9 %copy-start = (bf16[4,9,32,256]{3,2,1,0:T(8,128)(2,1)}, bf16[4,9,32,256]{3,2,1,0:T(8,128)(2,1)S(1)}, u32[]{:S(2)}) copy-start(bf16[4,9,32,256]{3,2,1,0:T(8,128)(2,1)S(1)} %all-to-all-done.6.column_ref) | copy-start | bytes 1769476
  165.5 4.6 %copy-start.7 = (bf16[2,32,256]{2,1,0:T(8,128)(2,1)S(1)}, bf16[2,32,256]{2,1,0:T(8,128)(2,1)}, u32[]{:S(2)}) copy-start(bf16[2,32,256]{2,1,0:T(8,128)(2,1)} %get-tuple-element.20) | copy-start | bytes 98308
  165.5 18.2 %all-to-all-start.8 = ((bf16[4,9,32,256]{3,2,1,0:T(8,128)(2,1)}), bf16[4,9,32,256]{3,2,1,0:T(8,128)(2,1)S(1)}, u32[]{:S(2)}, u32[]{:S(2)}) async-start(bf16[4,9,32,256]{3,2,1,0:T(8,128)(2,1)} %get-tuple-element.22), calls=%async_computation.8 | async-start | bytes 1179648 | tf_op jit(solution)/shard_map/all_to_all | solution.py:24
  170.1 13.5 %collective-permute-start.3 = (bf16[2,32,256]{2,1,0:T(8,128)(2,1)S(1)}, bf16[2,32,256]{2,1,0:T(8,128)(2,1)S(1)}, u32[]{:S(2)}, u32[]{:S(2)}) collective-permute-start(bf16[2,32,256]{2,1,0:T(8,128)(2,1)S(1)} %copy-done.7), channel_id=1, source_target_pairs={{0,8},{8,0},{1,9},{9,1},{2,10},{10,2},{3,11},{11,3},{4,12},{12,4},... | collective-permute-start | bytes 98312 | tf_op jit(solution)/shard_map/ppermute | solution.py:33
  184.7 15.3 %all-to-all-start.9 = ((bf16[8,2,32,256]{3,2,1,0:T(8,128)(2,1)}), bf16[8,2,32,256]{3,2,1,0:T(8,128)(2,1)S(1)}, u32[]{:S(2)}, u32[]{:S(2)}) async-start(bf16[8,2,32,256]{3,2,1,0:T(8,128)(2,1)} %pad_maximum_fusion), calls=%async_computation.9 | async-start | bytes 524288 | tf_op jit(solution)/shard_map/all_to_all | solution.py:24
  201.0 28.6 %all-to-all-start.10 = ((bf16[16,32,128]{2,1,0:T(8,128)(2,1)}), bf16[16,32,128]{2,1,0:T(8,128)(2,1)S(1)}, u32[]{:S(2)}, u32[]{:S(2)}) async-start(bf16[16,32,128]{2,1,0:T(8,128)(2,1)} %broadcast_in_dim.48), calls=%async_computation.10 | async-start | bytes 262144 | tf_op jit(solution)/shard_map/all_to_all | solution.py:24
  214.8 15.4 %copy-start.2 = (f32[32,256]{1,0:T(8,128)}, f32[32,256]{1,0:T(8,128)S(1)}, u32[]{:S(2)}) copy-start(f32[32,256]{1,0:T(8,128)S(1)} %fusion.60) | copy-start | bytes 98308
  214.8 0.8 copy-start.5
  230.2 0.9 copy-start.3

commit v3 on v2

v3 whole, which is shorter than its diff:
```python
import functools

import jax
import jax.numpy as jnp
from jax import lax
from jax.experimental import pallas as pl
from jax.experimental.pallas import tpu as pltpu
from jax.sharding import Mesh
from jax.sharding import PartitionSpec as P

Z_HI, X_CORE = ("col_0", ("col_1", "col_2"))
Z_LO, Y = ("row_0", "row_1")
Y_X_CORE = ("row_1", "col_1", "col_2")
COL = ("col_0", "col_1", "col_2")
ROW = ("row_0", "row_1")
COL_ROW = ("col_0", "col_1", "col_2", "row_0", "row_1")
HIGHEST = lax.Precision.HIGHEST
VMEM = pl.BlockSpec(memory_space=pltpu.VMEM)
SMEM = pl.BlockSpec(memory_space=pltpu.SMEM)
F32, BF16 = (jnp.float32, jnp.bfloat16)


def placed(value):
    return pltpu.with_memory_space_constraint(value, pltpu.VMEM)


ROWS, LANES, VECTORS = (8, 128, 32)


def exchange(parts, axis):
    return lax.all_to_all(parts, axis, 0, 0, tiled=True)


def call(kernel, *outs, scalars=0, scratch=(), out=pltpu.VMEM):
    def run(*args):
        args = args[:scalars] + tuple(placed(arg) for arg in args[scalars:])
        return pl.pallas_call(
            kernel,
            out_shape=tuple(out(shape, kind) for shape, kind in outs),
            in_specs=[SMEM] * scalars + [VMEM] * (len(args) - scalars),
            out_specs=tuple(VMEM for _ in outs),
            scratch_shapes=list(scratch),
        )(*args)

    return run


def spread(value, axis):
    length = lax.axis_size(axis)
    return exchange(jnp.broadcast_to(value[None], (length, *value.shape)), axis)


def partner(value):
    return lax.ppermute(value, Z_HI, [(0, 1), (1, 0)])


def pack(small):
    return jnp.concatenate([small[k : k + ROWS] for k in range(0, small.shape[0], ROWS)], axis=1)


def unpack(packed):
    return jnp.concatenate([packed[:, k : k + VECTORS] for k in range(0, LANES, VECTORS)], axis=0)


def from_bits(bits):
    wide = bits.astype(F32)
    return wide[..., LANES:] + wide[..., :LANES]


def dot(left, right, left_dim, right_dim):
    return lax.dot_general(
        left, right, (((left_dim,), (right_dim,)), ((), ())),
        precision=HIGHEST, preferred_element_type=F32,
    )


def store_bits(out_ref, place, packed):
    high = packed.astype(BF16)
    out_ref[(*place, slice(0, LANES))] = high
    out_ref[(*place, slice(LANES, 2 * LANES))] = (packed - high.astype(F32)).astype(BF16)


def store_sums(out_ref, slots, sums_ref):
    for t, (index, place) in enumerate(slots):
        total = sums_ref[t]
        for other, (other_index, _) in enumerate(slots):
            if other != t:
                total = total + (other_index == index).astype(F32) * sums_ref[other]
        out_ref[place] = total.astype(BF16)


def span(slot, length, start=0):
    return pl.ds(pl.multiple_of(start + slot * length, length), length)


def direct_kernel(pair_ref, column_ref, tile_ref, own_ref, other_ref, out_ref, sums_ref):
    tiles, vectors = (tile_ref.shape[0], own_ref.shape[0])
    y_count, z_count, xc_count = (*column_ref.shape[:2], out_ref.shape[0])
    side = pair_ref[2 * tiles]
    for t in range(tiles):
        j = pair_ref[tiles + t]
        from_column = column_ref[lax.rem(j, y_count), lax.div(j, y_count), pl.ds(0, vectors)]
        sums_ref[t] = lax.dot_general(
            from_column, tile_ref[t], (((1,), (1,)), ((), ())), preferred_element_type=F32
        )
    blank = jnp.zeros((2 * vectors, out_ref.shape[2]), BF16)
    for k in range(xc_count):
        out_ref[k, pl.ds(0, vectors)] = own_ref[...]
        out_ref[k, pl.ds(vectors, vectors)] = other_ref[...]
        out_ref[k, pl.ds(2 * vectors, 2 * vectors)] = blank
    if out_ref.shape[1] > 4 * vectors:
        total = jnp.zeros((ROWS, LANES), F32)
        for y in range(y_count):
            for z in range(z_count):
                total += from_bits(column_ref[y, z, pl.ds(vectors, ROWS)])
        for k in range(xc_count):
            store_bits(out_ref, (k, pl.ds(4 * vectors, ROWS)), total)
    slots = []
    for t in range(tiles):
        i = pair_ref[t]
        half = lax.rem(lax.div(i, xc_count) + side, 2)
        slots.append((i, (lax.rem(i, xc_count), span(half, vectors, 2 * vectors))))
    store_sums(out_ref, slots, sums_ref)


def mirror_kernel(
    pair_ref, row_ref, tile_ref, direct_ref, out_ref, own_ref, far_ref, sums_ref
):
    tiles, vectors = (tile_ref.shape[0], own_ref.shape[0])
    y_count, xc_count = (out_ref.shape[0], row_ref.shape[0])
    extra = row_ref.shape[1] > 4 * vectors
    side = pair_ref[2 * tiles]
    form = jnp.zeros((vectors, vectors), F32)
    for t in range(tiles):
        i = pair_ref[t]
        half = lax.rem(lax.div(i, xc_count) + side, 2)
        from_row = row_ref[lax.rem(i, xc_count), span(half, vectors)]
        sums_ref[t] = jnp.dot(from_row, tile_ref[t], preferred_element_type=F32)
        if extra:
            form += dot(from_row.astype(F32), direct_ref[t], 1, 1)
    for s in range(2):
        rows = pl.ds((2 + s) * vectors, vectors)
        total = row_ref[0, rows].astype(F32)
        for k in range(1, xc_count):
            total = total + row_ref[k, rows].astype(F32)
        if s == 0:
            own_ref[...] = total
        else:
            far_ref[pl.ds(0, vectors)] = total.astype(BF16)
    if extra:
        total = jnp.zeros((ROWS, LANES), F32)
        for k in range(xc_count):
            total += from_bits(row_ref[k, pl.ds(4 * vectors, ROWS)])
        store_bits(far_ref, (pl.ds(vectors, ROWS),), total)
        store_bits(far_ref, (pl.ds(vectors + ROWS, ROWS),), pack(form))
    for k in range(y_count):
        out_ref[k] = jnp.zeros(out_ref.shape[1:], BF16)
    slots = []
    for t in range(tiles):
        j = pair_ref[tiles + t]
        slots.append((j, (lax.rem(j, y_count), lax.div(j, y_count))))
    store_sums(out_ref, slots, sums_ref)


def image_kernel(direct_ref, far_ref, mirror_ref, image_ref, current_ref, send_ref):
    image = direct_ref[...] + far_ref[...].astype(F32)
    for z in range(mirror_ref.shape[0]):
        image = image + mirror_ref[z].astype(F32)
    image_ref[...] = image
    current = image.astype(BF16)
    current_ref[...] = current
    gram = pack(dot(image, image, 1, 1))
    for z in range(send_ref.shape[0]):
        send_ref[z, pl.ds(0, image.shape[0])] = current
        store_bits(send_ref, (z, pl.ds(image.shape[0], ROWS)), gram)


def middle_kernel(mirror_ref, sent_ref, far_ref, send_ref, gram_ref):
    vectors = gram_ref.shape[0]
    for z in range(send_ref.shape[0]):
        total = mirror_ref[0, z].astype(F32)
        for y in range(1, mirror_ref.shape[0]):
            total = total + mirror_ref[y, z].astype(F32)
        send_ref[z, pl.ds(0, vectors)] = total.astype(BF16)
    rows = pl.ds(vectors, ROWS)
    gram_ref[...] = unpack(from_bits(sent_ref[rows]) + from_bits(far_ref[rows]))
    rows = pl.ds(vectors + ROWS, ROWS)
    form = from_bits(sent_ref[rows]) + from_bits(far_ref[rows])
    for z in range(send_ref.shape[0]):
        store_bits(send_ref, (z, pl.ds(vectors, ROWS)), form)


def last_kernel(direct_ref, far_ref, mirror_ref, image_ref, send_ref):
    vectors = image_ref.shape[0]
    form = jnp.zeros((ROWS, LANES), F32)
    for z in range(mirror_ref.shape[0]):
        form += from_bits(mirror_ref[z, pl.ds(vectors, ROWS)])
    for k in range(send_ref.shape[0]):
        store_bits(send_ref, (k, pl.ds(0, ROWS)), form)
    image = direct_ref[...] + far_ref[pl.ds(0, vectors)].astype(F32)
    for z in range(mirror_ref.shape[0]):
        image = image + mirror_ref[z, pl.ds(0, vectors)].astype(F32)
    image_ref[...] = image


def finish_kernel(bits_ref, inverse_ref, ritz_ref, last_ref, residual_ref, projected_ref, *, rows):
    form = jnp.zeros((ROWS, LANES), F32)
    for k in range(bits_ref.shape[0]):
        form += from_bits(bits_ref[k])
    inverse = inverse_ref[...]
    half = dot(inverse, unpack(form), 1, 0)
    projected = (dot(half, inverse, 1, 1) + dot(inverse, half, 1, 1)) * (1.0 / rows)
    projected_ref[...] = projected
    residual_ref[...] = last_ref[...] - dot(projected, ritz_ref[...], 0, 0)


def product(pairs, tiles, current, send_z):
    vectors, size = current.shape
    count = tiles.shape[0]
    y_count, z_count, xc_count = (lax.axis_size(Y), lax.axis_size(Z_LO), lax.axis_size(X_CORE))
    extra = send_z is not None
    if not extra:
        send_z = jnp.broadcast_to(current[None], (z_count, *current.shape))
    by_z = exchange(send_z, Z_LO)
    other = partner(current)
    column_block = spread(by_z, Y)
    send, direct = call(
        direct_kernel,
        ((xc_count, 4 * vectors + ROWS * extra, size), BF16),
        ((count, vectors, size), F32),
        scalars=1,
    )(pairs, column_block, tiles, current, other)
    arrived = exchange(send, X_CORE)
    send, own_direct, far = call(
        mirror_kernel,
        ((y_count, z_count, vectors, size), BF16),
        ((vectors, size), F32),
        ((vectors + 2 * ROWS * extra, size), BF16),
        scalars=1,
        scratch=[pltpu.VMEM((count, vectors, size), F32)],
    )(pairs, arrived, tiles, direct)
    mirror = exchange(send, Y)
    sent, far = (far, partner(far))
    if extra:
        mirror, gram = call(
            middle_kernel,
            ((z_count, vectors + ROWS, size), BF16),
            ((vectors, vectors), F32),
        )(mirror, sent, far)
    else:
        mirror, gram = (mirror.astype(F32).sum(axis=0).astype(BF16), None)
    mirror = exchange(mirror, Z_LO)
    return own_direct, far, mirror, gram


def steps(tile_values, tile_row, tile_col, basis_init):
    tiles = tile_values[0, 0]
    side = lax.axis_index(Z_HI).astype(jnp.int32)
    pairs = jnp.concatenate([tile_row[0, 0], tile_col[0, 0], side[None]])
    vectors, size = basis_init.shape
    total_rows = size * lax.axis_size(COL_ROW)

    own_direct, far, mirror, _ = product(pairs, tiles, basis_init, None)
    image, current, send = call(
        image_kernel,
        ((vectors, size), F32),
        ((vectors, size), BF16),
        ((mirror.shape[0], vectors + ROWS, size), BF16),
    )(own_direct, far, mirror)
    own_direct, far, mirror, gram = product(pairs, tiles, current, send)
    raw_image, send = call(
        last_kernel,
        ((vectors, size), F32),
        ((lax.axis_size(Y_X_CORE), ROWS, 2 * LANES), BF16),
    )(own_direct, far, mirror)
    form = exchange(send, Y_X_CORE)
    factor = jnp.linalg.cholesky(gram / total_rows)
    inverse = lax.linalg.triangular_solve(
        factor, jnp.eye(vectors, dtype=F32), left_side=True, lower=True
    )
    ritz_basis = jnp.dot(inverse, image, precision=HIGHEST)
    last_image = jnp.dot(inverse, raw_image, precision=HIGHEST)
    residual, projected = call(
        functools.partial(finish_kernel, rows=total_rows),
        ((vectors, size), F32),
        ((vectors, vectors), F32),
        out=jax.ShapeDtypeStruct,
    )(form, inverse, ritz_basis, last_image)
    return (ritz_basis, residual, projected)


def solution(mesh):
    finer = Mesh(mesh.devices.reshape(8, 4, 2, 4, 2), ("row_0", "row_1", "col_0", "col_1", "col_2"))
    placed = (P(ROW, COL, None, None, None), P(ROW, COL, None), P(ROW, COL, None), P(None, COL_ROW))
    return jax.shard_map(
        steps,
        mesh=finer,
        in_specs=placed,
        out_specs=(P(None, COL_ROW), P(None, COL_ROW), P()),
        check_vma=False,
    )
```

time: 235 us -> 204 us (0.87); the launches traced: 231 us -> 203 us
  waiting for transfers between devices: 38.7 us -> 31.1 us
  blocking collectives: 98 us -> 91.9 us
  starting transfers between devices: 65.1 us -> 60.1 us
  other arithmetic: 11.5 us -> 8.02 us
    all_to_all x6, waiting for transfers between devices: 21 us -> 10.9 us  [exchange(): return lax.all_to_all(parts, axis, 0, 0, tiled=True)]
    all_to_all x5, blocking collectives: 98 us -> 91.9 us  [exchange(): return lax.all_to_all(parts, axis, 0, 0, tiled=True)]
    all_to_all x6, starting transfers between devices: 33.7 us -> 28.6 us  [exchange(): return lax.all_to_all(parts, axis, 0, 0, tiled=True)]
    ppermute x4, waiting for transfers between devices: 17.6 us -> 20.2 us  [partner(): return lax.ppermute(value, Z_HI, [(0, 1), (1, 0)])]
    pallas_call x4 -> x8, Pallas kernels: 9.41 us -> 7.51 us  [run(): pl.pallas_call(kernel, out_shape=tuple((out(shape, kind) for shape, kind...]
  transfers between devices with their start and end apart: 10 -> 10, of which waited for: 7 -> 6; matrix products, arithmetic and copies ran while one was open for 4% -> 4% of each run, Pallas kernels for 0% -> 0%
where the time goes in v3:
time: 204 us; the launch traced here: 203 us
  blocking collectives  91.9 us (45%)
  starting transfers between devices  60.1 us (29%)
  waiting for transfers between devices  31.1 us (15%)
  other arithmetic  8.02 us (4%)
  Pallas kernels  7.51 us (4%)
  local copies, waits for them, and re-layouts  3.29 us (2%)
    all_to_all x5, blocking collectives, exchange(): return lax.all_to_all(parts, axis, 0, 0, tiled=True)  91.9 us
    ppermute x4, starting transfers between devices, partner(): return lax.ppermute(value, Z_HI, [(0, 1), (1, 0)])  31.5 us
    all_to_all x6, starting transfers between devices, exchange(): return lax.all_to_all(parts, axis, 0, 0, tiled=True)  28.6 us
    ppermute x4, waiting for transfers between devices, partner(): return lax.ppermute(value, Z_HI, [(0, 1), (1, 0)])  20.2 us
    all_to_all x6, waiting for transfers between devices, exchange(): return lax.all_to_all(parts, axis, 0, 0, tiled=True)  10.9 us
    pallas_call x8, Pallas kernels, run(): pl.pallas_call(kernel, out_shape=tuple((out(shape, kind) for shape, kind...  7.51 us
  transfers between devices with their start and end apart: 10, of which 6 were waited for; matrix products, arithmetic and copies ran while one was open for 4% of the time, Pallas kernels for 0%

profile of v3, /device:TPU:1, one launch (start us, length us, event | category | flops | bytes accessed | tf_op | source)
XLA Modules:
  0.0 203.2 jit_solution(4903504334529198168)
XLA Ops:
  1.4 23.2 %all_to_all.55 = bf16[8,32,256]{2,1,0:T(8,128)(2,1)S(1)} all-to-all(bf16[8,32,256]{2,1,0:T(8,128)(2,1)S(1)} %broadcast_in_dim.10), channel_id=1, replica_groups=mesh['row_0'=8,'row_1'=4,'col_0'=2,'col_1'=4,'col_2'=2] {'row_0'}, dimensions={0} | all-to-all | bytes 262144 | tf_op jit(solution)/shard_map/all_to_all | solution.py:31
  25.4 4.3 %all-to-all-start.1 = ((bf16[4,8,32,256]{3,2,1,0:T(8,128)(2,1)}), bf16[4,8,32,256]{3,2,1,0:T(8,128)(2,1)S(1)}, u32[]{:S(2)}, u32[]{:S(2)}) async-start(bf16[4,8,32,256]{3,2,1,0:T(8,128)(2,1)} %broadcast_in_dim.11), calls=%async_computation.1 | async-start | bytes 1048576 | tf_op jit(solution)/shard_map/all_to_all | solution.py:31
  29.7 7.9 %collective-permute-start = (bf16[32,256]{1,0:T(8,128)(2,1)S(1)}, bf16[32,256]{1,0:T(8,128)(2,1)S(1)}, u32[]{:S(2)}, u32[]{:S(2)}) collective-permute-start(bf16[32,256]{1,0:T(8,128)(2,1)S(1)} %copy-done.2), channel_id=1, source_target_pairs={{0,8},{8,0},{1,9},{9,1},{2,10},{10,2},{3,11},{11,3},{4,12},{12,4},... | collective-permute-start | bytes 49160 | tf_op jit(solution)/shard_map/ppermute | solution.py:54
  38.9 4.0 %collective-permute-done.other_ref = bf16[32,256]{1,0:T(8,128)(2,1)S(1)} collective-permute-done((bf16[32,256]{1,0:T(8,128)(2,1)S(1)}, bf16[32,256]{1,0:T(8,128)(2,1)S(1)}, u32[]{:S(2)}, u32[]{:S(2)}) %collective-permute-start) | collective-permute-done | bytes 16416 | tf_op jit(solution)/shard_map/ppermute | solution.py:54
  43.9 17.7 %all_to_all.56.row_ref = bf16[8,128,256]{2,1,0:T(8,128)(2,1)S(1)} all-to-all(bf16[8,128,256]{2,1,0:T(8,128)(2,1)S(1)} %get-tuple-element.22), channel_id=1, replica_groups=mesh['row_0'=8,'row_1'=4,'col_0'=2,'col_1'=4,'col_2'=2] {'col_1','col_2'}, dimensions={0} | all-to-all | bytes 1048576 | tf_op jit(solution)/shard_map/all_to_all | solution.py:31
  62.5 12.0 %all_to_all.57 = bf16[4,8,32,256]{3,2,1,0:T(8,128)(2,1)S(1)} all-to-all(bf16[4,8,32,256]{3,2,1,0:T(8,128)(2,1)S(1)} %get-tuple-element.26), channel_id=1, replica_groups=mesh['row_0'=8,'row_1'=4,'col_0'=2,'col_1'=4,'col_2'=2] {'row_1'}, dimensions={0} | all-to-all | bytes 1048576 | tf_op jit(solution)/shard_map/all_to_all | solution.py:31
  75.2 4.1 %all-to-all-start.4 = ((bf16[8,32,256]{2,1,0:T(8,128)(2,1)}), bf16[8,32,256]{2,1,0:T(8,128)(2,1)S(1)}, u32[]{:S(2)}, u32[]{:S(2)}) async-start(bf16[8,32,256]{2,1,0:T(8,128)(2,1)} %reduce_sum.12), calls=%async_computation.4 | async-start | bytes 262144 | tf_op jit(solution)/shard_map/all_to_all | solution.py:31
  79.3 7.8 %collective-permute-start.1 = (bf16[32,256]{1,0:T(8,128)(2,1)S(1)}, bf16[32,256]{1,0:T(8,128)(2,1)S(1)}, u32[]{:S(2)}, u32[]{:S(2)}) collective-permute-start(bf16[32,256]{1,0:T(8,128)(2,1)S(1)} %get-tuple-element.25), channel_id=1, source_target_pairs={{0,8},{8,0},{1,9},{9,1},{2,10},{10,2},{3,11},{11,3},{4,12},{12,4},... | collective-permute-start | bytes 49160 | tf_op jit(solution)/shard_map/ppermute | solution.py:54
  87.1 5.3 %collective-permute-done.1.far_ref = bf16[32,256]{1,0:T(8,128)(2,1)S(1)} collective-permute-done((bf16[32,256]{1,0:T(8,128)(2,1)S(1)}, bf16[32,256]{1,0:T(8,128)(2,1)S(1)}, u32[]{:S(2)}, u32[]{:S(2)}) %collective-permute-start.1) | collective-permute-done | bytes 16416 | tf_op jit(solution)/shard_map/ppermute | solution.py:54
  92.7 19.8 %all_to_all.58 = bf16[8,40,256]{2,1,0:T(8,128)(2,1)S(1)} all-to-all(bf16[8,40,256]{2,1,0:T(8,128)(2,1)S(1)} %get-tuple-element.27), channel_id=1, replica_groups=mesh['row_0'=8,'row_1'=4,'col_0'=2,'col_1'=4,'col_2'=2] {'row_0'}, dimensions={0} | all-to-all | bytes 327680 | tf_op jit(solution)/shard_map/all_to_all | solution.py:31
  113.4 3.5 %all-to-all-start.6 = ((bf16[4,8,40,256]{3,2,1,0:T(8,128)(2,1)}), bf16[4,8,40,256]{3,2,1,0:T(8,128)(2,1)S(1)}, u32[]{:S(2)}, u32[]{:S(2)}) async-start(bf16[4,8,40,256]{3,2,1,0:T(8,128)(2,1)} %broadcast_in_dim.12), calls=%async_computation.6 | async-start | bytes 1310720 | tf_op jit(solution)/shard_map/all_to_all | solution.py:31
  116.9 7.9 %collective-permute-start.2 = (bf16[32,256]{1,0:T(8,128)(2,1)S(1)}, bf16[32,256]{1,0:T(8,128)(2,1)S(1)}, u32[]{:S(2)}, u32[]{:S(2)}) collective-permute-start(bf16[32,256]{1,0:T(8,128)(2,1)S(1)} %get-tuple-element.28.own_ref), channel_id=1, source_target_pairs={{0,8},{8,0},{1,9},{9,1},{2,10},{10,2},{3,11},{11,3},{4,12},{12,4},... | collective-permute-start | bytes 49160 | tf_op jit(solution)/shard_map/ppermute | solution.py:54
  124.7 5.4 %collective-permute-done.2.other_ref = bf16[32,256]{1,0:T(8,128)(2,1)S(1)} collective-permute-done((bf16[32,256]{1,0:T(8,128)(2,1)S(1)}, bf16[32,256]{1,0:T(8,128)(2,1)S(1)}, u32[]{:S(2)}, u32[]{:S(2)}) %collective-permute-start.2) | collective-permute-done | bytes 16416 | tf_op jit(solution)/shard_map/ppermute | solution.py:54
  131.1 19.2 %all_to_all.59.row_ref = bf16[8,136,256]{2,1,0:T(8,128)(2,1)S(1)} all-to-all(bf16[8,136,256]{2,1,0:T(8,128)(2,1)S(1)} %get-tuple-element.29), channel_id=1, replica_groups=mesh['row_0'=8,'row_1'=4,'col_0'=2,'col_1'=4,'col_2'=2] {'col_1','col_2'}, dimensions={0} | all-to-all | bytes 1114112 | tf_op jit(solution)/shard_map/all_to_all | solution.py:31
  150.3 1.8 shard_map.71
  152.1 4.5 %all-to-all-start.8 = ((bf16[4,8,32,256]{3,2,1,0:T(8,128)(2,1)}), bf16[4,8,32,256]{3,2,1,0:T(8,128)(2,1)S(1)}, u32[]{:S(2)}, u32[]{:S(2)}) async-start(bf16[4,8,32,256]{3,2,1,0:T(8,128)(2,1)} %get-tuple-element.31), calls=%async_computation.8 | async-start | bytes 1048576 | tf_op jit(solution)/shard_map/all_to_all | solution.py:31
  156.5 7.8 %collective-permute-start.3 = (bf16[48,256]{1,0:T(8,128)(2,1)S(1)}, bf16[48,256]{1,0:T(8,128)(2,1)S(1)}, u32[]{:S(2)}, u32[]{:S(2)}) collective-permute-start(bf16[48,256]{1,0:T(8,128)(2,1)S(1)} %get-tuple-element.32.sent_ref), channel_id=1, source_target_pairs={{0,8},{8,0},{1,9},{9,1},{2,10},{10,2},{3,11},{11,3},{4,12},{12,4},... | collective-permute-start | bytes 73736 | tf_op jit(solution)/shard_map/ppermute | solution.py:54
  164.4 5.5 %collective-permute-done.3.far_ref = bf16[48,256]{1,0:T(8,128)(2,1)S(1)} collective-permute-done((bf16[48,256]{1,0:T(8,128)(2,1)S(1)}, bf16[48,256]{1,0:T(8,128)(2,1)S(1)}, u32[]{:S(2)}, u32[]{:S(2)}) %collective-permute-start.3) | collective-permute-done | bytes 24608 | tf_op jit(solution)/shard_map/ppermute | solution.py:54
  170.7 3.4 %all-to-all-start.9 = ((bf16[8,40,256]{2,1,0:T(8,128)(2,1)}), bf16[8,40,256]{2,1,0:T(8,128)(2,1)S(1)}, u32[]{:S(2)}, u32[]{:S(2)}) async-start(bf16[8,40,256]{2,1,0:T(8,128)(2,1)} %get-tuple-element.36), calls=%async_computation.9 | async-start | bytes 327680 | tf_op jit(solution)/shard_map/all_to_all | solution.py:31
  174.2 2.9 %cholesky.17 = f32[32,32]{1,0:T(8,128)S(1)} custom-call(f32[32,32]{1,0:T(8,128)S(1)} %fusion.3), custom_call_target="Cholesky" | custom-call | tf_op jit(solution)/shard_map/jit(cholesky)/cholesky | solution.py:277
  178.4 2.4 %custom-call.6 = f32[1,32,32]{1,2,0:T(8,128)S(1)} custom-call(f32[1,32,32]{2,1,0:T(8,128)S(1)} %fusion), custom_call_target="InvertDiagBlocksLowerTriangular" | custom-call | tf_op jit(solution)/shard_map/triangular_solve | solution.py:278
  181.3 3.4 %all-to-all-done.9.mirror_ref = bf16[8,40,256]{2,1,0:T(8,128)(2,1)S(1)} async-done(((bf16[8,40,256]{2,1,0:T(8,128)(2,1)}), bf16[8,40,256]{2,1,0:T(8,128)(2,1)S(1)}, u32[]{:S(2)}, u32[]{:S(2)}) %all-to-all-start.9) | async-done | bytes 163872 | tf_op jit(solution)/shard_map/all_to_all | solution.py:31
  185.4 8.9 %all-to-all-start.10 = ((bf16[32,8,256]{2,1,0:T(8,128)(2,1)}), bf16[32,8,256]{2,1,0:T(8,128)(2,1)S(1)}, u32[]{:S(2)}, u32[]{:S(2)}) async-start(bf16[32,8,256]{2,1,0:T(8,128)(2,1)} %get-tuple-element.37), calls=%async_computation.10 | async-start | bytes 262144 | tf_op jit(solution)/shard_map/all_to_all | solution.py:31
  194.5 7.4 %all-to-all-done.10.bits_ref = bf16[32,8,256]{2,1,0:T(8,128)(2,1)S(1)} async-done(((bf16[32,8,256]{2,1,0:T(8,128)(2,1)}), bf16[32,8,256]{2,1,0:T(8,128)(2,1)S(1)}, u32[]{:S(2)}, u32[]{:S(2)}) %all-to-all-start.10) | async-done | bytes 131104 | tf_op jit(solution)/shard_map/all_to_all | solution.py:31
  (36 shorter events, 12.3 us)
Async XLA Ops:
  25.4 4.3 %copy-start.2 = (bf16[32,256]{1,0:T(8,128)(2,1)S(1)}, bf16[32,256]{1,0:T(8,128)(2,1)}, u32[]{:S(2)}) copy-start(bf16[32,256]{1,0:T(8,128)(2,1)} %own_ref.1) | copy-start | bytes 49156
  25.4 17.5 %copy-start = (bf16[1,1,4,256,256]{4,3,2,1,0:T(8,128)(2,1)S(1)}, bf16[1,1,4,256,256]{4,3,2,1,0:T(8,128)(2,1)}, u32[]{:S(2)}) copy-start(bf16[1,1,4,256,256]{4,3,2,1,0:T(8,128)(2,1)} %param.4) | copy-start | bytes 1572868
  25.4 17.5 %all-to-all-start.1 = ((bf16[4,8,32,256]{3,2,1,0:T(8,128)(2,1)}), bf16[4,8,32,256]{3,2,1,0:T(8,128)(2,1)S(1)}, u32[]{:S(2)}, u32[]{:S(2)}) async-start(bf16[4,8,32,256]{3,2,1,0:T(8,128)(2,1)} %broadcast_in_dim.11), calls=%async_computation.1 | async-start | bytes 1048576 | tf_op jit(solution)/shard_map/all_to_all | solution.py:31
  29.7 13.2 %collective-permute-start = (bf16[32,256]{1,0:T(8,128)(2,1)S(1)}, bf16[32,256]{1,0:T(8,128)(2,1)S(1)}, u32[]{:S(2)}, u32[]{:S(2)}) collective-permute-start(bf16[32,256]{1,0:T(8,128)(2,1)S(1)} %copy-done.2), channel_id=1, source_target_pairs={{0,8},{8,0},{1,9},{9,1},{2,10},{10,2},{3,11},{11,3},{4,12},{12,4},... | collective-permute-start | bytes 49160 | tf_op jit(solution)/shard_map/ppermute | solution.py:54
  37.7 0.7 copy-start.3
  37.7 0.7 copy-start.4
  75.2 17.3 %all-to-all-start.4 = ((bf16[8,32,256]{2,1,0:T(8,128)(2,1)}), bf16[8,32,256]{2,1,0:T(8,128)(2,1)S(1)}, u32[]{:S(2)}, u32[]{:S(2)}) async-start(bf16[8,32,256]{2,1,0:T(8,128)(2,1)} %reduce_sum.12), calls=%async_computation.4 | async-start | bytes 262144 | tf_op jit(solution)/shard_map/all_to_all | solution.py:31
  79.3 13.2 %collective-permute-start.1 = (bf16[32,256]{1,0:T(8,128)(2,1)S(1)}, bf16[32,256]{1,0:T(8,128)(2,1)S(1)}, u32[]{:S(2)}, u32[]{:S(2)}) collective-permute-start(bf16[32,256]{1,0:T(8,128)(2,1)S(1)} %get-tuple-element.25), channel_id=1, source_target_pairs={{0,8},{8,0},{1,9},{9,1},{2,10},{10,2},{3,11},{11,3},{4,12},{12,4},... | collective-permute-start | bytes 49160 | tf_op jit(solution)/shard_map/ppermute | solution.py:54
  113.4 16.7 %all-to-all-start.6 = ((bf16[4,8,40,256]{3,2,1,0:T(8,128)(2,1)}), bf16[4,8,40,256]{3,2,1,0:T(8,128)(2,1)S(1)}, u32[]{:S(2)}, u32[]{:S(2)}) async-start(bf16[4,8,40,256]{3,2,1,0:T(8,128)(2,1)} %broadcast_in_dim.12), calls=%async_computation.6 | async-start | bytes 1310720 | tf_op jit(solution)/shard_map/all_to_all | solution.py:31
  116.9 13.3 %collective-permute-start.2 = (bf16[32,256]{1,0:T(8,128)(2,1)S(1)}, bf16[32,256]{1,0:T(8,128)(2,1)S(1)}, u32[]{:S(2)}, u32[]{:S(2)}) collective-permute-start(bf16[32,256]{1,0:T(8,128)(2,1)S(1)} %get-tuple-element.28.own_ref), channel_id=1, source_target_pairs={{0,8},{8,0},{1,9},{9,1},{2,10},{10,2},{3,11},{11,3},{4,12},{12,4},... | collective-permute-start | bytes 49160 | tf_op jit(solution)/shard_map/ppermute | solution.py:54
  152.1 17.8 %all-to-all-start.8 = ((bf16[4,8,32,256]{3,2,1,0:T(8,128)(2,1)}), bf16[4,8,32,256]{3,2,1,0:T(8,128)(2,1)S(1)}, u32[]{:S(2)}, u32[]{:S(2)}) async-start(bf16[4,8,32,256]{3,2,1,0:T(8,128)(2,1)} %get-tuple-element.31), calls=%async_computation.8 | async-start | bytes 1048576 | tf_op jit(solution)/shard_map/all_to_all | solution.py:31
  156.5 13.4 %collective-permute-start.3 = (bf16[48,256]{1,0:T(8,128)(2,1)S(1)}, bf16[48,256]{1,0:T(8,128)(2,1)S(1)}, u32[]{:S(2)}, u32[]{:S(2)}) collective-permute-start(bf16[48,256]{1,0:T(8,128)(2,1)S(1)} %get-tuple-element.32.sent_ref), channel_id=1, source_target_pairs={{0,8},{8,0},{1,9},{9,1},{2,10},{10,2},{3,11},{11,3},{4,12},{12,4},... | collective-permute-start | bytes 73736 | tf_op jit(solution)/shard_map/ppermute | solution.py:54
  170.7 14.0 %all-to-all-start.9 = ((bf16[8,40,256]{2,1,0:T(8,128)(2,1)}), bf16[8,40,256]{2,1,0:T(8,128)(2,1)S(1)}, u32[]{:S(2)}, u32[]{:S(2)}) async-start(bf16[8,40,256]{2,1,0:T(8,128)(2,1)} %get-tuple-element.36), calls=%async_computation.9 | async-start | bytes 327680 | tf_op jit(solution)/shard_map/all_to_all | solution.py:31
  181.3 20.6 %copy-start.1 = (f32[32,256]{1,0:T(8,128)}, f32[32,256]{1,0:T(8,128)S(1)}, u32[]{:S(2)}) copy-start(f32[32,256]{1,0:T(8,128)S(1)} %fusion.4.ritz_ref) | copy-start | bytes 98308
  185.4 16.5 %all-to-all-start.10 = ((bf16[32,8,256]{2,1,0:T(8,128)(2,1)}), bf16[32,8,256]{2,1,0:T(8,128)(2,1)S(1)}, u32[]{:S(2)}, u32[]{:S(2)}) async-start(bf16[32,8,256]{2,1,0:T(8,128)(2,1)} %get-tuple-element.37), calls=%async_computation.10 | async-start | bytes 262144 | tf_op jit(solution)/shard_map/all_to_all | solution.py:31

commit v4 on v3

--- a/solution.py
+++ b/solution.py
@@ -45,11 +45,6 @@
     return run
 
 
-def spread(value, axis):
-    length = lax.axis_size(axis)
-    return exchange(jnp.broadcast_to(value[None], (length, *value.shape)), axis)
-
-
 def partner(value):
     return lax.ppermute(value, Z_HI, [(0, 1), (1, 0)])
 
@@ -90,16 +85,42 @@
 
 
 def span(slot, length, start=0):
+    if isinstance(slot, int):
+        return pl.ds(start + slot * length, length)
     return pl.ds(pl.multiple_of(start + slot * length, length), length)
 
 
-def direct_kernel(pair_ref, column_ref, tile_ref, own_ref, other_ref, out_ref, sums_ref):
+def spread_kernel(by_z_ref, note_ref, out_ref):
+    length = by_z_ref.shape[1]
+    for y in range(out_ref.shape[0]):
+        for z in range(by_z_ref.shape[0]):
+            out_ref[y, pl.ds(z * length, length)] = by_z_ref[z]
+        out_ref[y, pl.ds(by_z_ref.shape[0] * length, ROWS)] = note_ref[...]
+
+
+def select_kernel(peer_ref, by_z_ref, out_ref, *, vectors):
+    y_count = out_ref.shape[0]
+    tiles = peer_ref.shape[0] // y_count
+    total = jnp.zeros((ROWS, LANES), F32)
+    for z in range(by_z_ref.shape[0]):
+        total += from_bits(by_z_ref[z, pl.ds(vectors, ROWS)])
+    for y in range(y_count):
+        for t in range(tiles):
+            place = lax.div(peer_ref[y * tiles + t], y_count)
+            out_ref[y, pl.ds(t * vectors, vectors)] = by_z_ref[place, pl.ds(0, vectors)]
+        store_bits(out_ref, (y, pl.ds(tiles * vectors, ROWS)), total)
+
+
+def direct_kernel(
+    pair_ref, column_ref, tile_ref, own_ref, other_ref, out_ref, sums_ref, *, extra
+):
     tiles, vectors = (tile_ref.shape[0], own_ref.shape[0])
-    y_count, z_count, xc_count = (*column_ref.shape[:2], out_ref.shape[0])
+    y_count, xc_count = (column_ref.shape[0], out_ref.shape[0])
     side = pair_ref[2 * tiles]
     for t in range(tiles):
         j = pair_ref[tiles + t]
-        from_column = column_ref[lax.rem(j, y_count), lax.div(j, y_count), pl.ds(0, vectors)]
+        slot = t if extra else lax.div(j, y_count)
+        from_column = column_ref[lax.rem(j, y_count), span(slot, vectors)]
         sums_ref[t] = lax.dot_general(
             from_column, tile_ref[t], (((1,), (1,)), ((), ())), preferred_element_type=F32
         )
@@ -108,11 +129,10 @@
         out_ref[k, pl.ds(0, vectors)] = own_ref[...]
         out_ref[k, pl.ds(vectors, vectors)] = other_ref[...]
         out_ref[k, pl.ds(2 * vectors, 2 * vectors)] = blank
-    if out_ref.shape[1] > 4 * vectors:
+    if extra:
         total = jnp.zeros((ROWS, LANES), F32)
         for y in range(y_count):
-            for z in range(z_count):
-                total += from_bits(column_ref[y, z, pl.ds(vectors, ROWS)])
+            total += from_bits(column_ref[y, pl.ds(tiles * vectors, ROWS)])
         for k in range(xc_count):
             store_bits(out_ref, (k, pl.ds(4 * vectors, ROWS)), total)
     slots = []
@@ -214,18 +234,31 @@
     residual_ref[...] = last_ref[...] - dot(projected, ritz_ref[...], 0, 0)
 
 
-def product(pairs, tiles, current, send_z):
+def product(pairs, tiles, current, send_z, cols):
     vectors, size = current.shape
     count = tiles.shape[0]
     y_count, z_count, xc_count = (lax.axis_size(Y), lax.axis_size(Z_LO), lax.axis_size(X_CORE))
     extra = send_z is not None
     if not extra:
-        send_z = jnp.broadcast_to(current[None], (z_count, *current.shape))
+        send_z = placed(jnp.broadcast_to(current[None], (z_count, *current.shape)))
     by_z = exchange(send_z, Z_LO)
     other = partner(current)
-    column_block = spread(by_z, Y)
+    if extra:
+        send = call(
+            functools.partial(select_kernel, vectors=vectors),
+            ((y_count, count * vectors + ROWS, size), BF16),
+            scalars=1,
+        )(cols, by_z)[0]
+    else:
+        note = jnp.pad(cols.astype(BF16)[None], [(0, ROWS - 1), (0, size - count)])
+        send = call(
+            spread_kernel, ((y_count, z_count * vectors + ROWS, size), BF16)
+        )(by_z, note)[0]
+    column_block = exchange(send, Y)
+    if not extra:
+        cols = column_block[:, z_count * vectors, :count].astype(jnp.int32).reshape(-1)
     send, direct = call(
-        direct_kernel,
+        functools.partial(direct_kernel, extra=extra),
         ((xc_count, 4 * vectors + ROWS * extra, size), BF16),
         ((count, vectors, size), F32),
         scalars=1,
@@ -250,7 +283,7 @@
     else:
         mirror, gram = (mirror.astype(F32).sum(axis=0).astype(BF16), None)
     mirror = exchange(mirror, Z_LO)
-    return own_direct, far, mirror, gram
+    return own_direct, far, mirror, gram, cols
 
 
 def steps(tile_values, tile_row, tile_col, basis_init):
@@ -260,14 +293,14 @@
     vectors, size = basis_init.shape
     total_rows = size * lax.axis_size(COL_ROW)
 
-    own_direct, far, mirror, _ = product(pairs, tiles, basis_init, None)
+    own_direct, far, mirror, _, cols = product(pairs, tiles, basis_init, None, tile_col[0, 0])
     image, current, send = call(
         image_kernel,
         ((vectors, size), F32),
         ((vectors, size), BF16),
         ((mirror.shape[0], vectors + ROWS, size), BF16),
     )(own_direct, far, mirror)
-    own_direct, far, mirror, gram = product(pairs, tiles, current, send)
+    own_direct, far, mirror, gram, _ = product(pairs, tiles, current, send, cols)
     raw_image, send = call(
         last_kernel,
         ((vectors, size), F32),

time: 204 us -> 207 us (1.015)
  blocking collectives: 91.9 us -> 48.9 us
  starting transfers between devices: 60.1 us -> 82.6 us
  waiting for transfers between devices: 31.1 us -> 51.4 us
  Pallas kernels: 7.51 us -> 10.5 us
    all_to_all x5 -> x3, blocking collectives: 91.9 us -> 48.9 us  [exchange(): return lax.all_to_all(parts, axis, 0, 0, tiled=True)]
    all_to_all x6 -> x8, starting transfers between devices: 28.6 us -> 51.1 us  [exchange(): return lax.all_to_all(parts, axis, 0, 0, tiled=True)]
    all_to_all x6 -> x8, waiting for transfers between devices: 10.9 us -> 31.2 us  [exchange(): return lax.all_to_all(parts, axis, 0, 0, tiled=True)]
    pallas_call x8 -> x10, Pallas kernels: 7.51 us -> 10.5 us  [run(): pl.pallas_call(kernel, out_shape=tuple((out(shape, kind) for shape, kind...]
  transfers between devices with their start and end apart: 10 -> 12, of which waited for: 6 -> 8; matrix products, arithmetic and copies ran while one was open for 4% -> 4% of each run, Pallas kernels for 0% -> 0%
where the time goes in v4:
time: 207 us; the launch traced here: 206 us
  starting transfers between devices  82.6 us (40%)
  waiting for transfers between devices  51.4 us (25%)
  blocking collectives  48.9 us (24%)
  Pallas kernels  10.5 us (5%)
  other arithmetic  8.04 us (4%)
  local copies, waits for them, and re-layouts  2.78 us (1%)
    all_to_all x8, starting transfers between devices, exchange(): return lax.all_to_all(parts, axis, 0, 0, tiled=True)  51.1 us
    all_to_all x3, blocking collectives, exchange(): return lax.all_to_all(parts, axis, 0, 0, tiled=True)  48.9 us
    ppermute x4, starting transfers between devices, partner(): return lax.ppermute(value, Z_HI, [(0, 1), (1, 0)])  31.5 us
    all_to_all x8, waiting for transfers between devices, exchange(): return lax.all_to_all(parts, axis, 0, 0, tiled=True)  31.2 us
    ppermute x4, waiting for transfers between devices, partner(): return lax.ppermute(value, Z_HI, [(0, 1), (1, 0)])  20.2 us
    pallas_call x10, Pallas kernels, run(): pl.pallas_call(kernel, out_shape=tuple((out(shape, kind) for shape, kind...  10.5 us
  transfers between devices with their start and end apart: 12, of which 8 were waited for; matrix products, arithmetic and copies ran while one was open for 4% of the time, Pallas kernels for 0%

profile of v4, /device:TPU:1, one launch (start us, length us, event | category | flops | bytes accessed | tf_op | source)
XLA Modules:
  0.0 205.6 jit_solution(12691014767943747668)
XLA Ops:
  2.0 13.2 %all-to-all-start = ((bf16[8,32,256]{2,1,0:T(8,128)(2,1)}), bf16[8,32,256]{2,1,0:T(8,128)(2,1)S(1)}, u32[]{:S(2)}, u32[]{:S(2)}) async-start(bf16[8,32,256]{2,1,0:T(8,128)(2,1)} %broadcast_in_dim.6), calls=%async_computation | async-start | bytes 262144 | tf_op jit(solution)/shard_map/all_to_all | solution.py:31
  15.2 10.3 %all-to-all-done.by_z_ref = bf16[8,32,256]{2,1,0:T(8,128)(2,1)S(1)} async-done(((bf16[8,32,256]{2,1,0:T(8,128)(2,1)}), bf16[8,32,256]{2,1,0:T(8,128)(2,1)S(1)}, u32[]{:S(2)}, u32[]{:S(2)}) %all-to-all-start) | async-done | bytes 131104 | tf_op jit(solution)/shard_map/all_to_all | solution.py:31
  26.4 4.3 %all-to-all-start.1 = ((bf16[4,264,256]{2,1,0:T(8,128)(2,1)}), bf16[4,264,256]{2,1,0:T(8,128)(2,1)S(1)}, u32[]{:S(2)}, u32[]{:S(2)}) async-start(bf16[4,264,256]{2,1,0:T(8,128)(2,1)} %shard_map.67), calls=%async_computation.1 | async-start | bytes 1081344 | tf_op jit(solution)/shard_map/all_to_all | solution.py:31
  30.7 7.9 %collective-permute-start = (bf16[32,256]{1,0:T(8,128)(2,1)S(1)}, bf16[32,256]{1,0:T(8,128)(2,1)S(1)}, u32[]{:S(2)}, u32[]{:S(2)}) collective-permute-start(bf16[32,256]{1,0:T(8,128)(2,1)S(1)} %copy-done.2), channel_id=1, source_target_pairs={{0,8},{8,0},{1,9},{9,1},{2,10},{10,2},{3,11},{11,3},{4,12},{12,4},... | collective-permute-start | bytes 49160 | tf_op jit(solution)/shard_map/ppermute | solution.py:49
  39.9 4.0 %collective-permute-done.other_ref = bf16[32,256]{1,0:T(8,128)(2,1)S(1)} collective-permute-done((bf16[32,256]{1,0:T(8,128)(2,1)S(1)}, bf16[32,256]{1,0:T(8,128)(2,1)S(1)}, u32[]{:S(2)}, u32[]{:S(2)}) %collective-permute-start) | collective-permute-done | bytes 16416 | tf_op jit(solution)/shard_map/ppermute | solution.py:49
  44.8 17.7 %all_to_all.55.row_ref = bf16[8,128,256]{2,1,0:T(8,128)(2,1)S(1)} all-to-all(bf16[8,128,256]{2,1,0:T(8,128)(2,1)S(1)} %get-tuple-element.22), channel_id=1, replica_groups=mesh['row_0'=8,'row_1'=4,'col_0'=2,'col_1'=4,'col_2'=2] {'col_1','col_2'}, dimensions={0} | all-to-all | bytes 1048576 | tf_op jit(solution)/shard_map/all_to_all | solution.py:31
  63.4 12.0 %all_to_all.56 = bf16[4,8,32,256]{3,2,1,0:T(8,128)(2,1)S(1)} all-to-all(bf16[4,8,32,256]{3,2,1,0:T(8,128)(2,1)S(1)} %get-tuple-element.26), channel_id=1, replica_groups=mesh['row_0'=8,'row_1'=4,'col_0'=2,'col_1'=4,'col_2'=2] {'row_1'}, dimensions={0} | all-to-all | bytes 1048576 | tf_op jit(solution)/shard_map/all_to_all | solution.py:31
  76.2 4.1 %all-to-all-start.4 = ((bf16[8,32,256]{2,1,0:T(8,128)(2,1)}), bf16[8,32,256]{2,1,0:T(8,128)(2,1)S(1)}, u32[]{:S(2)}, u32[]{:S(2)}) async-start(bf16[8,32,256]{2,1,0:T(8,128)(2,1)} %reduce_sum.12), calls=%async_computation.4 | async-start | bytes 262144 | tf_op jit(solution)/shard_map/all_to_all | solution.py:31
  80.2 7.8 %collective-permute-start.1 = (bf16[32,256]{1,0:T(8,128)(2,1)S(1)}, bf16[32,256]{1,0:T(8,128)(2,1)S(1)}, u32[]{:S(2)}, u32[]{:S(2)}) collective-permute-start(bf16[32,256]{1,0:T(8,128)(2,1)S(1)} %get-tuple-element.25), channel_id=1, source_target_pairs={{0,8},{8,0},{1,9},{9,1},{2,10},{10,2},{3,11},{11,3},{4,12},{12,4},... | collective-permute-start | bytes 49160 | tf_op jit(solution)/shard_map/ppermute | solution.py:49
  88.1 5.3 %collective-permute-done.1.far_ref = bf16[32,256]{1,0:T(8,128)(2,1)S(1)} collective-permute-done((bf16[32,256]{1,0:T(8,128)(2,1)S(1)}, bf16[32,256]{1,0:T(8,128)(2,1)S(1)}, u32[]{:S(2)}, u32[]{:S(2)}) %collective-permute-start.1) | collective-permute-done | bytes 16416 | tf_op jit(solution)/shard_map/ppermute | solution.py:49
  94.4 9.3 %all-to-all-start.5 = ((bf16[8,40,256]{2,1,0:T(8,128)(2,1)}), bf16[8,40,256]{2,1,0:T(8,128)(2,1)S(1)}, u32[]{:S(2)}, u32[]{:S(2)}) async-start(bf16[8,40,256]{2,1,0:T(8,128)(2,1)} %get-tuple-element.27), calls=%async_computation.5 | async-start | bytes 327680 | tf_op jit(solution)/shard_map/all_to_all | solution.py:31
  104.3 10.0 %all-to-all-done.5.by_z_ref = bf16[8,40,256]{2,1,0:T(8,128)(2,1)S(1)} async-done(((bf16[8,40,256]{2,1,0:T(8,128)(2,1)}), bf16[8,40,256]{2,1,0:T(8,128)(2,1)S(1)}, u32[]{:S(2)}, u32[]{:S(2)}) %all-to-all-start.5) | async-done | bytes 163872 | tf_op jit(solution)/shard_map/all_to_all | solution.py:31
  115.7 3.4 %all-to-all-start.6 = ((bf16[4,136,256]{2,1,0:T(8,128)(2,1)}), bf16[4,136,256]{2,1,0:T(8,128)(2,1)S(1)}, u32[]{:S(2)}, u32[]{:S(2)}) async-start(bf16[4,136,256]{2,1,0:T(8,128)(2,1)} %shard_map.71), calls=%async_computation.6 | async-start | bytes 557056 | tf_op jit(solution)/shard_map/all_to_all | solution.py:31
  119.2 7.9 %collective-permute-start.2 = (bf16[32,256]{1,0:T(8,128)(2,1)S(1)}, bf16[32,256]{1,0:T(8,128)(2,1)S(1)}, u32[]{:S(2)}, u32[]{:S(2)}) collective-permute-start(bf16[32,256]{1,0:T(8,128)(2,1)S(1)} %get-tuple-element.28.own_ref), channel_id=1, source_target_pairs={{0,8},{8,0},{1,9},{9,1},{2,10},{10,2},{3,11},{11,3},{4,12},{12,4},... | collective-permute-start | bytes 49160 | tf_op jit(solution)/shard_map/ppermute | solution.py:49
  127.1 5.4 %collective-permute-done.2.other_ref = bf16[32,256]{1,0:T(8,128)(2,1)S(1)} collective-permute-done((bf16[32,256]{1,0:T(8,128)(2,1)S(1)}, bf16[32,256]{1,0:T(8,128)(2,1)S(1)}, u32[]{:S(2)}, u32[]{:S(2)}) %collective-permute-start.2) | collective-permute-done | bytes 16416 | tf_op jit(solution)/shard_map/ppermute | solution.py:49
  133.4 19.2 %all_to_all.57.row_ref = bf16[8,136,256]{2,1,0:T(8,128)(2,1)S(1)} all-to-all(bf16[8,136,256]{2,1,0:T(8,128)(2,1)S(1)} %get-tuple-element.29), channel_id=1, replica_groups=mesh['row_0'=8,'row_1'=4,'col_0'=2,'col_1'=4,'col_2'=2] {'col_1','col_2'}, dimensions={0} | all-to-all | bytes 1114112 | tf_op jit(solution)/shard_map/all_to_all | solution.py:31
  154.4 4.5 %all-to-all-start.8 = ((bf16[4,8,32,256]{3,2,1,0:T(8,128)(2,1)}), bf16[4,8,32,256]{3,2,1,0:T(8,128)(2,1)S(1)}, u32[]{:S(2)}, u32[]{:S(2)}) async-start(bf16[4,8,32,256]{3,2,1,0:T(8,128)(2,1)} %get-tuple-element.31), calls=%async_computation.8 | async-start | bytes 1048576 | tf_op jit(solution)/shard_map/all_to_all | solution.py:31
  158.9 7.8 %collective-permute-start.3 = (bf16[48,256]{1,0:T(8,128)(2,1)S(1)}, bf16[48,256]{1,0:T(8,128)(2,1)S(1)}, u32[]{:S(2)}, u32[]{:S(2)}) collective-permute-start(bf16[48,256]{1,0:T(8,128)(2,1)S(1)} %get-tuple-element.32.sent_ref), channel_id=1, source_target_pairs={{0,8},{8,0},{1,9},{9,1},{2,10},{10,2},{3,11},{11,3},{4,12},{12,4},... | collective-permute-start | bytes 73736 | tf_op jit(solution)/shard_map/ppermute | solution.py:49
  166.7 5.5 %collective-permute-done.3.far_ref = bf16[48,256]{1,0:T(8,128)(2,1)S(1)} collective-permute-done((bf16[48,256]{1,0:T(8,128)(2,1)S(1)}, bf16[48,256]{1,0:T(8,128)(2,1)S(1)}, u32[]{:S(2)}, u32[]{:S(2)}) %collective-permute-start.3) | collective-permute-done | bytes 24608 | tf_op jit(solution)/shard_map/ppermute | solution.py:49
  173.1 3.4 %all-to-all-start.9 = ((bf16[8,40,256]{2,1,0:T(8,128)(2,1)}), bf16[8,40,256]{2,1,0:T(8,128)(2,1)S(1)}, u32[]{:S(2)}, u32[]{:S(2)}) async-start(bf16[8,40,256]{2,1,0:T(8,128)(2,1)} %get-tuple-element.36), calls=%async_computation.9 | async-start | bytes 327680 | tf_op jit(solution)/shard_map/all_to_all | solution.py:31
  176.5 2.9 %cholesky.17 = f32[32,32]{1,0:T(8,128)S(1)} custom-call(f32[32,32]{1,0:T(8,128)S(1)} %fusion.3), custom_call_target="Cholesky" | custom-call | tf_op jit(solution)/shard_map/jit(cholesky)/cholesky | solution.py:310
  183.6 3.4 %all-to-all-done.9.mirror_ref = bf16[8,40,256]{2,1,0:T(8,128)(2,1)S(1)} async-done(((bf16[8,40,256]{2,1,0:T(8,128)(2,1)}), bf16[8,40,256]{2,1,0:T(8,128)(2,1)S(1)}, u32[]{:S(2)}, u32[]{:S(2)}) %all-to-all-start.9) | async-done | bytes 163872 | tf_op jit(solution)/shard_map/all_to_all | solution.py:31
  187.8 8.9 %all-to-all-start.10 = ((bf16[32,8,256]{2,1,0:T(8,128)(2,1)}), bf16[32,8,256]{2,1,0:T(8,128)(2,1)S(1)}, u32[]{:S(2)}, u32[]{:S(2)}) async-start(bf16[32,8,256]{2,1,0:T(8,128)(2,1)} %get-tuple-element.37), calls=%async_computation.10 | async-start | bytes 262144 | tf_op jit(solution)/shard_map/all_to_all | solution.py:31
  196.8 7.4 %all-to-all-done.10.bits_ref = bf16[32,8,256]{2,1,0:T(8,128)(2,1)S(1)} async-done(((bf16[32,8,256]{2,1,0:T(8,128)(2,1)}), bf16[32,8,256]{2,1,0:T(8,128)(2,1)S(1)}, u32[]{:S(2)}, u32[]{:S(2)}) %all-to-all-start.10) | async-done | bytes 131104 | tf_op jit(solution)/shard_map/all_to_all | solution.py:31
  (42 shorter events, 18.9 us)
Async XLA Ops:
  2.0 13.2 %copy-start.3 = (s32[1,1,4]{2,1,0:T(1,128)S(1)}, s32[1,1,4]{2,1,0:T(1,128)}, u32[]{:S(2)}) copy-start(s32[1,1,4]{2,1,0:T(1,128)} %param.6) | copy-start | bytes 52
  2.0 23.5 %all-to-all-start = ((bf16[8,32,256]{2,1,0:T(8,128)(2,1)}), bf16[8,32,256]{2,1,0:T(8,128)(2,1)S(1)}, u32[]{:S(2)}, u32[]{:S(2)}) async-start(bf16[8,32,256]{2,1,0:T(8,128)(2,1)} %broadcast_in_dim.6), calls=%async_computation | async-start | bytes 262144 | tf_op jit(solution)/shard_map/all_to_all | solution.py:31
  26.4 4.3 %copy-start.2 = (bf16[32,256]{1,0:T(8,128)(2,1)S(1)}, bf16[32,256]{1,0:T(8,128)(2,1)}, u32[]{:S(2)}) copy-start(bf16[32,256]{1,0:T(8,128)(2,1)} %own_ref.1) | copy-start | bytes 49156
  26.4 17.5 %copy-start = (bf16[1,1,4,256,256]{4,3,2,1,0:T(8,128)(2,1)S(1)}, bf16[1,1,4,256,256]{4,3,2,1,0:T(8,128)(2,1)}, u32[]{:S(2)}) copy-start(bf16[1,1,4,256,256]{4,3,2,1,0:T(8,128)(2,1)} %param.4) | copy-start | bytes 1572868
  26.4 17.5 %all-to-all-start.1 = ((bf16[4,264,256]{2,1,0:T(8,128)(2,1)}), bf16[4,264,256]{2,1,0:T(8,128)(2,1)S(1)}, u32[]{:S(2)}, u32[]{:S(2)}) async-start(bf16[4,264,256]{2,1,0:T(8,128)(2,1)} %shard_map.67), calls=%async_computation.1 | async-start | bytes 1081344 | tf_op jit(solution)/shard_map/all_to_all | solution.py:31
  30.7 13.2 %collective-permute-start = (bf16[32,256]{1,0:T(8,128)(2,1)S(1)}, bf16[32,256]{1,0:T(8,128)(2,1)S(1)}, u32[]{:S(2)}, u32[]{:S(2)}) collective-permute-start(bf16[32,256]{1,0:T(8,128)(2,1)S(1)} %copy-done.2), channel_id=1, source_target_pairs={{0,8},{8,0},{1,9},{9,1},{2,10},{10,2},{3,11},{11,3},{4,12},{12,4},... | collective-permute-start | bytes 49160 | tf_op jit(solution)/shard_map/ppermute | solution.py:49
  38.6 0.7 copy-start.4
  76.2 17.3 %all-to-all-start.4 = ((bf16[8,32,256]{2,1,0:T(8,128)(2,1)}), bf16[8,32,256]{2,1,0:T(8,128)(2,1)S(1)}, u32[]{:S(2)}, u32[]{:S(2)}) async-start(bf16[8,32,256]{2,1,0:T(8,128)(2,1)} %reduce_sum.12), calls=%async_computation.4 | async-start | bytes 262144 | tf_op jit(solution)/shard_map/all_to_all | solution.py:31
  80.2 13.2 %collective-permute-start.1 = (bf16[32,256]{1,0:T(8,128)(2,1)S(1)}, bf16[32,256]{1,0:T(8,128)(2,1)S(1)}, u32[]{:S(2)}, u32[]{:S(2)}) collective-permute-start(bf16[32,256]{1,0:T(8,128)(2,1)S(1)} %get-tuple-element.25), channel_id=1, source_target_pairs={{0,8},{8,0},{1,9},{9,1},{2,10},{10,2},{3,11},{11,3},{4,12},{12,4},... | collective-permute-start | bytes 49160 | tf_op jit(solution)/shard_map/ppermute | solution.py:49
  94.4 20.0 %all-to-all-start.5 = ((bf16[8,40,256]{2,1,0:T(8,128)(2,1)}), bf16[8,40,256]{2,1,0:T(8,128)(2,1)S(1)}, u32[]{:S(2)}, u32[]{:S(2)}) async-start(bf16[8,40,256]{2,1,0:T(8,128)(2,1)} %get-tuple-element.27), calls=%async_computation.5 | async-start | bytes 327680 | tf_op jit(solution)/shard_map/all_to_all | solution.py:31
  115.7 16.7 %all-to-all-start.6 = ((bf16[4,136,256]{2,1,0:T(8,128)(2,1)}), bf16[4,136,256]{2,1,0:T(8,128)(2,1)S(1)}, u32[]{:S(2)}, u32[]{:S(2)}) async-start(bf16[4,136,256]{2,1,0:T(8,128)(2,1)} %shard_map.71), calls=%async_computation.6 | async-start | bytes 557056 | tf_op jit(solution)/shard_map/all_to_all | solution.py:31
  119.2 13.3 %collective-permute-start.2 = (bf16[32,256]{1,0:T(8,128)(2,1)S(1)}, bf16[32,256]{1,0:T(8,128)(2,1)S(1)}, u32[]{:S(2)}, u32[]{:S(2)}) collective-permute-start(bf16[32,256]{1,0:T(8,128)(2,1)S(1)} %get-tuple-element.28.own_ref), channel_id=1, source_target_pairs={{0,8},{8,0},{1,9},{9,1},{2,10},{10,2},{3,11},{11,3},{4,12},{12,4},... | collective-permute-start | bytes 49160 | tf_op jit(solution)/shard_map/ppermute | solution.py:49
  154.4 17.8 %all-to-all-start.8 = ((bf16[4,8,32,256]{3,2,1,0:T(8,128)(2,1)}), bf16[4,8,32,256]{3,2,1,0:T(8,128)(2,1)S(1)}, u32[]{:S(2)}, u32[]{:S(2)}) async-start(bf16[4,8,32,256]{3,2,1,0:T(8,128)(2,1)} %get-tuple-element.31), calls=%async_computation.8 | async-start | bytes 1048576 | tf_op jit(solution)/shard_map/all_to_all | solution.py:31
  158.9 13.4 %collective-permute-start.3 = (bf16[48,256]{1,0:T(8,128)(2,1)S(1)}, bf16[48,256]{1,0:T(8,128)(2,1)S(1)}, u32[]{:S(2)}, u32[]{:S(2)}) collective-permute-start(bf16[48,256]{1,0:T(8,128)(2,1)S(1)} %get-tuple-element.32.sent_ref), channel_id=1, source_target_pairs={{0,8},{8,0},{1,9},{9,1},{2,10},{10,2},{3,11},{11,3},{4,12},{12,4},... | collective-permute-start | bytes 73736 | tf_op jit(solution)/shard_map/ppermute | solution.py:49
  173.1 14.0 %all-to-all-start.9 = ((bf16[8,40,256]{2,1,0:T(8,128)(2,1)}), bf16[8,40,256]{2,1,0:T(8,128)(2,1)S(1)}, u32[]{:S(2)}, u32[]{:S(2)}) async-start(bf16[8,40,256]{2,1,0:T(8,128)(2,1)} %get-tuple-element.36), calls=%async_computation.9 | async-start | bytes 327680 | tf_op jit(solution)/shard_map/all_to_all | solution.py:31
  183.6 20.6 %copy-start.1 = (f32[32,256]{1,0:T(8,128)}, f32[32,256]{1,0:T(8,128)S(1)}, u32[]{:S(2)}) copy-start(f32[32,256]{1,0:T(8,128)S(1)} %fusion.5.ritz_ref) | copy-start | bytes 98308
  187.8 16.5 %all-to-all-start.10 = ((bf16[32,8,256]{2,1,0:T(8,128)(2,1)}), bf16[32,8,256]{2,1,0:T(8,128)(2,1)S(1)}, u32[]{:S(2)}, u32[]{:S(2)}) async-start(bf16[32,8,256]{2,1,0:T(8,128)(2,1)} %get-tuple-element.37), calls=%async_computation.10 | async-start | bytes 262144 | tf_op jit(solution)/shard_map/all_to_all | solution.py:31

commit v5 on v4

--- a/solution.py
+++ b/solution.py
@@ -10,7 +10,6 @@
 
 Z_HI, X_CORE = ("col_0", ("col_1", "col_2"))
 Z_LO, Y = ("row_0", "row_1")
-Y_X_CORE = ("row_1", "col_1", "col_2")
 COL = ("col_0", "col_1", "col_2")
 ROW = ("row_0", "row_1")
 COL_ROW = ("col_0", "col_1", "col_2", "row_0", "row_1")
@@ -84,6 +83,11 @@
         out_ref[place] = total.astype(BF16)
 
 
+def parted(index, count):
+    assert count & (count - 1) == 0
+    return lax.shift_right_logical(index, count.bit_length() - 1), lax.bitwise_and(index, count - 1)
+
+
 def span(slot, length, start=0):
     if isinstance(slot, int):
         return pl.ds(start + slot * length, length)
@@ -106,7 +110,7 @@
         total += from_bits(by_z_ref[z, pl.ds(vectors, ROWS)])
     for y in range(y_count):
         for t in range(tiles):
-            place = lax.div(peer_ref[y * tiles + t], y_count)
+            place, _ = parted(peer_ref[y * tiles + t], y_count)
             out_ref[y, pl.ds(t * vectors, vectors)] = by_z_ref[place, pl.ds(0, vectors)]
         store_bits(out_ref, (y, pl.ds(tiles * vectors, ROWS)), total)
 
@@ -119,8 +123,8 @@
     side = pair_ref[2 * tiles]
     for t in range(tiles):
         j = pair_ref[tiles + t]
-        slot = t if extra else lax.div(j, y_count)
-        from_column = column_ref[lax.rem(j, y_count), span(slot, vectors)]
+        z, y = parted(j, y_count)
+        from_column = column_ref[y, span(t if extra else z, vectors)]
         sums_ref[t] = lax.dot_general(
             from_column, tile_ref[t], (((1,), (1,)), ((), ())), preferred_element_type=F32
         )
@@ -138,8 +142,9 @@
     slots = []
     for t in range(tiles):
         i = pair_ref[t]
-        half = lax.rem(lax.div(i, xc_count) + side, 2)
-        slots.append((i, (lax.rem(i, xc_count), span(half, vectors, 2 * vectors))))
+        half, xc = parted(i, xc_count)
+        half = lax.bitwise_xor(half, side)
+        slots.append((i, (xc, span(half, vectors, 2 * vectors))))
     store_sums(out_ref, slots, sums_ref)
 
 
@@ -153,8 +158,8 @@
     form = jnp.zeros((vectors, vectors), F32)
     for t in range(tiles):
         i = pair_ref[t]
-        half = lax.rem(lax.div(i, xc_count) + side, 2)
-        from_row = row_ref[lax.rem(i, xc_count), span(half, vectors)]
+        half, xc = parted(i, xc_count)
+        from_row = row_ref[xc, span(lax.bitwise_xor(half, side), vectors)]
         sums_ref[t] = jnp.dot(from_row, tile_ref[t], preferred_element_type=F32)
         if extra:
             form += dot(from_row.astype(F32), direct_ref[t], 1, 1)
@@ -172,13 +177,17 @@
         for k in range(xc_count):
             total += from_bits(row_ref[k, pl.ds(4 * vectors, ROWS)])
         store_bits(far_ref, (pl.ds(vectors, ROWS),), total)
-        store_bits(far_ref, (pl.ds(vectors + ROWS, ROWS),), pack(form))
+        packed = pack(form)
+    length = out_ref.shape[1] - ROWS * extra
     for k in range(y_count):
-        out_ref[k] = jnp.zeros(out_ref.shape[1:], BF16)
+        out_ref[k, pl.ds(0, length)] = jnp.zeros((length, out_ref.shape[2]), BF16)
+        if extra:
+            store_bits(out_ref, (k, pl.ds(length, ROWS)), packed)
     slots = []
     for t in range(tiles):
         j = pair_ref[tiles + t]
-        slots.append((j, (lax.rem(j, y_count), lax.div(j, y_count))))
+        z, y = parted(j, y_count)
+        slots.append((j, (y, span(z, vectors))))
     store_sums(out_ref, slots, sums_ref)
 
 
@@ -195,19 +204,26 @@
         store_bits(send_ref, (z, pl.ds(image.shape[0], ROWS)), gram)
 
 
-def middle_kernel(mirror_ref, sent_ref, far_ref, send_ref, gram_ref):
-    vectors = gram_ref.shape[0]
-    for z in range(send_ref.shape[0]):
-        total = mirror_ref[0, z].astype(F32)
+def middle_kernel(mirror_ref, send_ref, *, vectors):
+    z_count = send_ref.shape[0]
+    for z in range(z_count):
+        rows = pl.ds(z * vectors, vectors)
+        total = mirror_ref[0, rows].astype(F32)
         for y in range(1, mirror_ref.shape[0]):
-            total = total + mirror_ref[y, z].astype(F32)
+            total = total + mirror_ref[y, rows].astype(F32)
         send_ref[z, pl.ds(0, vectors)] = total.astype(BF16)
-    rows = pl.ds(vectors, ROWS)
-    gram_ref[...] = unpack(from_bits(sent_ref[rows]) + from_bits(far_ref[rows]))
-    rows = pl.ds(vectors + ROWS, ROWS)
-    form = from_bits(sent_ref[rows]) + from_bits(far_ref[rows])
-    for z in range(send_ref.shape[0]):
-        store_bits(send_ref, (z, pl.ds(vectors, ROWS)), form)
+    if send_ref.shape[1] > vectors:
+        form = jnp.zeros((ROWS, LANES), F32)
+        for y in range(mirror_ref.shape[0]):
+            form += from_bits(mirror_ref[y, pl.ds(z_count * vectors, ROWS)])
+        for z in range(z_count):
+            store_bits(send_ref, (z, pl.ds(vectors, ROWS)), form)
+
+
+def gram_kernel(sent_ref, far_ref, gram_ref, *, rows):
+    place = pl.ds(gram_ref.shape[0], ROWS)
+    both = from_bits(sent_ref[place]) + from_bits(far_ref[place])
+    gram_ref[...] = unpack(both) * (1.0 / rows)
 
 
 def last_kernel(direct_ref, far_ref, mirror_ref, image_ref, send_ref):
@@ -227,11 +243,11 @@
     form = jnp.zeros((ROWS, LANES), F32)
     for k in range(bits_ref.shape[0]):
         form += from_bits(bits_ref[k])
+    form = unpack(form)
     inverse = inverse_ref[...]
-    half = dot(inverse, unpack(form), 1, 0)
-    projected = (dot(half, inverse, 1, 1) + dot(inverse, half, 1, 1)) * (1.0 / rows)
-    projected_ref[...] = projected
-    residual_ref[...] = last_ref[...] - dot(projected, ritz_ref[...], 0, 0)
+    half = dot(inverse, (form + form.T) * (1.0 / rows), 1, 0)
+    projected_ref[...] = dot(half, inverse, 1, 1)
+    residual_ref[...] = last_ref[...] - dot(half, ritz_ref[...], 1, 0)
 
 
 def product(pairs, tiles, current, send_z, cols):
@@ -266,24 +282,20 @@
     arrived = exchange(send, X_CORE)
     send, own_direct, far = call(
         mirror_kernel,
-        ((y_count, z_count, vectors, size), BF16),
+        ((y_count, z_count * vectors + ROWS * extra, size), BF16),
         ((vectors, size), F32),
-        ((vectors + 2 * ROWS * extra, size), BF16),
+        ((vectors + ROWS * extra, size), BF16),
         scalars=1,
         scratch=[pltpu.VMEM((count, vectors, size), F32)],
     )(pairs, arrived, tiles, direct)
     mirror = exchange(send, Y)
     sent, far = (far, partner(far))
-    if extra:
-        mirror, gram = call(
-            middle_kernel,
-            ((z_count, vectors + ROWS, size), BF16),
-            ((vectors, vectors), F32),
-        )(mirror, sent, far)
-    else:
-        mirror, gram = (mirror.astype(F32).sum(axis=0).astype(BF16), None)
+    mirror = call(
+        functools.partial(middle_kernel, vectors=vectors),
+        ((z_count, vectors + ROWS * extra, size), BF16),
+    )(mirror)[0]
     mirror = exchange(mirror, Z_LO)
-    return own_direct, far, mirror, gram, cols
+    return own_direct, sent, far, mirror, cols
 
 
 def steps(tile_values, tile_row, tile_col, basis_init):
@@ -293,32 +305,36 @@
     vectors, size = basis_init.shape
     total_rows = size * lax.axis_size(COL_ROW)
 
-    own_direct, far, mirror, _, cols = product(pairs, tiles, basis_init, None, tile_col[0, 0])
+    own_direct, _, far, mirror, cols = product(pairs, tiles, basis_init, None, tile_col[0, 0])
     image, current, send = call(
         image_kernel,
         ((vectors, size), F32),
         ((vectors, size), BF16),
         ((mirror.shape[0], vectors + ROWS, size), BF16),
     )(own_direct, far, mirror)
-    own_direct, far, mirror, gram, _ = product(pairs, tiles, current, send, cols)
+    own_direct, sent, far, mirror, _ = product(pairs, tiles, current, send, cols)
     raw_image, send = call(
         last_kernel,
         ((vectors, size), F32),
-        ((lax.axis_size(Y_X_CORE), ROWS, 2 * LANES), BF16),
+        ((lax.axis_size(COL), ROWS, 2 * LANES), BF16),
     )(own_direct, far, mirror)
-    form = exchange(send, Y_X_CORE)
-    factor = jnp.linalg.cholesky(gram / total_rows)
+    form = exchange(send, COL)
+    gram = call(
+        functools.partial(gram_kernel, rows=total_rows), ((vectors, vectors), F32)
+    )(sent, far)[0]
+    factor = jnp.linalg.cholesky(gram)
     inverse = lax.linalg.triangular_solve(
         factor, jnp.eye(vectors, dtype=F32), left_side=True, lower=True
     )
     ritz_basis = jnp.dot(inverse, image, precision=HIGHEST)
     last_image = jnp.dot(inverse, raw_image, precision=HIGHEST)
+    turned = jnp.dot(inverse.T, ritz_basis, precision=HIGHEST)
     residual, projected = call(
         functools.partial(finish_kernel, rows=total_rows),
         ((vectors, size), F32),
         ((vectors, vectors), F32),
         out=jax.ShapeDtypeStruct,
-    )(form, inverse, ritz_basis, last_image)
+    )(form, inverse, turned, last_image)
     return (ritz_basis, residual, projected)
 
 

time: 207 us -> 217 us (1.048)
  waiting for transfers between devices: 51.4 us -> 60.8 us
    all_to_all x8, waiting for transfers between devices: 31.2 us -> 45.2 us  [exchange(): return lax.all_to_all(parts, axis, 0, 0, tiled=True)]
    ppermute x4, waiting for transfers between devices: 20.2 us -> 15.6 us  [partner(): return lax.ppermute(value, Z_HI, [(0, 1), (1, 0)])]
    pallas_call x10 -> x12, Pallas kernels: 10.5 us -> 11.1 us  [run(): pl.pallas_call(kernel, out_shape=tuple((out(shape, kind) for shape, kind...]
  transfers between devices with their start and end apart: 12 -> 12, of which waited for: 8 -> 9; matrix products, arithmetic and copies ran while one was open for 4% -> 4% of each run, Pallas kernels for 0% -> 0%
where the time goes in v5:
time: 217 us; the launch traced here: 216 us
  starting transfers between devices  83.8 us (39%)
  waiting for transfers between devices  60.8 us (28%)
  blocking collectives  48.9 us (23%)
  Pallas kernels  11.1 us (5%)
  other arithmetic  7.31 us (3%)
  local copies, waits for them, and re-layouts  2.72 us (1%)
    all_to_all x8, starting transfers between devices, exchange(): return lax.all_to_all(parts, axis, 0, 0, tiled=True)  52.4 us
    all_to_all x3, blocking collectives, exchange(): return lax.all_to_all(parts, axis, 0, 0, tiled=True)  48.9 us
    all_to_all x8, waiting for transfers between devices, exchange(): return lax.all_to_all(parts, axis, 0, 0, tiled=True)  45.2 us
    ppermute x4, starting transfers between devices, partner(): return lax.ppermute(value, Z_HI, [(0, 1), (1, 0)])  31.5 us
    ppermute x4, waiting for transfers between devices, partner(): return lax.ppermute(value, Z_HI, [(0, 1), (1, 0)])  15.6 us
    pallas_call x12, Pallas kernels, run(): pl.pallas_call(kernel, out_shape=tuple((out(shape, kind) for shape, kind...  11.1 us
  transfers between devices with their start and end apart: 12, of which 9 were waited for; matrix products, arithmetic and copies ran while one was open for 4% of the time, Pallas kernels for 0%

profile of v5, /device:TPU:1, one launch (start us, length us, event | category | flops | bytes accessed | tf_op | source)
XLA Modules:
  0.0 216.3 jit_solution(13229993590648132553)
XLA Ops:
  2.0 13.2 %all-to-all-start = ((bf16[8,32,256]{2,1,0:T(8,128)(2,1)}), bf16[8,32,256]{2,1,0:T(8,128)(2,1)S(1)}, u32[]{:S(2)}, u32[]{:S(2)}) async-start(bf16[8,32,256]{2,1,0:T(8,128)(2,1)} %broadcast_in_dim.6), calls=%async_computation | async-start | bytes 262144 | tf_op jit(solution)/shard_map/all_to_all | solution.py:30
  15.2 10.3 %all-to-all-done.by_z_ref = bf16[8,32,256]{2,1,0:T(8,128)(2,1)S(1)} async-done(((bf16[8,32,256]{2,1,0:T(8,128)(2,1)}), bf16[8,32,256]{2,1,0:T(8,128)(2,1)S(1)}, u32[]{:S(2)}, u32[]{:S(2)}) %all-to-all-start) | async-done | bytes 131104 | tf_op jit(solution)/shard_map/all_to_all | solution.py:30
  26.4 4.3 %all-to-all-start.1 = ((bf16[4,264,256]{2,1,0:T(8,128)(2,1)}), bf16[4,264,256]{2,1,0:T(8,128)(2,1)S(1)}, u32[]{:S(2)}, u32[]{:S(2)}) async-start(bf16[4,264,256]{2,1,0:T(8,128)(2,1)} %shard_map.67), calls=%async_computation.1 | async-start | bytes 1081344 | tf_op jit(solution)/shard_map/all_to_all | solution.py:30
  30.7 7.9 %collective-permute-start = (bf16[32,256]{1,0:T(8,128)(2,1)S(1)}, bf16[32,256]{1,0:T(8,128)(2,1)S(1)}, u32[]{:S(2)}, u32[]{:S(2)}) collective-permute-start(bf16[32,256]{1,0:T(8,128)(2,1)S(1)} %copy-done.1), channel_id=1, source_target_pairs={{0,8},{8,0},{1,9},{9,1},{2,10},{10,2},{3,11},{11,3},{4,12},{12,4},... | collective-permute-start | bytes 49160 | tf_op jit(solution)/shard_map/ppermute | solution.py:48
  39.9 4.0 %collective-permute-done.other_ref = bf16[32,256]{1,0:T(8,128)(2,1)S(1)} collective-permute-done((bf16[32,256]{1,0:T(8,128)(2,1)S(1)}, bf16[32,256]{1,0:T(8,128)(2,1)S(1)}, u32[]{:S(2)}, u32[]{:S(2)}) %collective-permute-start) | collective-permute-done | bytes 16416 | tf_op jit(solution)/shard_map/ppermute | solution.py:48
  44.9 17.7 %all_to_all.55.row_ref = bf16[8,128,256]{2,1,0:T(8,128)(2,1)S(1)} all-to-all(bf16[8,128,256]{2,1,0:T(8,128)(2,1)S(1)} %get-tuple-element.20), channel_id=1, replica_groups=mesh['row_0'=8,'row_1'=4,'col_0'=2,'col_1'=4,'col_2'=2] {'col_1','col_2'}, dimensions={0} | all-to-all | bytes 1048576 | tf_op jit(solution)/shard_map/all_to_all | solution.py:30
  63.4 12.0 %all_to_all.56.mirror_ref = bf16[4,256,256]{2,1,0:T(8,128)(2,1)S(1)} all-to-all(bf16[4,256,256]{2,1,0:T(8,128)(2,1)S(1)} %get-tuple-element.24), channel_id=1, replica_groups=mesh['row_0'=8,'row_1'=4,'col_0'=2,'col_1'=4,'col_2'=2] {'row_1'}, dimensions={0} | all-to-all | bytes 1048576 | tf_op jit(solution)/shard_map/all_to_all | solution.py:30
  76.1 4.1 %all-to-all-start.4 = ((bf16[8,32,256]{2,1,0:T(8,128)(2,1)}), bf16[8,32,256]{2,1,0:T(8,128)(2,1)S(1)}, u32[]{:S(2)}, u32[]{:S(2)}) async-start(bf16[8,32,256]{2,1,0:T(8,128)(2,1)} %shard_map.70), calls=%async_computation.4 | async-start | bytes 262144 | tf_op jit(solution)/shard_map/all_to_all | solution.py:30
  80.2 7.8 %collective-permute-start.1 = (bf16[32,256]{1,0:T(8,128)(2,1)S(1)}, bf16[32,256]{1,0:T(8,128)(2,1)S(1)}, u32[]{:S(2)}, u32[]{:S(2)}) collective-permute-start(bf16[32,256]{1,0:T(8,128)(2,1)S(1)} %get-tuple-element.23), channel_id=1, source_target_pairs={{0,8},{8,0},{1,9},{9,1},{2,10},{10,2},{3,11},{11,3},{4,12},{12,4},... | collective-permute-start | bytes 49160 | tf_op jit(solution)/shard_map/ppermute | solution.py:48
  88.1 5.3 %collective-permute-done.1.far_ref = bf16[32,256]{1,0:T(8,128)(2,1)S(1)} collective-permute-done((bf16[32,256]{1,0:T(8,128)(2,1)S(1)}, bf16[32,256]{1,0:T(8,128)(2,1)S(1)}, u32[]{:S(2)}, u32[]{:S(2)}) %collective-permute-start.1) | collective-permute-done | bytes 16416 | tf_op jit(solution)/shard_map/ppermute | solution.py:48
  94.3 9.3 %all-to-all-start.5 = ((bf16[8,40,256]{2,1,0:T(8,128)(2,1)}), bf16[8,40,256]{2,1,0:T(8,128)(2,1)S(1)}, u32[]{:S(2)}, u32[]{:S(2)}) async-start(bf16[8,40,256]{2,1,0:T(8,128)(2,1)} %get-tuple-element.25), calls=%async_computation.5 | async-start | bytes 327680 | tf_op jit(solution)/shard_map/all_to_all | solution.py:30
  104.3 10.0 %all-to-all-done.5.by_z_ref = bf16[8,40,256]{2,1,0:T(8,128)(2,1)S(1)} async-done(((bf16[8,40,256]{2,1,0:T(8,128)(2,1)}), bf16[8,40,256]{2,1,0:T(8,128)(2,1)S(1)}, u32[]{:S(2)}, u32[]{:S(2)}) %all-to-all-start.5) | async-done | bytes 163872 | tf_op jit(solution)/shard_map/all_to_all | solution.py:30
  115.7 3.4 %all-to-all-start.6 = ((bf16[4,136,256]{2,1,0:T(8,128)(2,1)}), bf16[4,136,256]{2,1,0:T(8,128)(2,1)S(1)}, u32[]{:S(2)}, u32[]{:S(2)}) async-start(bf16[4,136,256]{2,1,0:T(8,128)(2,1)} %shard_map.72), calls=%async_computation.6 | async-start | bytes 557056 | tf_op jit(solution)/shard_map/all_to_all | solution.py:30
  119.2 7.9 %collective-permute-start.2 = (bf16[32,256]{1,0:T(8,128)(2,1)S(1)}, bf16[32,256]{1,0:T(8,128)(2,1)S(1)}, u32[]{:S(2)}, u32[]{:S(2)}) collective-permute-start(bf16[32,256]{1,0:T(8,128)(2,1)S(1)} %get-tuple-element.26.own_ref), channel_id=1, source_target_pairs={{0,8},{8,0},{1,9},{9,1},{2,10},{10,2},{3,11},{11,3},{4,12},{12,4},... | collective-permute-start | bytes 49160 | tf_op jit(solution)/shard_map/ppermute | solution.py:48
  127.1 5.4 %collective-permute-done.2.other_ref = bf16[32,256]{1,0:T(8,128)(2,1)S(1)} collective-permute-done((bf16[32,256]{1,0:T(8,128)(2,1)S(1)}, bf16[32,256]{1,0:T(8,128)(2,1)S(1)}, u32[]{:S(2)}, u32[]{:S(2)}) %collective-permute-start.2) | collective-permute-done | bytes 16416 | tf_op jit(solution)/shard_map/ppermute | solution.py:48
  133.4 19.2 %all_to_all.57.row_ref = bf16[8,136,256]{2,1,0:T(8,128)(2,1)S(1)} all-to-all(bf16[8,136,256]{2,1,0:T(8,128)(2,1)S(1)} %get-tuple-element.27), channel_id=1, replica_groups=mesh['row_0'=8,'row_1'=4,'col_0'=2,'col_1'=4,'col_2'=2] {'col_1','col_2'}, dimensions={0} | all-to-all | bytes 1114112 | tf_op jit(solution)/shard_map/all_to_all | solution.py:30
  154.5 7.8 %collective-permute-start.3 = (bf16[40,256]{1,0:T(8,128)(2,1)S(1)}, bf16[40,256]{1,0:T(8,128)(2,1)S(1)}, u32[]{:S(2)}, u32[]{:S(2)}) collective-permute-start(bf16[40,256]{1,0:T(8,128)(2,1)S(1)} %get-tuple-element.29.sent_ref), channel_id=1, source_target_pairs={{0,8},{8,0},{1,9},{9,1},{2,10},{10,2},{3,11},{11,3},{4,12},{12,4},... | collective-permute-start | bytes 61448 | tf_op jit(solution)/shard_map/ppermute | solution.py:48
  162.3 4.5 %all-to-all-start.8 = ((bf16[4,264,256]{2,1,0:T(8,128)(2,1)}), bf16[4,264,256]{2,1,0:T(8,128)(2,1)S(1)}, u32[]{:S(2)}, u32[]{:S(2)}) async-start(bf16[4,264,256]{2,1,0:T(8,128)(2,1)} %get-tuple-element.32), calls=%async_computation.8 | async-start | bytes 1081344 | tf_op jit(solution)/shard_map/all_to_all | solution.py:30
  167.9 2.9 %cholesky.17 = f32[32,32]{1,0:T(8,128)S(1)} custom-call(f32[32,32]{1,0:T(8,128)S(1)} %fusion.3), custom_call_target="Cholesky" | custom-call | tf_op jit(solution)/shard_map/jit(cholesky)/cholesky | solution.py:325
  171.5 3.7 %all-to-all-done.8.mirror_ref = bf16[4,264,256]{2,1,0:T(8,128)(2,1)S(1)} async-done(((bf16[4,264,256]{2,1,0:T(8,128)(2,1)}), bf16[4,264,256]{2,1,0:T(8,128)(2,1)S(1)}, u32[]{:S(2)}, u32[]{:S(2)}) %all-to-all-start.8) | async-done | bytes 540704 | tf_op jit(solution)/shard_map/all_to_all | solution.py:30
  175.9 3.4 %all-to-all-start.9 = ((bf16[8,40,256]{2,1,0:T(8,128)(2,1)}), bf16[8,40,256]{2,1,0:T(8,128)(2,1)S(1)}, u32[]{:S(2)}, u32[]{:S(2)}) async-start(bf16[8,40,256]{2,1,0:T(8,128)(2,1)} %shard_map.76), calls=%async_computation.9 | async-start | bytes 327680 | tf_op jit(solution)/shard_map/all_to_all | solution.py:30
  182.8 7.1 %all-to-all-done.9.mirror_ref = bf16[8,40,256]{2,1,0:T(8,128)(2,1)S(1)} async-done(((bf16[8,40,256]{2,1,0:T(8,128)(2,1)}), bf16[8,40,256]{2,1,0:T(8,128)(2,1)S(1)}, u32[]{:S(2)}, u32[]{:S(2)}) %all-to-all-start.9) | async-done | bytes 163872 | tf_op jit(solution)/shard_map/all_to_all | solution.py:30
  190.5 10.1 %all-to-all-start.10 = ((bf16[16,8,256]{2,1,0:T(8,128)(2,1)}), bf16[16,8,256]{2,1,0:T(8,128)(2,1)S(1)}, u32[]{:S(2)}, u32[]{:S(2)}) async-start(bf16[16,8,256]{2,1,0:T(8,128)(2,1)} %get-tuple-element.33), calls=%async_computation.10 | async-start | bytes 131072 | tf_op jit(solution)/shard_map/all_to_all | solution.py:30
  201.0 14.1 %all-to-all-done.10.bits_ref = bf16[16,8,256]{2,1,0:T(8,128)(2,1)S(1)} async-done(((bf16[16,8,256]{2,1,0:T(8,128)(2,1)}), bf16[16,8,256]{2,1,0:T(8,128)(2,1)S(1)}, u32[]{:S(2)}, u32[]{:S(2)}) %all-to-all-start.10) | async-done | bytes 65568 | tf_op jit(solution)/shard_map/all_to_all | solution.py:30
  (42 shorter events, 19.8 us)
Async XLA Ops:
  2.0 13.2 %copy-start.3 = (s32[1,1,4]{2,1,0:T(1,128)S(1)}, s32[1,1,4]{2,1,0:T(1,128)}, u32[]{:S(2)}) copy-start(s32[1,1,4]{2,1,0:T(1,128)} %param.6) | copy-start | bytes 52
  2.0 23.5 %all-to-all-start = ((bf16[8,32,256]{2,1,0:T(8,128)(2,1)}), bf16[8,32,256]{2,1,0:T(8,128)(2,1)S(1)}, u32[]{:S(2)}, u32[]{:S(2)}) async-start(bf16[8,32,256]{2,1,0:T(8,128)(2,1)} %broadcast_in_dim.6), calls=%async_computation | async-start | bytes 262144 | tf_op jit(solution)/shard_map/all_to_all | solution.py:30
  26.4 4.3 %copy-start.1 = (bf16[32,256]{1,0:T(8,128)(2,1)S(1)}, bf16[32,256]{1,0:T(8,128)(2,1)}, u32[]{:S(2)}) copy-start(bf16[32,256]{1,0:T(8,128)(2,1)} %own_ref.1) | copy-start | bytes 49156
  26.4 17.5 %copy-start = (bf16[1,1,4,256,256]{4,3,2,1,0:T(8,128)(2,1)S(1)}, bf16[1,1,4,256,256]{4,3,2,1,0:T(8,128)(2,1)}, u32[]{:S(2)}) copy-start(bf16[1,1,4,256,256]{4,3,2,1,0:T(8,128)(2,1)} %param.4) | copy-start | bytes 1572868
  26.4 17.5 %all-to-all-start.1 = ((bf16[4,264,256]{2,1,0:T(8,128)(2,1)}), bf16[4,264,256]{2,1,0:T(8,128)(2,1)S(1)}, u32[]{:S(2)}, u32[]{:S(2)}) async-start(bf16[4,264,256]{2,1,0:T(8,128)(2,1)} %shard_map.67), calls=%async_computation.1 | async-start | bytes 1081344 | tf_op jit(solution)/shard_map/all_to_all | solution.py:30
  30.7 13.2 %collective-permute-start = (bf16[32,256]{1,0:T(8,128)(2,1)S(1)}, bf16[32,256]{1,0:T(8,128)(2,1)S(1)}, u32[]{:S(2)}, u32[]{:S(2)}) collective-permute-start(bf16[32,256]{1,0:T(8,128)(2,1)S(1)} %copy-done.1), channel_id=1, source_target_pairs={{0,8},{8,0},{1,9},{9,1},{2,10},{10,2},{3,11},{11,3},{4,12},{12,4},... | collective-permute-start | bytes 49160 | tf_op jit(solution)/shard_map/ppermute | solution.py:48
  38.6 0.7 copy-start.4
  76.1 17.3 %all-to-all-start.4 = ((bf16[8,32,256]{2,1,0:T(8,128)(2,1)}), bf16[8,32,256]{2,1,0:T(8,128)(2,1)S(1)}, u32[]{:S(2)}, u32[]{:S(2)}) async-start(bf16[8,32,256]{2,1,0:T(8,128)(2,1)} %shard_map.70), calls=%async_computation.4 | async-start | bytes 262144 | tf_op jit(solution)/shard_map/all_to_all | solution.py:30
  80.2 13.2 %collective-permute-start.1 = (bf16[32,256]{1,0:T(8,128)(2,1)S(1)}, bf16[32,256]{1,0:T(8,128)(2,1)S(1)}, u32[]{:S(2)}, u32[]{:S(2)}) collective-permute-start(bf16[32,256]{1,0:T(8,128)(2,1)S(1)} %get-tuple-element.23), channel_id=1, source_target_pairs={{0,8},{8,0},{1,9},{9,1},{2,10},{10,2},{3,11},{11,3},{4,12},{12,4},... | collective-permute-start | bytes 49160 | tf_op jit(solution)/shard_map/ppermute | solution.py:48
  94.3 20.0 %all-to-all-start.5 = ((bf16[8,40,256]{2,1,0:T(8,128)(2,1)}), bf16[8,40,256]{2,1,0:T(8,128)(2,1)S(1)}, u32[]{:S(2)}, u32[]{:S(2)}) async-start(bf16[8,40,256]{2,1,0:T(8,128)(2,1)} %get-tuple-element.25), calls=%async_computation.5 | async-start | bytes 327680 | tf_op jit(solution)/shard_map/all_to_all | solution.py:30
  115.7 16.7 %all-to-all-start.6 = ((bf16[4,136,256]{2,1,0:T(8,128)(2,1)}), bf16[4,136,256]{2,1,0:T(8,128)(2,1)S(1)}, u32[]{:S(2)}, u32[]{:S(2)}) async-start(bf16[4,136,256]{2,1,0:T(8,128)(2,1)} %shard_map.72), calls=%async_computation.6 | async-start | bytes 557056 | tf_op jit(solution)/shard_map/all_to_all | solution.py:30
  119.2 13.3 %collective-permute-start.2 = (bf16[32,256]{1,0:T(8,128)(2,1)S(1)}, bf16[32,256]{1,0:T(8,128)(2,1)S(1)}, u32[]{:S(2)}, u32[]{:S(2)}) collective-permute-start(bf16[32,256]{1,0:T(8,128)(2,1)S(1)} %get-tuple-element.26.own_ref), channel_id=1, source_target_pairs={{0,8},{8,0},{1,9},{9,1},{2,10},{10,2},{3,11},{11,3},{4,12},{12,4},... | collective-permute-start | bytes 49160 | tf_op jit(solution)/shard_map/ppermute | solution.py:48
  154.5 13.2 %collective-permute-start.3 = (bf16[40,256]{1,0:T(8,128)(2,1)S(1)}, bf16[40,256]{1,0:T(8,128)(2,1)S(1)}, u32[]{:S(2)}, u32[]{:S(2)}) collective-permute-start(bf16[40,256]{1,0:T(8,128)(2,1)S(1)} %get-tuple-element.29.sent_ref), channel_id=1, source_target_pairs={{0,8},{8,0},{1,9},{9,1},{2,10},{10,2},{3,11},{11,3},{4,12},{12,4},... | collective-permute-start | bytes 61448 | tf_op jit(solution)/shard_map/ppermute | solution.py:48
  162.3 12.8 %all-to-all-start.8 = ((bf16[4,264,256]{2,1,0:T(8,128)(2,1)}), bf16[4,264,256]{2,1,0:T(8,128)(2,1)S(1)}, u32[]{:S(2)}, u32[]{:S(2)}) async-start(bf16[4,264,256]{2,1,0:T(8,128)(2,1)} %get-tuple-element.32), calls=%async_computation.8 | async-start | bytes 1081344 | tf_op jit(solution)/shard_map/all_to_all | solution.py:30
  175.9 14.0 %all-to-all-start.9 = ((bf16[8,40,256]{2,1,0:T(8,128)(2,1)}), bf16[8,40,256]{2,1,0:T(8,128)(2,1)S(1)}, u32[]{:S(2)}, u32[]{:S(2)}) async-start(bf16[8,40,256]{2,1,0:T(8,128)(2,1)} %shard_map.76), calls=%async_computation.9 | async-start | bytes 327680 | tf_op jit(solution)/shard_map/all_to_all | solution.py:30
  182.7 17.9 %copy-start.2 = (f32[32,256]{1,0:T(8,128)}, f32[32,256]{1,0:T(8,128)S(1)}, u32[]{:S(2)}) copy-start(f32[32,256]{1,0:T(8,128)S(1)} %fusion.5) | copy-start | bytes 98308
  190.5 24.6 %all-to-all-start.10 = ((bf16[16,8,256]{2,1,0:T(8,128)(2,1)}), bf16[16,8,256]{2,1,0:T(8,128)(2,1)S(1)}, u32[]{:S(2)}, u32[]{:S(2)}) async-start(bf16[16,8,256]{2,1,0:T(8,128)(2,1)} %get-tuple-element.33), calls=%async_computation.10 | async-start | bytes 131072 | tf_op jit(solution)/shard_map/all_to_all | solution.py:30

commit v6 on v5

--- a/solution.py
+++ b/solution.py
@@ -10,6 +10,7 @@
 
 Z_HI, X_CORE = ("col_0", ("col_1", "col_2"))
 Z_LO, Y = ("row_0", "row_1")
+Y_X_CORE = ("row_1", "col_1", "col_2")
 COL = ("col_0", "col_1", "col_2")
 ROW = ("row_0", "row_1")
 COL_ROW = ("col_0", "col_1", "col_2", "row_0", "row_1")
@@ -92,14 +93,6 @@
     if isinstance(slot, int):
         return pl.ds(start + slot * length, length)
     return pl.ds(pl.multiple_of(start + slot * length, length), length)
-
-
-def spread_kernel(by_z_ref, note_ref, out_ref):
-    length = by_z_ref.shape[1]
-    for y in range(out_ref.shape[0]):
-        for z in range(by_z_ref.shape[0]):
-            out_ref[y, pl.ds(z * length, length)] = by_z_ref[z]
-        out_ref[y, pl.ds(by_z_ref.shape[0] * length, ROWS)] = note_ref[...]
 
 
 def select_kernel(peer_ref, by_z_ref, out_ref, *, vectors):
@@ -123,8 +116,10 @@
     side = pair_ref[2 * tiles]
     for t in range(tiles):
         j = pair_ref[tiles + t]
-        z, y = parted(j, y_count)
-        from_column = column_ref[y, span(t if extra else z, vectors)]
+        if extra:
+            from_column = column_ref[parted(j, y_count)[1], pl.ds(t * vectors, vectors)]
+        else:
+            from_column = column_ref[j]
         sums_ref[t] = lax.dot_general(
             from_column, tile_ref[t], (((1,), (1,)), ((), ())), preferred_element_type=F32
         )
@@ -149,40 +144,38 @@
 
 
 def mirror_kernel(
-    pair_ref, row_ref, tile_ref, direct_ref, out_ref, own_ref, far_ref, sums_ref
+    pair_ref, row_ref, tile_ref, near_ref, other_ref, out_ref, own_ref, far_ref, sums_ref
 ):
     tiles, vectors = (tile_ref.shape[0], own_ref.shape[0])
     y_count, xc_count = (out_ref.shape[0], row_ref.shape[0])
     extra = row_ref.shape[1] > 4 * vectors
     side = pair_ref[2 * tiles]
-    form = jnp.zeros((vectors, vectors), F32)
     for t in range(tiles):
-        i = pair_ref[t]
-        half, xc = parted(i, xc_count)
+        half, xc = parted(pair_ref[t], xc_count)
         from_row = row_ref[xc, span(lax.bitwise_xor(half, side), vectors)]
         sums_ref[t] = jnp.dot(from_row, tile_ref[t], preferred_element_type=F32)
-        if extra:
-            form += dot(from_row.astype(F32), direct_ref[t], 1, 1)
+    sums = []
     for s in range(2):
         rows = pl.ds((2 + s) * vectors, vectors)
         total = row_ref[0, rows].astype(F32)
         for k in range(1, xc_count):
             total = total + row_ref[k, rows].astype(F32)
-        if s == 0:
-            own_ref[...] = total
-        else:
-            far_ref[pl.ds(0, vectors)] = total.astype(BF16)
+        sums.append(total)
+    own_ref[...] = sums[0]
+    far_ref[pl.ds(0, vectors)] = sums[1].astype(BF16)
     if extra:
         total = jnp.zeros((ROWS, LANES), F32)
         for k in range(xc_count):
             total += from_bits(row_ref[k, pl.ds(4 * vectors, ROWS)])
         store_bits(far_ref, (pl.ds(vectors, ROWS),), total)
-        packed = pack(form)
-    length = out_ref.shape[1] - ROWS * extra
+        form = dot(near_ref[...].astype(F32), sums[0], 1, 1)
+        form += dot(other_ref[...].astype(F32), sums[1], 1, 1)
+        store_bits(far_ref, (pl.ds(vectors + ROWS, ROWS),), pack(form))
+    length = out_ref.shape[1] - ROWS * (not extra)
     for k in range(y_count):
         out_ref[k, pl.ds(0, length)] = jnp.zeros((length, out_ref.shape[2]), BF16)
-        if extra:
-            store_bits(out_ref, (k, pl.ds(length, ROWS)), packed)
+        if not extra:
+            out_ref[k, pl.ds(length, ROWS)] = other_ref[...]
     slots = []
     for t in range(tiles):
         j = pair_ref[tiles + t]
@@ -204,20 +197,25 @@
         store_bits(send_ref, (z, pl.ds(image.shape[0], ROWS)), gram)
 
 
-def middle_kernel(mirror_ref, send_ref, *, vectors):
-    z_count = send_ref.shape[0]
-    for z in range(z_count):
+def sum_over_y(mirror_ref, send_ref, vectors):
+    for z in range(send_ref.shape[0]):
         rows = pl.ds(z * vectors, vectors)
         total = mirror_ref[0, rows].astype(F32)
         for y in range(1, mirror_ref.shape[0]):
             total = total + mirror_ref[y, rows].astype(F32)
         send_ref[z, pl.ds(0, vectors)] = total.astype(BF16)
-    if send_ref.shape[1] > vectors:
-        form = jnp.zeros((ROWS, LANES), F32)
-        for y in range(mirror_ref.shape[0]):
-            form += from_bits(mirror_ref[y, pl.ds(z_count * vectors, ROWS)])
-        for z in range(z_count):
-            store_bits(send_ref, (z, pl.ds(vectors, ROWS)), form)
+
+
+def first_middle_kernel(mirror_ref, send_ref):
+    sum_over_y(mirror_ref, send_ref, send_ref.shape[1])
+
+
+def second_middle_kernel(mirror_ref, sent_ref, far_ref, send_ref, *, vectors):
+    sum_over_y(mirror_ref, send_ref, vectors)
+    rows = pl.ds(vectors + ROWS, ROWS)
+    form = from_bits(sent_ref[rows]) + from_bits(far_ref[rows])
+    for z in range(send_ref.shape[0]):
+        store_bits(send_ref, (z, pl.ds(vectors, ROWS)), form)
 
 
 def gram_kernel(sent_ref, far_ref, gram_ref, *, rows):
@@ -250,52 +248,51 @@
     residual_ref[...] = last_ref[...] - dot(half, ritz_ref[...], 1, 0)
 
 
-def product(pairs, tiles, current, send_z, cols):
+def product(pairs, tiles, current, send_z, note, peers):
     vectors, size = current.shape
     count = tiles.shape[0]
     y_count, z_count, xc_count = (lax.axis_size(Y), lax.axis_size(Z_LO), lax.axis_size(X_CORE))
     extra = send_z is not None
-    if not extra:
-        send_z = placed(jnp.broadcast_to(current[None], (z_count, *current.shape)))
-    by_z = exchange(send_z, Z_LO)
-    other = partner(current)
     if extra:
+        by_z = exchange(send_z, Z_LO)
+        other = partner(current)
         send = call(
             functools.partial(select_kernel, vectors=vectors),
             ((y_count, count * vectors + ROWS, size), BF16),
             scalars=1,
-        )(cols, by_z)[0]
+        )(peers, by_z)[0]
+        column_block = exchange(send, Y)
     else:
-        note = jnp.pad(cols.astype(BF16)[None], [(0, ROWS - 1), (0, size - count)])
-        send = call(
-            spread_kernel, ((y_count, z_count * vectors + ROWS, size), BF16)
-        )(by_z, note)[0]
-    column_block = exchange(send, Y)
-    if not extra:
-        cols = column_block[:, z_count * vectors, :count].astype(jnp.int32).reshape(-1)
-    send, direct = call(
+        other = partner(current)
+        row_count = lax.axis_size(ROW)
+        send = jnp.broadcast_to(current[None], (row_count, vectors, size))
+        column_block = exchange(send, ROW)
+    send = call(
         functools.partial(direct_kernel, extra=extra),
         ((xc_count, 4 * vectors + ROWS * extra, size), BF16),
-        ((count, vectors, size), F32),
         scalars=1,
-    )(pairs, column_block, tiles, current, other)
+        scratch=[pltpu.VMEM((count, vectors, size), F32)],
+    )(pairs, column_block, tiles, current, other)[0]
     arrived = exchange(send, X_CORE)
     send, own_direct, far = call(
         mirror_kernel,
-        ((y_count, z_count * vectors + ROWS * extra, size), BF16),
+        ((y_count, z_count * vectors + ROWS * (not extra), size), BF16),
         ((vectors, size), F32),
-        ((vectors + ROWS * extra, size), BF16),
+        ((vectors + 2 * ROWS * extra, size), BF16),
         scalars=1,
         scratch=[pltpu.VMEM((count, vectors, size), F32)],
-    )(pairs, arrived, tiles, direct)
+    )(pairs, arrived, tiles, current, other if extra else note)
     mirror = exchange(send, Y)
     sent, far = (far, partner(far))
-    mirror = call(
-        functools.partial(middle_kernel, vectors=vectors),
-        ((z_count, vectors + ROWS * extra, size), BF16),
-    )(mirror)[0]
+    out = ((z_count, vectors + ROWS * extra, size), BF16)
+    if extra:
+        middle = functools.partial(second_middle_kernel, vectors=vectors)
+        mirror = call(middle, out)(mirror, sent, far)[0]
+    else:
+        peers = mirror[:, z_count * vectors, :count].astype(jnp.int32).reshape(-1)
+        mirror = call(first_middle_kernel, out)(mirror)[0]
     mirror = exchange(mirror, Z_LO)
-    return own_direct, sent, far, mirror, cols
+    return own_direct, sent, far, mirror, peers
 
 
 def steps(tile_values, tile_row, tile_col, basis_init):
@@ -305,20 +302,23 @@
     vectors, size = basis_init.shape
     total_rows = size * lax.axis_size(COL_ROW)
 
-    own_direct, _, far, mirror, cols = product(pairs, tiles, basis_init, None, tile_col[0, 0])
+    note = jnp.pad(
+        tile_col[0].astype(BF16), [(0, ROWS - 1), (0, size - tiles.shape[0])]
+    )
+    own_direct, _, far, mirror, peers = product(pairs, tiles, basis_init, None, note, None)
     image, current, send = call(
         image_kernel,
         ((vectors, size), F32),
         ((vectors, size), BF16),
         ((mirror.shape[0], vectors + ROWS, size), BF16),
     )(own_direct, far, mirror)
-    own_direct, sent, far, mirror, _ = product(pairs, tiles, current, send, cols)
+    own_direct, sent, far, mirror, _ = product(pairs, tiles, current, send, None, peers)
     raw_image, send = call(
         last_kernel,
         ((vectors, size), F32),
-        ((lax.axis_size(COL), ROWS, 2 * LANES), BF16),
+        ((lax.axis_size(Y_X_CORE), ROWS, 2 * LANES), BF16),
     )(own_direct, far, mirror)
-    form = exchange(send, COL)
+    form = exchange(send, Y_X_CORE)
     gram = call(
         functools.partial(gram_kernel, rows=total_rows), ((vectors, vectors), F32)
     )(sent, far)[0]

time: 217 us -> 213 us (0.982)
  blocking collectives: 48.9 us -> 30.1 us
  waiting for transfers between devices: 60.8 us -> 72.1 us
  starting transfers between devices: 83.8 us -> 86.6 us
    all_to_all x3 -> x2, blocking collectives: 48.9 us -> 30.1 us  [exchange(): return lax.all_to_all(parts, axis, 0, 0, tiled=True)]
    ppermute x4, waiting for transfers between devices: 15.6 us -> 23.9 us  [partner(): return lax.ppermute(value, Z_HI, [(0, 1), (1, 0)])]
    all_to_all x8, starting transfers between devices: 52.4 us -> 60.5 us  [exchange(): return lax.all_to_all(parts, axis, 0, 0, tiled=True)]
    ppermute x4, starting transfers between devices: 31.5 us -> 26.1 us  [partner(): return lax.ppermute(value, Z_HI, [(0, 1), (1, 0)])]
    all_to_all x8, waiting for transfers between devices: 45.2 us -> 48.2 us  [exchange(): return lax.all_to_all(parts, axis, 0, 0, tiled=True)]
    pallas_call x12 -> x11, Pallas kernels: 11.1 us -> 10.9 us  [run(): pl.pallas_call(kernel, out_shape=tuple((out(shape, kind) for shape, kind...]
where the time goes in v6:
time: 213 us; the launch traced here: 212 us
  starting transfers between devices  86.6 us (41%)
  waiting for transfers between devices  72.1 us (34%)
  blocking collectives  30.1 us (14%)
  Pallas kernels  10.9 us (5%)
  other arithmetic  7.3 us (3%)
  local copies, waits for them, and re-layouts  3.31 us (2%)
    all_to_all x8, starting transfers between devices, exchange(): return lax.all_to_all(parts, axis, 0, 0, tiled=True)  60.5 us
    all_to_all x8, waiting for transfers between devices, exchange(): return lax.all_to_all(parts, axis, 0, 0, tiled=True)  48.2 us
    all_to_all x2, blocking collectives, exchange(): return lax.all_to_all(parts, axis, 0, 0, tiled=True)  30.1 us
    ppermute x4, starting transfers between devices, partner(): return lax.ppermute(value, Z_HI, [(0, 1), (1, 0)])  26.1 us
    ppermute x4, waiting for transfers between devices, partner(): return lax.ppermute(value, Z_HI, [(0, 1), (1, 0)])  23.9 us
    pallas_call x11, Pallas kernels, run(): pl.pallas_call(kernel, out_shape=tuple((out(shape, kind) for shape, kind...  10.9 us
  transfers between devices with their start and end apart: 12, of which 9 were waited for; matrix products, arithmetic and copies ran while one was open for 4% of the time, Pallas kernels for 0%

profile of v6, /device:TPU:1, one launch (start us, length us, event | category | flops | bytes accessed | tf_op | source)
XLA Modules:
  0.0 211.9 jit_solution(9703622030546976365)
XLA Ops:
  2.2 16.2 %all-to-all-start = ((bf16[32,32,256]{2,1,0:T(8,128)(2,1)}), bf16[32,32,256]{2,1,0:T(8,128)(2,1)S(1)}, u32[]{:S(2)}, u32[]{:S(2)}) async-start(bf16[32,32,256]{2,1,0:T(8,128)(2,1)} %broadcast_in_dim.12), calls=%async_computation | async-start | bytes 1048576 | tf_op jit(solution)/shard_map/all_to_all | solution.py:31
  18.4 7.9 %collective-permute-start = (bf16[32,256]{1,0:T(8,128)(2,1)S(1)}, bf16[32,256]{1,0:T(8,128)(2,1)S(1)}, u32[]{:S(2)}, u32[]{:S(2)}) collective-permute-start(bf16[32,256]{1,0:T(8,128)(2,1)S(1)} %copy-done.1), channel_id=1, source_target_pairs={{0,8},{8,0},{1,9},{9,1},{2,10},{10,2},{3,11},{11,3},{4,12},{12,4},... | collective-permute-start | bytes 49160 | tf_op jit(solution)/shard_map/ppermute | solution.py:49
  27.7 6.8 %collective-permute-done.other_ref = bf16[32,256]{1,0:T(8,128)(2,1)S(1)} collective-permute-done((bf16[32,256]{1,0:T(8,128)(2,1)S(1)}, bf16[32,256]{1,0:T(8,128)(2,1)S(1)}, u32[]{:S(2)}, u32[]{:S(2)}) %collective-permute-start) | collective-permute-done | bytes 16416 | tf_op jit(solution)/shard_map/ppermute | solution.py:49
  34.4 11.8 %all-to-all-done.column_ref = bf16[32,32,256]{2,1,0:T(8,128)(2,1)S(1)} async-done(((bf16[32,32,256]{2,1,0:T(8,128)(2,1)}), bf16[32,32,256]{2,1,0:T(8,128)(2,1)S(1)}, u32[]{:S(2)}, u32[]{:S(2)}) %all-to-all-start) | async-done | bytes 524320 | tf_op jit(solution)/shard_map/all_to_all | solution.py:31
  48.0 8.3 %all-to-all-start.1 = ((bf16[8,128,256]{2,1,0:T(8,128)(2,1)}), bf16[8,128,256]{2,1,0:T(8,128)(2,1)S(1)}, u32[]{:S(2)}, u32[]{:S(2)}) async-start(bf16[8,128,256]{2,1,0:T(8,128)(2,1)} %shard_map.67), calls=%async_computation.1 | async-start | bytes 1048576 | tf_op jit(solution)/shard_map/all_to_all | solution.py:31
  56.3 9.3 %all-to-all-done.1.row_ref = bf16[8,128,256]{2,1,0:T(8,128)(2,1)S(1)} async-done(((bf16[8,128,256]{2,1,0:T(8,128)(2,1)}), bf16[8,128,256]{2,1,0:T(8,128)(2,1)S(1)}, u32[]{:S(2)}, u32[]{:S(2)}) %all-to-all-start.1) | async-done | bytes 524320 | tf_op jit(solution)/shard_map/all_to_all | solution.py:31
  66.5 11.2 %all_to_all.50.mirror_ref = bf16[4,264,256]{2,1,0:T(8,128)(2,1)S(1)} all-to-all(bf16[4,264,256]{2,1,0:T(8,128)(2,1)S(1)} %get-tuple-element.16), channel_id=1, replica_groups=mesh['row_0'=8,'row_1'=4,'col_0'=2,'col_1'=4,'col_2'=2] {'row_1'}, dimensions={0} | all-to-all | bytes 1081344 | tf_op jit(solution)/shard_map/all_to_all | solution.py:31
  78.4 6.8 %all-to-all-start.3 = ((bf16[8,32,256]{2,1,0:T(8,128)(2,1)}), bf16[8,32,256]{2,1,0:T(8,128)(2,1)S(1)}, u32[]{:S(2)}, u32[]{:S(2)}) async-start(bf16[8,32,256]{2,1,0:T(8,128)(2,1)} %shard_map.69), calls=%async_computation.3 | async-start | bytes 262144 | tf_op jit(solution)/shard_map/all_to_all | solution.py:31
  85.3 6.0 %collective-permute-start.1 = (bf16[32,256]{1,0:T(8,128)(2,1)S(1)}, bf16[32,256]{1,0:T(8,128)(2,1)S(1)}, u32[]{:S(2)}, u32[]{:S(2)}) collective-permute-start(bf16[32,256]{1,0:T(8,128)(2,1)S(1)} %get-tuple-element.18), channel_id=1, source_target_pairs={{0,8},{8,0},{1,9},{9,1},{2,10},{10,2},{3,11},{11,3},{4,12},{12,4},... | collective-permute-start | bytes 49160 | tf_op jit(solution)/shard_map/ppermute | solution.py:49
  91.3 7.1 %collective-permute-done.1.far_ref = bf16[32,256]{1,0:T(8,128)(2,1)S(1)} collective-permute-done((bf16[32,256]{1,0:T(8,128)(2,1)S(1)}, bf16[32,256]{1,0:T(8,128)(2,1)S(1)}, u32[]{:S(2)}, u32[]{:S(2)}) %collective-permute-start.1) | collective-permute-done | bytes 16416 | tf_op jit(solution)/shard_map/ppermute | solution.py:49
  99.4 9.3 %all-to-all-start.4 = ((bf16[8,40,256]{2,1,0:T(8,128)(2,1)}), bf16[8,40,256]{2,1,0:T(8,128)(2,1)S(1)}, u32[]{:S(2)}, u32[]{:S(2)}) async-start(bf16[8,40,256]{2,1,0:T(8,128)(2,1)} %get-tuple-element.19), calls=%async_computation.4 | async-start | bytes 327680 | tf_op jit(solution)/shard_map/all_to_all | solution.py:31
  109.3 10.0 %all-to-all-done.4.by_z_ref = bf16[8,40,256]{2,1,0:T(8,128)(2,1)S(1)} async-done(((bf16[8,40,256]{2,1,0:T(8,128)(2,1)}), bf16[8,40,256]{2,1,0:T(8,128)(2,1)S(1)}, u32[]{:S(2)}, u32[]{:S(2)}) %all-to-all-start.4) | async-done | bytes 163872 | tf_op jit(solution)/shard_map/all_to_all | solution.py:31
  120.8 3.4 %all-to-all-start.5 = ((bf16[4,136,256]{2,1,0:T(8,128)(2,1)}), bf16[4,136,256]{2,1,0:T(8,128)(2,1)S(1)}, u32[]{:S(2)}, u32[]{:S(2)}) async-start(bf16[4,136,256]{2,1,0:T(8,128)(2,1)} %shard_map.71), calls=%async_computation.5 | async-start | bytes 557056 | tf_op jit(solution)/shard_map/all_to_all | solution.py:31
  124.2 6.1 %collective-permute-start.2 = (bf16[32,256]{1,0:T(8,128)(2,1)S(1)}, bf16[32,256]{1,0:T(8,128)(2,1)S(1)}, u32[]{:S(2)}, u32[]{:S(2)}) collective-permute-start(bf16[32,256]{1,0:T(8,128)(2,1)S(1)} %get-tuple-element.20.own_ref.near_ref), channel_id=1, source_target_pairs={{0,8},{8,0},{1,9},{9,1},{2,10},{10,2},{3,11},{11,3},{4,12},{12,4},... | collective-permute-start | bytes 49160 | tf_op jit(solution)/shard_map/ppermute | solution.py:49
  130.3 7.1 %collective-permute-done.2.other_ref = bf16[32,256]{1,0:T(8,128)(2,1)S(1)} collective-permute-done((bf16[32,256]{1,0:T(8,128)(2,1)S(1)}, bf16[32,256]{1,0:T(8,128)(2,1)S(1)}, u32[]{:S(2)}, u32[]{:S(2)}) %collective-permute-start.2) | collective-permute-done | bytes 16416 | tf_op jit(solution)/shard_map/ppermute | solution.py:49
  138.4 18.9 %all_to_all.51.row_ref = bf16[8,136,256]{2,1,0:T(8,128)(2,1)S(1)} all-to-all(bf16[8,136,256]{2,1,0:T(8,128)(2,1)S(1)} %shard_map.72), channel_id=1, replica_groups=mesh['row_0'=8,'row_1'=4,'col_0'=2,'col_1'=4,'col_2'=2] {'col_1','col_2'}, dimensions={0} | all-to-all | bytes 1114112 | tf_op jit(solution)/shard_map/all_to_all | solution.py:31
  159.0 6.0 %collective-permute-start.3 = (bf16[48,256]{1,0:T(8,128)(2,1)S(1)}, bf16[48,256]{1,0:T(8,128)(2,1)S(1)}, u32[]{:S(2)}, u32[]{:S(2)}) collective-permute-start(bf16[48,256]{1,0:T(8,128)(2,1)S(1)} %get-tuple-element.21.sent_ref), channel_id=1, source_target_pairs={{0,8},{8,0},{1,9},{9,1},{2,10},{10,2},{3,11},{11,3},{4,12},{12,4},... | collective-permute-start | bytes 73736 | tf_op jit(solution)/shard_map/ppermute | solution.py:49
  165.0 4.5 %all-to-all-start.7 = ((bf16[4,256,256]{2,1,0:T(8,128)(2,1)}), bf16[4,256,256]{2,1,0:T(8,128)(2,1)S(1)}, u32[]{:S(2)}, u32[]{:S(2)}) async-start(bf16[4,256,256]{2,1,0:T(8,128)(2,1)} %get-tuple-element.24), calls=%async_computation.7 | async-start | bytes 1048576 | tf_op jit(solution)/shard_map/all_to_all | solution.py:31
  169.5 2.9 %collective-permute-done.3.far_ref = bf16[48,256]{1,0:T(8,128)(2,1)S(1)} collective-permute-done((bf16[48,256]{1,0:T(8,128)(2,1)S(1)}, bf16[48,256]{1,0:T(8,128)(2,1)S(1)}, u32[]{:S(2)}, u32[]{:S(2)}) %collective-permute-start.3) | collective-permute-done | bytes 24608 | tf_op jit(solution)/shard_map/ppermute | solution.py:49
  172.6 2.9 %cholesky.17 = f32[32,32]{1,0:T(8,128)S(1)} custom-call(f32[32,32]{1,0:T(8,128)S(1)} %fusion.3), custom_call_target="Cholesky" | custom-call | tf_op jit(solution)/shard_map/jit(cholesky)/cholesky | solution.py:325
  180.0 3.4 %all-to-all-start.8 = ((bf16[8,40,256]{2,1,0:T(8,128)(2,1)}), bf16[8,40,256]{2,1,0:T(8,128)(2,1)S(1)}, u32[]{:S(2)}, u32[]{:S(2)}) async-start(bf16[8,40,256]{2,1,0:T(8,128)(2,1)} %shard_map.75), calls=%async_computation.8 | async-start | bytes 327680 | tf_op jit(solution)/shard_map/all_to_all | solution.py:31
  184.4 9.6 %all-to-all-done.8.mirror_ref = bf16[8,40,256]{2,1,0:T(8,128)(2,1)S(1)} async-done(((bf16[8,40,256]{2,1,0:T(8,128)(2,1)}), bf16[8,40,256]{2,1,0:T(8,128)(2,1)S(1)}, u32[]{:S(2)}, u32[]{:S(2)}) %all-to-all-start.8) | async-done | bytes 163872 | tf_op jit(solution)/shard_map/all_to_all | solution.py:31
  194.7 8.5 %all-to-all-start.9 = ((bf16[32,8,256]{2,1,0:T(8,128)(2,1)}), bf16[32,8,256]{2,1,0:T(8,128)(2,1)S(1)}, u32[]{:S(2)}, u32[]{:S(2)}) async-start(bf16[32,8,256]{2,1,0:T(8,128)(2,1)} %get-tuple-element.25), calls=%async_computation.9 | async-start | bytes 262144 | tf_op jit(solution)/shard_map/all_to_all | solution.py:31
  203.3 7.4 %all-to-all-done.9.bits_ref = bf16[32,8,256]{2,1,0:T(8,128)(2,1)S(1)} async-done(((bf16[32,8,256]{2,1,0:T(8,128)(2,1)}), bf16[32,8,256]{2,1,0:T(8,128)(2,1)S(1)}, u32[]{:S(2)}, u32[]{:S(2)}) %all-to-all-start.9) | async-done | bytes 131104 | tf_op jit(solution)/shard_map/all_to_all | solution.py:31
  (40 shorter events, 19.4 us)
Async XLA Ops:
  2.2 16.2 %copy-start.1 = (bf16[32,256]{1,0:T(8,128)(2,1)S(1)}, bf16[32,256]{1,0:T(8,128)(2,1)}, u32[]{:S(2)}) copy-start(bf16[32,256]{1,0:T(8,128)(2,1)} %near_ref.1) | copy-start | bytes 49156
  2.2 44.0 %copy-start = (bf16[1,1,4,256,256]{4,3,2,1,0:T(8,128)(2,1)S(1)}, bf16[1,1,4,256,256]{4,3,2,1,0:T(8,128)(2,1)}, u32[]{:S(2)}) copy-start(bf16[1,1,4,256,256]{4,3,2,1,0:T(8,128)(2,1)} %param.4) | copy-start | bytes 1572868
  2.2 44.0 %all-to-all-start = ((bf16[32,32,256]{2,1,0:T(8,128)(2,1)}), bf16[32,32,256]{2,1,0:T(8,128)(2,1)S(1)}, u32[]{:S(2)}, u32[]{:S(2)}) async-start(bf16[32,32,256]{2,1,0:T(8,128)(2,1)} %broadcast_in_dim.12), calls=%async_computation | async-start | bytes 1048576 | tf_op jit(solution)/shard_map/all_to_all | solution.py:31
  18.4 16.0 %collective-permute-start = (bf16[32,256]{1,0:T(8,128)(2,1)S(1)}, bf16[32,256]{1,0:T(8,128)(2,1)S(1)}, u32[]{:S(2)}, u32[]{:S(2)}) collective-permute-start(bf16[32,256]{1,0:T(8,128)(2,1)S(1)} %copy-done.1), channel_id=1, source_target_pairs={{0,8},{8,0},{1,9},{9,1},{2,10},{10,2},{3,11},{11,3},{4,12},{12,4},... | collective-permute-start | bytes 49160 | tf_op jit(solution)/shard_map/ppermute | solution.py:49
  26.4 0.7 copy-start.3
  26.4 0.7 copy-start.4
  48.0 17.7 %all-to-all-start.1 = ((bf16[8,128,256]{2,1,0:T(8,128)(2,1)}), bf16[8,128,256]{2,1,0:T(8,128)(2,1)S(1)}, u32[]{:S(2)}, u32[]{:S(2)}) async-start(bf16[8,128,256]{2,1,0:T(8,128)(2,1)} %shard_map.67), calls=%async_computation.1 | async-start | bytes 1048576 | tf_op jit(solution)/shard_map/all_to_all | solution.py:31
  78.4 20.0 %all-to-all-start.3 = ((bf16[8,32,256]{2,1,0:T(8,128)(2,1)}), bf16[8,32,256]{2,1,0:T(8,128)(2,1)S(1)}, u32[]{:S(2)}, u32[]{:S(2)}) async-start(bf16[8,32,256]{2,1,0:T(8,128)(2,1)} %shard_map.69), calls=%async_computation.3 | async-start | bytes 262144 | tf_op jit(solution)/shard_map/all_to_all | solution.py:31
  85.3 13.2 %collective-permute-start.1 = (bf16[32,256]{1,0:T(8,128)(2,1)S(1)}, bf16[32,256]{1,0:T(8,128)(2,1)S(1)}, u32[]{:S(2)}, u32[]{:S(2)}) collective-permute-start(bf16[32,256]{1,0:T(8,128)(2,1)S(1)} %get-tuple-element.18), channel_id=1, source_target_pairs={{0,8},{8,0},{1,9},{9,1},{2,10},{10,2},{3,11},{11,3},{4,12},{12,4},... | collective-permute-start | bytes 49160 | tf_op jit(solution)/shard_map/ppermute | solution.py:49
  99.4 20.0 %all-to-all-start.4 = ((bf16[8,40,256]{2,1,0:T(8,128)(2,1)}), bf16[8,40,256]{2,1,0:T(8,128)(2,1)S(1)}, u32[]{:S(2)}, u32[]{:S(2)}) async-start(bf16[8,40,256]{2,1,0:T(8,128)(2,1)} %get-tuple-element.19), calls=%async_computation.4 | async-start | bytes 327680 | tf_op jit(solution)/shard_map/all_to_all | solution.py:31
  120.8 16.7 %all-to-all-start.5 = ((bf16[4,136,256]{2,1,0:T(8,128)(2,1)}), bf16[4,136,256]{2,1,0:T(8,128)(2,1)S(1)}, u32[]{:S(2)}, u32[]{:S(2)}) async-start(bf16[4,136,256]{2,1,0:T(8,128)(2,1)} %shard_map.71), calls=%async_computation.5 | async-start | bytes 557056 | tf_op jit(solution)/shard_map/all_to_all | solution.py:31
  124.2 13.2 %collective-permute-start.2 = (bf16[32,256]{1,0:T(8,128)(2,1)S(1)}, bf16[32,256]{1,0:T(8,128)(2,1)S(1)}, u32[]{:S(2)}, u32[]{:S(2)}) collective-permute-start(bf16[32,256]{1,0:T(8,128)(2,1)S(1)} %get-tuple-element.20.own_ref.near_ref), channel_id=1, source_target_pairs={{0,8},{8,0},{1,9},{9,1},{2,10},{10,2},{3,11},{11,3},{4,12},{12,4},... | collective-permute-start | bytes 49160 | tf_op jit(solution)/shard_map/ppermute | solution.py:49
  159.0 13.4 %collective-permute-start.3 = (bf16[48,256]{1,0:T(8,128)(2,1)S(1)}, bf16[48,256]{1,0:T(8,128)(2,1)S(1)}, u32[]{:S(2)}, u32[]{:S(2)}) collective-permute-start(bf16[48,256]{1,0:T(8,128)(2,1)S(1)} %get-tuple-element.21.sent_ref), channel_id=1, source_target_pairs={{0,8},{8,0},{1,9},{9,1},{2,10},{10,2},{3,11},{11,3},{4,12},{12,4},... | collective-permute-start | bytes 73736 | tf_op jit(solution)/shard_map/ppermute | solution.py:49
  165.0 14.2 %all-to-all-start.7 = ((bf16[4,256,256]{2,1,0:T(8,128)(2,1)}), bf16[4,256,256]{2,1,0:T(8,128)(2,1)S(1)}, u32[]{:S(2)}, u32[]{:S(2)}) async-start(bf16[4,256,256]{2,1,0:T(8,128)(2,1)} %get-tuple-element.24), calls=%async_computation.7 | async-start | bytes 1048576 | tf_op jit(solution)/shard_map/all_to_all | solution.py:31
  180.0 14.0 %all-to-all-start.8 = ((bf16[8,40,256]{2,1,0:T(8,128)(2,1)}), bf16[8,40,256]{2,1,0:T(8,128)(2,1)S(1)}, u32[]{:S(2)}, u32[]{:S(2)}) async-start(bf16[8,40,256]{2,1,0:T(8,128)(2,1)} %shard_map.75), calls=%async_computation.8 | async-start | bytes 327680 | tf_op jit(solution)/shard_map/all_to_all | solution.py:31
  183.8 0.6 copy-start.2
  194.7 16.1 %all-to-all-start.9 = ((bf16[32,8,256]{2,1,0:T(8,128)(2,1)}), bf16[32,8,256]{2,1,0:T(8,128)(2,1)S(1)}, u32[]{:S(2)}, u32[]{:S(2)}) async-start(bf16[32,8,256]{2,1,0:T(8,128)(2,1)} %get-tuple-element.25), calls=%async_computation.9 | async-start | bytes 262144 | tf_op jit(solution)/shard_map/all_to_all | solution.py:31

commit v7 on v6

--- a/solution.py
+++ b/solution.py
@@ -93,6 +93,14 @@
     if isinstance(slot, int):
         return pl.ds(start + slot * length, length)
     return pl.ds(pl.multiple_of(start + slot * length, length), length)
+
+
+def spread_kernel(by_z_ref, note_ref, out_ref):
+    length = by_z_ref.shape[1]
+    for y in range(out_ref.shape[0]):
+        for z in range(by_z_ref.shape[0]):
+            out_ref[y, pl.ds(z * length, length)] = by_z_ref[z]
+        out_ref[y, pl.ds(by_z_ref.shape[0] * length, ROWS)] = note_ref[...]
 
 
 def select_kernel(peer_ref, by_z_ref, out_ref, *, vectors):
@@ -116,10 +124,8 @@
     side = pair_ref[2 * tiles]
     for t in range(tiles):
         j = pair_ref[tiles + t]
-        if extra:
-            from_column = column_ref[parted(j, y_count)[1], pl.ds(t * vectors, vectors)]
-        else:
-            from_column = column_ref[j]
+        z, y = parted(j, y_count)
+        from_column = column_ref[y, span(t if extra else z, vectors)]
         sums_ref[t] = lax.dot_general(
             from_column, tile_ref[t], (((1,), (1,)), ((), ())), preferred_element_type=F32
         )
@@ -171,11 +177,8 @@
         form = dot(near_ref[...].astype(F32), sums[0], 1, 1)
         form += dot(other_ref[...].astype(F32), sums[1], 1, 1)
         store_bits(far_ref, (pl.ds(vectors + ROWS, ROWS),), pack(form))
-    length = out_ref.shape[1] - ROWS * (not extra)
     for k in range(y_count):
-        out_ref[k, pl.ds(0, length)] = jnp.zeros((length, out_ref.shape[2]), BF16)
-        if not extra:
-            out_ref[k, pl.ds(length, ROWS)] = other_ref[...]
+        out_ref[k] = jnp.zeros(out_ref.shape[1:], BF16)
     slots = []
     for t in range(tiles):
         j = pair_ref[tiles + t]
@@ -253,20 +256,20 @@
     count = tiles.shape[0]
     y_count, z_count, xc_count = (lax.axis_size(Y), lax.axis_size(Z_LO), lax.axis_size(X_CORE))
     extra = send_z is not None
+    if not extra:
+        send_z = jnp.broadcast_to(current[None], (z_count, vectors, size))
+    by_z = exchange(send_z, Z_LO)
+    other = partner(current)
     if extra:
-        by_z = exchange(send_z, Z_LO)
-        other = partner(current)
-        send = call(
-            functools.partial(select_kernel, vectors=vectors),
-            ((y_count, count * vectors + ROWS, size), BF16),
-            scalars=1,
-        )(peers, by_z)[0]
-        column_block = exchange(send, Y)
+        select = functools.partial(select_kernel, vectors=vectors)
+        out = ((y_count, count * vectors + ROWS, size), BF16)
+        send = call(select, out, scalars=1)(peers, by_z)[0]
     else:
-        other = partner(current)
-        row_count = lax.axis_size(ROW)
-        send = jnp.broadcast_to(current[None], (row_count, vectors, size))
-        column_block = exchange(send, ROW)
+        out = ((y_count, z_count * vectors + ROWS, size), BF16)
+        send = call(spread_kernel, out)(by_z, note)[0]
+    column_block = exchange(send, Y)
+    if not extra:
+        peers = column_block[:, z_count * vectors, :count].astype(jnp.int32).reshape(-1)
     send = call(
         functools.partial(direct_kernel, extra=extra),
         ((xc_count, 4 * vectors + ROWS * extra, size), BF16),
@@ -276,12 +279,12 @@
     arrived = exchange(send, X_CORE)
     send, own_direct, far = call(
         mirror_kernel,
-        ((y_count, z_count * vectors + ROWS * (not extra), size), BF16),
+        ((y_count, z_count * vectors, size), BF16),
         ((vectors, size), F32),
         ((vectors + 2 * ROWS * extra, size), BF16),
         scalars=1,
         scratch=[pltpu.VMEM((count, vectors, size), F32)],
-    )(pairs, arrived, tiles, current, other if extra else note)
+    )(pairs, arrived, tiles, current, other)
     mirror = exchange(send, Y)
     sent, far = (far, partner(far))
     out = ((z_count, vectors + ROWS * extra, size), BF16)
@@ -289,7 +292,6 @@
         middle = functools.partial(second_middle_kernel, vectors=vectors)
         mirror = call(middle, out)(mirror, sent, far)[0]
     else:
-        peers = mirror[:, z_count * vectors, :count].astype(jnp.int32).reshape(-1)
         mirror = call(first_middle_kernel, out)(mirror)[0]
     mirror = exchange(mirror, Z_LO)
     return own_direct, sent, far, mirror, peers

time: 213 us -> 208 us (0.977)
  blocking collectives: 30.1 us -> 48.9 us
  waiting for transfers between devices: 72.1 us -> 53.4 us
  starting transfers between devices: 86.6 us -> 82 us
    all_to_all x2 -> x3, blocking collectives: 30.1 us -> 48.9 us  [exchange(): return lax.all_to_all(parts, axis, 0, 0, tiled=True)]
    all_to_all x8, waiting for transfers between devices: 48.2 us -> 37.7 us  [exchange(): return lax.all_to_all(parts, axis, 0, 0, tiled=True)]
    all_to_all x8, starting transfers between devices: 60.5 us -> 50.5 us  [exchange(): return lax.all_to_all(parts, axis, 0, 0, tiled=True)]
    ppermute x4, waiting for transfers between devices: 23.9 us -> 15.6 us  [partner(): return lax.ppermute(value, Z_HI, [(0, 1), (1, 0)])]
    ppermute x4, starting transfers between devices: 26.1 us -> 31.5 us  [partner(): return lax.ppermute(value, Z_HI, [(0, 1), (1, 0)])]
    pallas_call x11 -> x12, Pallas kernels: 10.9 us -> 10.9 us  [run(): pl.pallas_call(kernel, out_shape=tuple((out(shape, kind) for shape, kind...]
where the time goes in v7:
time: 208 us; the launch traced here: 207 us
  starting transfers between devices  82 us (39%)
  waiting for transfers between devices  53.4 us (26%)
  blocking collectives  48.9 us (24%)
  Pallas kernels  10.9 us (5%)
  other arithmetic  7.3 us (4%)
  local copies, waits for them, and re-layouts  3.09 us (1%)
    all_to_all x8, starting transfers between devices, exchange(): return lax.all_to_all(parts, axis, 0, 0, tiled=True)  50.5 us
    all_to_all x3, blocking collectives, exchange(): return lax.all_to_all(parts, axis, 0, 0, tiled=True)  48.9 us
    all_to_all x8, waiting for transfers between devices, exchange(): return lax.all_to_all(parts, axis, 0, 0, tiled=True)  37.7 us
    ppermute x4, starting transfers between devices, partner(): return lax.ppermute(value, Z_HI, [(0, 1), (1, 0)])  31.5 us
    ppermute x4, waiting for transfers between devices, partner(): return lax.ppermute(value, Z_HI, [(0, 1), (1, 0)])  15.6 us
    pallas_call x12, Pallas kernels, run(): pl.pallas_call(kernel, out_shape=tuple((out(shape, kind) for shape, kind...  10.9 us
  transfers between devices with their start and end apart: 12, of which 9 were waited for; matrix products, arithmetic and copies ran while one was open for 4% of the time, Pallas kernels for 0%

profile of v7, /device:TPU:1, one launch (start us, length us, event | category | flops | bytes accessed | tf_op | source)
XLA Modules:
  0.0 207.2 jit_solution(5894775080401180415)
XLA Ops:
  2.0 13.2 %all-to-all-start = ((bf16[8,32,256]{2,1,0:T(8,128)(2,1)}), bf16[8,32,256]{2,1,0:T(8,128)(2,1)S(1)}, u32[]{:S(2)}, u32[]{:S(2)}) async-start(bf16[8,32,256]{2,1,0:T(8,128)(2,1)} %broadcast_in_dim.12), calls=%async_computation | async-start | bytes 262144 | tf_op jit(solution)/shard_map/all_to_all | solution.py:31
  15.2 10.3 %all-to-all-done.by_z_ref = bf16[8,32,256]{2,1,0:T(8,128)(2,1)S(1)} async-done(((bf16[8,32,256]{2,1,0:T(8,128)(2,1)}), bf16[8,32,256]{2,1,0:T(8,128)(2,1)S(1)}, u32[]{:S(2)}, u32[]{:S(2)}) %all-to-all-start) | async-done | bytes 131104 | tf_op jit(solution)/shard_map/all_to_all | solution.py:31
  26.4 4.3 %all-to-all-start.1 = ((bf16[4,264,256]{2,1,0:T(8,128)(2,1)}), bf16[4,264,256]{2,1,0:T(8,128)(2,1)S(1)}, u32[]{:S(2)}, u32[]{:S(2)}) async-start(bf16[4,264,256]{2,1,0:T(8,128)(2,1)} %shard_map.67), calls=%async_computation.1 | async-start | bytes 1081344 | tf_op jit(solution)/shard_map/all_to_all | solution.py:31
  30.7 7.9 %collective-permute-start = (bf16[32,256]{1,0:T(8,128)(2,1)S(1)}, bf16[32,256]{1,0:T(8,128)(2,1)S(1)}, u32[]{:S(2)}, u32[]{:S(2)}) collective-permute-start(bf16[32,256]{1,0:T(8,128)(2,1)S(1)} %copy-done.1), channel_id=1, source_target_pairs={{0,8},{8,0},{1,9},{9,1},{2,10},{10,2},{3,11},{11,3},{4,12},{12,4},... | collective-permute-start | bytes 49160 | tf_op jit(solution)/shard_map/ppermute | solution.py:49
  39.9 4.0 %collective-permute-done.other_ref = bf16[32,256]{1,0:T(8,128)(2,1)S(1)} collective-permute-done((bf16[32,256]{1,0:T(8,128)(2,1)S(1)}, bf16[32,256]{1,0:T(8,128)(2,1)S(1)}, u32[]{:S(2)}, u32[]{:S(2)}) %collective-permute-start) | collective-permute-done | bytes 16416 | tf_op jit(solution)/shard_map/ppermute | solution.py:49
  44.8 17.7 %all_to_all.55.row_ref = bf16[8,128,256]{2,1,0:T(8,128)(2,1)S(1)} all-to-all(bf16[8,128,256]{2,1,0:T(8,128)(2,1)S(1)} %shard_map.68), channel_id=1, replica_groups=mesh['row_0'=8,'row_1'=4,'col_0'=2,'col_1'=4,'col_2'=2] {'col_1','col_2'}, dimensions={0} | all-to-all | bytes 1048576 | tf_op jit(solution)/shard_map/all_to_all | solution.py:31
  63.4 12.0 %all_to_all.56.mirror_ref = bf16[4,256,256]{2,1,0:T(8,128)(2,1)S(1)} all-to-all(bf16[4,256,256]{2,1,0:T(8,128)(2,1)S(1)} %get-tuple-element.18), channel_id=1, replica_groups=mesh['row_0'=8,'row_1'=4,'col_0'=2,'col_1'=4,'col_2'=2] {'row_1'}, dimensions={0} | all-to-all | bytes 1048576 | tf_op jit(solution)/shard_map/all_to_all | solution.py:31
  76.1 4.1 %all-to-all-start.4 = ((bf16[8,32,256]{2,1,0:T(8,128)(2,1)}), bf16[8,32,256]{2,1,0:T(8,128)(2,1)S(1)}, u32[]{:S(2)}, u32[]{:S(2)}) async-start(bf16[8,32,256]{2,1,0:T(8,128)(2,1)} %shard_map.70), calls=%async_computation.4 | async-start | bytes 262144 | tf_op jit(solution)/shard_map/all_to_all | solution.py:31
  80.2 7.8 %collective-permute-start.1 = (bf16[32,256]{1,0:T(8,128)(2,1)S(1)}, bf16[32,256]{1,0:T(8,128)(2,1)S(1)}, u32[]{:S(2)}, u32[]{:S(2)}) collective-permute-start(bf16[32,256]{1,0:T(8,128)(2,1)S(1)} %get-tuple-element.17), channel_id=1, source_target_pairs={{0,8},{8,0},{1,9},{9,1},{2,10},{10,2},{3,11},{11,3},{4,12},{12,4},... | collective-permute-start | bytes 49160 | tf_op jit(solution)/shard_map/ppermute | solution.py:49
  88.1 5.3 %collective-permute-done.1.far_ref = bf16[32,256]{1,0:T(8,128)(2,1)S(1)} collective-permute-done((bf16[32,256]{1,0:T(8,128)(2,1)S(1)}, bf16[32,256]{1,0:T(8,128)(2,1)S(1)}, u32[]{:S(2)}, u32[]{:S(2)}) %collective-permute-start.1) | collective-permute-done | bytes 16416 | tf_op jit(solution)/shard_map/ppermute | solution.py:49
  94.3 9.3 %all-to-all-start.5 = ((bf16[8,40,256]{2,1,0:T(8,128)(2,1)}), bf16[8,40,256]{2,1,0:T(8,128)(2,1)S(1)}, u32[]{:S(2)}, u32[]{:S(2)}) async-start(bf16[8,40,256]{2,1,0:T(8,128)(2,1)} %get-tuple-element.19), calls=%async_computation.5 | async-start | bytes 327680 | tf_op jit(solution)/shard_map/all_to_all | solution.py:31
  104.3 10.0 %all-to-all-done.5.by_z_ref = bf16[8,40,256]{2,1,0:T(8,128)(2,1)S(1)} async-done(((bf16[8,40,256]{2,1,0:T(8,128)(2,1)}), bf16[8,40,256]{2,1,0:T(8,128)(2,1)S(1)}, u32[]{:S(2)}, u32[]{:S(2)}) %all-to-all-start.5) | async-done | bytes 163872 | tf_op jit(solution)/shard_map/all_to_all | solution.py:31
  115.7 3.4 %all-to-all-start.6 = ((bf16[4,136,256]{2,1,0:T(8,128)(2,1)}), bf16[4,136,256]{2,1,0:T(8,128)(2,1)S(1)}, u32[]{:S(2)}, u32[]{:S(2)}) async-start(bf16[4,136,256]{2,1,0:T(8,128)(2,1)} %shard_map.72), calls=%async_computation.6 | async-start | bytes 557056 | tf_op jit(solution)/shard_map/all_to_all | solution.py:31
  119.2 7.9 %collective-permute-start.2 = (bf16[32,256]{1,0:T(8,128)(2,1)S(1)}, bf16[32,256]{1,0:T(8,128)(2,1)S(1)}, u32[]{:S(2)}, u32[]{:S(2)}) collective-permute-start(bf16[32,256]{1,0:T(8,128)(2,1)S(1)} %get-tuple-element.20.own_ref.near_ref), channel_id=1, source_target_pairs={{0,8},{8,0},{1,9},{9,1},{2,10},{10,2},{3,11},{11,3},{4,12},{12,4},... | collective-permute-start | bytes 49160 | tf_op jit(solution)/shard_map/ppermute | solution.py:49
  127.0 5.4 %collective-permute-done.2.other_ref = bf16[32,256]{1,0:T(8,128)(2,1)S(1)} collective-permute-done((bf16[32,256]{1,0:T(8,128)(2,1)S(1)}, bf16[32,256]{1,0:T(8,128)(2,1)S(1)}, u32[]{:S(2)}, u32[]{:S(2)}) %collective-permute-start.2) | collective-permute-done | bytes 16416 | tf_op jit(solution)/shard_map/ppermute | solution.py:49
  133.4 19.2 %all_to_all.57.row_ref = bf16[8,136,256]{2,1,0:T(8,128)(2,1)S(1)} all-to-all(bf16[8,136,256]{2,1,0:T(8,128)(2,1)S(1)} %shard_map.73), channel_id=1, replica_groups=mesh['row_0'=8,'row_1'=4,'col_0'=2,'col_1'=4,'col_2'=2] {'col_1','col_2'}, dimensions={0} | all-to-all | bytes 1114112 | tf_op jit(solution)/shard_map/all_to_all | solution.py:31
  154.3 7.9 %collective-permute-start.3 = (bf16[48,256]{1,0:T(8,128)(2,1)S(1)}, bf16[48,256]{1,0:T(8,128)(2,1)S(1)}, u32[]{:S(2)}, u32[]{:S(2)}) collective-permute-start(bf16[48,256]{1,0:T(8,128)(2,1)S(1)} %get-tuple-element.21.sent_ref), channel_id=1, source_target_pairs={{0,8},{8,0},{1,9},{9,1},{2,10},{10,2},{3,11},{11,3},{4,12},{12,4},... | collective-permute-start | bytes 73736 | tf_op jit(solution)/shard_map/ppermute | solution.py:49
  162.2 4.5 %all-to-all-start.8 = ((bf16[4,256,256]{2,1,0:T(8,128)(2,1)}), bf16[4,256,256]{2,1,0:T(8,128)(2,1)S(1)}, u32[]{:S(2)}, u32[]{:S(2)}) async-start(bf16[4,256,256]{2,1,0:T(8,128)(2,1)} %get-tuple-element.24), calls=%async_computation.8 | async-start | bytes 1048576 | tf_op jit(solution)/shard_map/all_to_all | solution.py:31
  167.7 2.9 %cholesky.17 = f32[32,32]{1,0:T(8,128)S(1)} custom-call(f32[32,32]{1,0:T(8,128)S(1)} %fusion.3), custom_call_target="Cholesky" | custom-call | tf_op jit(solution)/shard_map/jit(cholesky)/cholesky | solution.py:327
  172.0 2.4 %custom-call.6 = f32[1,32,32]{1,2,0:T(8,128)S(1)} custom-call(f32[1,32,32]{2,1,0:T(8,128)S(1)} %fusion), custom_call_target="InvertDiagBlocksLowerTriangular" | custom-call | tf_op jit(solution)/shard_map/triangular_solve | solution.py:328
  175.5 3.4 %all-to-all-start.9 = ((bf16[8,40,256]{2,1,0:T(8,128)(2,1)}), bf16[8,40,256]{2,1,0:T(8,128)(2,1)S(1)}, u32[]{:S(2)}, u32[]{:S(2)}) async-start(bf16[8,40,256]{2,1,0:T(8,128)(2,1)} %shard_map.76), calls=%async_computation.9 | async-start | bytes 327680 | tf_op jit(solution)/shard_map/all_to_all | solution.py:31
  179.9 9.6 %all-to-all-done.9.mirror_ref = bf16[8,40,256]{2,1,0:T(8,128)(2,1)S(1)} async-done(((bf16[8,40,256]{2,1,0:T(8,128)(2,1)}), bf16[8,40,256]{2,1,0:T(8,128)(2,1)S(1)}, u32[]{:S(2)}, u32[]{:S(2)}) %all-to-all-start.9) | async-done | bytes 163872 | tf_op jit(solution)/shard_map/all_to_all | solution.py:31
  190.2 8.3 %all-to-all-start.10 = ((bf16[32,8,256]{2,1,0:T(8,128)(2,1)}), bf16[32,8,256]{2,1,0:T(8,128)(2,1)S(1)}, u32[]{:S(2)}, u32[]{:S(2)}) async-start(bf16[32,8,256]{2,1,0:T(8,128)(2,1)} %get-tuple-element.25), calls=%async_computation.10 | async-start | bytes 262144 | tf_op jit(solution)/shard_map/all_to_all | solution.py:31
  198.6 7.4 %all-to-all-done.10.bits_ref = bf16[32,8,256]{2,1,0:T(8,128)(2,1)S(1)} async-done(((bf16[32,8,256]{2,1,0:T(8,128)(2,1)}), bf16[32,8,256]{2,1,0:T(8,128)(2,1)S(1)}, u32[]{:S(2)}, u32[]{:S(2)}) %all-to-all-start.10) | async-done | bytes 131104 | tf_op jit(solution)/shard_map/all_to_all | solution.py:31
  (42 shorter events, 18.0 us)
Async XLA Ops:
  2.0 13.2 %copy-start.3 = (s32[1,1,4]{2,1,0:T(1,128)S(1)}, s32[1,1,4]{2,1,0:T(1,128)}, u32[]{:S(2)}) copy-start(s32[1,1,4]{2,1,0:T(1,128)} %param.6) | copy-start | bytes 52
  2.0 23.5 %all-to-all-start = ((bf16[8,32,256]{2,1,0:T(8,128)(2,1)}), bf16[8,32,256]{2,1,0:T(8,128)(2,1)S(1)}, u32[]{:S(2)}, u32[]{:S(2)}) async-start(bf16[8,32,256]{2,1,0:T(8,128)(2,1)} %broadcast_in_dim.12), calls=%async_computation | async-start | bytes 262144 | tf_op jit(solution)/shard_map/all_to_all | solution.py:31
  26.4 4.3 %copy-start.1 = (bf16[32,256]{1,0:T(8,128)(2,1)S(1)}, bf16[32,256]{1,0:T(8,128)(2,1)}, u32[]{:S(2)}) copy-start(bf16[32,256]{1,0:T(8,128)(2,1)} %near_ref.1) | copy-start | bytes 49156
  26.4 17.5 %copy-start = (bf16[1,1,4,256,256]{4,3,2,1,0:T(8,128)(2,1)S(1)}, bf16[1,1,4,256,256]{4,3,2,1,0:T(8,128)(2,1)}, u32[]{:S(2)}) copy-start(bf16[1,1,4,256,256]{4,3,2,1,0:T(8,128)(2,1)} %param.4) | copy-start | bytes 1572868
  26.4 17.5 %all-to-all-start.1 = ((bf16[4,264,256]{2,1,0:T(8,128)(2,1)}), bf16[4,264,256]{2,1,0:T(8,128)(2,1)S(1)}, u32[]{:S(2)}, u32[]{:S(2)}) async-start(bf16[4,264,256]{2,1,0:T(8,128)(2,1)} %shard_map.67), calls=%async_computation.1 | async-start | bytes 1081344 | tf_op jit(solution)/shard_map/all_to_all | solution.py:31
  30.7 13.2 %collective-permute-start = (bf16[32,256]{1,0:T(8,128)(2,1)S(1)}, bf16[32,256]{1,0:T(8,128)(2,1)S(1)}, u32[]{:S(2)}, u32[]{:S(2)}) collective-permute-start(bf16[32,256]{1,0:T(8,128)(2,1)S(1)} %copy-done.1), channel_id=1, source_target_pairs={{0,8},{8,0},{1,9},{9,1},{2,10},{10,2},{3,11},{11,3},{4,12},{12,4},... | collective-permute-start | bytes 49160 | tf_op jit(solution)/shard_map/ppermute | solution.py:49
  38.6 0.7 copy-start.4
  76.1 17.3 %all-to-all-start.4 = ((bf16[8,32,256]{2,1,0:T(8,128)(2,1)}), bf16[8,32,256]{2,1,0:T(8,128)(2,1)S(1)}, u32[]{:S(2)}, u32[]{:S(2)}) async-start(bf16[8,32,256]{2,1,0:T(8,128)(2,1)} %shard_map.70), calls=%async_computation.4 | async-start | bytes 262144 | tf_op jit(solution)/shard_map/all_to_all | solution.py:31
  80.2 13.2 %collective-permute-start.1 = (bf16[32,256]{1,0:T(8,128)(2,1)S(1)}, bf16[32,256]{1,0:T(8,128)(2,1)S(1)}, u32[]{:S(2)}, u32[]{:S(2)}) collective-permute-start(bf16[32,256]{1,0:T(8,128)(2,1)S(1)} %get-tuple-element.17), channel_id=1, source_target_pairs={{0,8},{8,0},{1,9},{9,1},{2,10},{10,2},{3,11},{11,3},{4,12},{12,4},... | collective-permute-start | bytes 49160 | tf_op jit(solution)/shard_map/ppermute | solution.py:49
  94.3 20.0 %all-to-all-start.5 = ((bf16[8,40,256]{2,1,0:T(8,128)(2,1)}), bf16[8,40,256]{2,1,0:T(8,128)(2,1)S(1)}, u32[]{:S(2)}, u32[]{:S(2)}) async-start(bf16[8,40,256]{2,1,0:T(8,128)(2,1)} %get-tuple-element.19), calls=%async_computation.5 | async-start | bytes 327680 | tf_op jit(solution)/shard_map/all_to_all | solution.py:31
  115.7 16.7 %all-to-all-start.6 = ((bf16[4,136,256]{2,1,0:T(8,128)(2,1)}), bf16[4,136,256]{2,1,0:T(8,128)(2,1)S(1)}, u32[]{:S(2)}, u32[]{:S(2)}) async-start(bf16[4,136,256]{2,1,0:T(8,128)(2,1)} %shard_map.72), calls=%async_computation.6 | async-start | bytes 557056 | tf_op jit(solution)/shard_map/all_to_all | solution.py:31
  119.2 13.3 %collective-permute-start.2 = (bf16[32,256]{1,0:T(8,128)(2,1)S(1)}, bf16[32,256]{1,0:T(8,128)(2,1)S(1)}, u32[]{:S(2)}, u32[]{:S(2)}) collective-permute-start(bf16[32,256]{1,0:T(8,128)(2,1)S(1)} %get-tuple-element.20.own_ref.near_ref), channel_id=1, source_target_pairs={{0,8},{8,0},{1,9},{9,1},{2,10},{10,2},{3,11},{11,3},{4,12},{12,4},... | collective-permute-start | bytes 49160 | tf_op jit(solution)/shard_map/ppermute | solution.py:49
  154.3 13.3 %collective-permute-start.3 = (bf16[48,256]{1,0:T(8,128)(2,1)S(1)}, bf16[48,256]{1,0:T(8,128)(2,1)S(1)}, u32[]{:S(2)}, u32[]{:S(2)}) collective-permute-start(bf16[48,256]{1,0:T(8,128)(2,1)S(1)} %get-tuple-element.21.sent_ref), channel_id=1, source_target_pairs={{0,8},{8,0},{1,9},{9,1},{2,10},{10,2},{3,11},{11,3},{4,12},{12,4},... | collective-permute-start | bytes 73736 | tf_op jit(solution)/shard_map/ppermute | solution.py:49
  162.2 12.6 %all-to-all-start.8 = ((bf16[4,256,256]{2,1,0:T(8,128)(2,1)}), bf16[4,256,256]{2,1,0:T(8,128)(2,1)S(1)}, u32[]{:S(2)}, u32[]{:S(2)}) async-start(bf16[4,256,256]{2,1,0:T(8,128)(2,1)} %get-tuple-element.24), calls=%async_computation.8 | async-start | bytes 1048576 | tf_op jit(solution)/shard_map/all_to_all | solution.py:31
  175.5 14.0 %all-to-all-start.9 = ((bf16[8,40,256]{2,1,0:T(8,128)(2,1)}), bf16[8,40,256]{2,1,0:T(8,128)(2,1)S(1)}, u32[]{:S(2)}, u32[]{:S(2)}) async-start(bf16[8,40,256]{2,1,0:T(8,128)(2,1)} %shard_map.76), calls=%async_computation.9 | async-start | bytes 327680 | tf_op jit(solution)/shard_map/all_to_all | solution.py:31
  179.3 0.6 copy-start.2
  190.2 15.9 %all-to-all-start.10 = ((bf16[32,8,256]{2,1,0:T(8,128)(2,1)}), bf16[32,8,256]{2,1,0:T(8,128)(2,1)S(1)}, u32[]{:S(2)}, u32[]{:S(2)}) async-start(bf16[32,8,256]{2,1,0:T(8,128)(2,1)} %get-tuple-element.25), calls=%async_computation.10 | async-start | bytes 262144 | tf_op jit(solution)/shard_map/all_to_all | solution.py:31

commit v8 on v7

--- a/solution.py
+++ b/solution.py
@@ -16,7 +16,6 @@
 COL_ROW = ("col_0", "col_1", "col_2", "row_0", "row_1")
 HIGHEST = lax.Precision.HIGHEST
 VMEM = pl.BlockSpec(memory_space=pltpu.VMEM)
-SMEM = pl.BlockSpec(memory_space=pltpu.SMEM)
 F32, BF16 = (jnp.float32, jnp.bfloat16)
 
 
@@ -31,13 +30,13 @@
     return lax.all_to_all(parts, axis, 0, 0, tiled=True)
 
 
-def call(kernel, *outs, scalars=0, scratch=(), out=pltpu.VMEM):
+def call(kernel, *outs, scratch=(), out=pltpu.VMEM):
     def run(*args):
-        args = args[:scalars] + tuple(placed(arg) for arg in args[scalars:])
+        args = tuple(placed(arg) for arg in args)
         return pl.pallas_call(
             kernel,
             out_shape=tuple(out(shape, kind) for shape, kind in outs),
-            in_specs=[SMEM] * scalars + [VMEM] * (len(args) - scalars),
+            in_specs=[VMEM] * len(args),
             out_specs=tuple(VMEM for _ in outs),
             scratch_shapes=list(scratch),
         )(*args)
@@ -105,13 +104,13 @@
 
 def select_kernel(peer_ref, by_z_ref, out_ref, *, vectors):
     y_count = out_ref.shape[0]
-    tiles = peer_ref.shape[0] // y_count
+    tiles = (out_ref.shape[1] - ROWS) // vectors
     total = jnp.zeros((ROWS, LANES), F32)
     for z in range(by_z_ref.shape[0]):
         total += from_bits(by_z_ref[z, pl.ds(vectors, ROWS)])
     for y in range(y_count):
         for t in range(tiles):
-            place, _ = parted(peer_ref[y * tiles + t], y_count)
+            place, _ = parted(peer_ref[y, t], y_count)
             out_ref[y, pl.ds(t * vectors, vectors)] = by_z_ref[place, pl.ds(0, vectors)]
         store_bits(out_ref, (y, pl.ds(tiles * vectors, ROWS)), total)
 
@@ -121,9 +120,9 @@
 ):
     tiles, vectors = (tile_ref.shape[0], own_ref.shape[0])
     y_count, xc_count = (column_ref.shape[0], out_ref.shape[0])
-    side = pair_ref[2 * tiles]
+    side = pair_ref[0, 2 * tiles]
     for t in range(tiles):
-        j = pair_ref[tiles + t]
+        j = pair_ref[0, tiles + t]
         z, y = parted(j, y_count)
         from_column = column_ref[y, span(t if extra else z, vectors)]
         sums_ref[t] = lax.dot_general(
@@ -142,7 +141,7 @@
             store_bits(out_ref, (k, pl.ds(4 * vectors, ROWS)), total)
     slots = []
     for t in range(tiles):
-        i = pair_ref[t]
+        i = pair_ref[0, t]
         half, xc = parted(i, xc_count)
         half = lax.bitwise_xor(half, side)
         slots.append((i, (xc, span(half, vectors, 2 * vectors))))
@@ -155,9 +154,9 @@
     tiles, vectors = (tile_ref.shape[0], own_ref.shape[0])
     y_count, xc_count = (out_ref.shape[0], row_ref.shape[0])
     extra = row_ref.shape[1] > 4 * vectors
-    side = pair_ref[2 * tiles]
+    side = pair_ref[0, 2 * tiles]
     for t in range(tiles):
-        half, xc = parted(pair_ref[t], xc_count)
+        half, xc = parted(pair_ref[0, t], xc_count)
         from_row = row_ref[xc, span(lax.bitwise_xor(half, side), vectors)]
         sums_ref[t] = jnp.dot(from_row, tile_ref[t], preferred_element_type=F32)
     sums = []
@@ -181,7 +180,7 @@
         out_ref[k] = jnp.zeros(out_ref.shape[1:], BF16)
     slots = []
     for t in range(tiles):
-        j = pair_ref[tiles + t]
+        j = pair_ref[0, tiles + t]
         z, y = parted(j, y_count)
         slots.append((j, (y, span(z, vectors))))
     store_sums(out_ref, slots, sums_ref)
@@ -263,17 +262,16 @@
     if extra:
         select = functools.partial(select_kernel, vectors=vectors)
         out = ((y_count, count * vectors + ROWS, size), BF16)
-        send = call(select, out, scalars=1)(peers, by_z)[0]
+        send = call(select, out)(peers, by_z)[0]
     else:
         out = ((y_count, z_count * vectors + ROWS, size), BF16)
         send = call(spread_kernel, out)(by_z, note)[0]
     column_block = exchange(send, Y)
     if not extra:
-        peers = column_block[:, z_count * vectors, :count].astype(jnp.int32).reshape(-1)
+        peers = column_block[:, z_count * vectors, :LANES].astype(jnp.int32)
     send = call(
         functools.partial(direct_kernel, extra=extra),
         ((xc_count, 4 * vectors + ROWS * extra, size), BF16),
-        scalars=1,
         scratch=[pltpu.VMEM((count, vectors, size), F32)],
     )(pairs, column_block, tiles, current, other)[0]
     arrived = exchange(send, X_CORE)
@@ -282,7 +280,6 @@
         ((y_count, z_count * vectors, size), BF16),
         ((vectors, size), F32),
         ((vectors + 2 * ROWS * extra, size), BF16),
-        scalars=1,
         scratch=[pltpu.VMEM((count, vectors, size), F32)],
     )(pairs, arrived, tiles, current, other)
     mirror = exchange(send, Y)
@@ -300,7 +297,8 @@
 def steps(tile_values, tile_row, tile_col, basis_init):
     tiles = tile_values[0, 0]
     side = lax.axis_index(Z_HI).astype(jnp.int32)
-    pairs = jnp.concatenate([tile_row[0, 0], tile_col[0, 0], side[None]])
+    pairs = jnp.concatenate([tile_row[0], tile_col[0], side[None, None]], axis=1)
+    pairs = jnp.pad(pairs, [(0, 0), (0, LANES - pairs.shape[1])])
     vectors, size = basis_init.shape
     total_rows = size * lax.axis_size(COL_ROW)
 

time: 208 us -> 205 us (0.986)
  Pallas kernels: 10.9 us -> 7.96 us
    pallas_call x12, Pallas kernels: 10.9 us -> 7.96 us  [run(): pl.pallas_call(kernel, out_shape=tuple((out(shape, kind) for shape, kind...]
where the time goes in v8:
time: 205 us; the launch traced here: 204 us
  starting transfers between devices  82 us (40%)
  waiting for transfers between devices  54.5 us (27%)
  blocking collectives  48.9 us (24%)
  Pallas kernels  7.96 us (4%)
  other arithmetic  6.78 us (3%)
  local copies, waits for them, and re-layouts  2.51 us (1%)
    all_to_all x8, starting transfers between devices, exchange(): return lax.all_to_all(parts, axis, 0, 0, tiled=True)  50.5 us
    all_to_all x3, blocking collectives, exchange(): return lax.all_to_all(parts, axis, 0, 0, tiled=True)  48.9 us
    all_to_all x8, waiting for transfers between devices, exchange(): return lax.all_to_all(parts, axis, 0, 0, tiled=True)  38.3 us
    ppermute x4, starting transfers between devices, partner(): return lax.ppermute(value, Z_HI, [(0, 1), (1, 0)])  31.5 us
    ppermute x4, waiting for transfers between devices, partner(): return lax.ppermute(value, Z_HI, [(0, 1), (1, 0)])  16.2 us
    pallas_call x12, Pallas kernels, run(): pl.pallas_call(kernel, out_shape=tuple((out(shape, kind) for shape, kind...  7.96 us
  transfers between devices with their start and end apart: 12, of which 9 were waited for; matrix products, arithmetic and copies ran while one was open for 4% of the time, Pallas kernels for 0%

profile of v8, /device:TPU:1, one launch (start us, length us, event | category | flops | bytes accessed | tf_op | source)
XLA Modules:
  0.0 204.2 jit_solution(8029441115343347654)
XLA Ops:
  2.0 13.2 %all-to-all-start = ((bf16[8,32,256]{2,1,0:T(8,128)(2,1)}), bf16[8,32,256]{2,1,0:T(8,128)(2,1)S(1)}, u32[]{:S(2)}, u32[]{:S(2)}) async-start(bf16[8,32,256]{2,1,0:T(8,128)(2,1)} %broadcast_in_dim.12), calls=%async_computation | async-start | bytes 262144 | tf_op jit(solution)/shard_map/all_to_all | solution.py:30
  15.2 10.3 %all-to-all-done.by_z_ref = bf16[8,32,256]{2,1,0:T(8,128)(2,1)S(1)} async-done(((bf16[8,32,256]{2,1,0:T(8,128)(2,1)}), bf16[8,32,256]{2,1,0:T(8,128)(2,1)S(1)}, u32[]{:S(2)}, u32[]{:S(2)}) %all-to-all-start) | async-done | bytes 131104 | tf_op jit(solution)/shard_map/all_to_all | solution.py:30
  26.4 4.3 %all-to-all-start.1 = ((bf16[4,264,256]{2,1,0:T(8,128)(2,1)}), bf16[4,264,256]{2,1,0:T(8,128)(2,1)S(1)}, u32[]{:S(2)}, u32[]{:S(2)}) async-start(bf16[4,264,256]{2,1,0:T(8,128)(2,1)} %shard_map.67), calls=%async_computation.1 | async-start | bytes 1081344 | tf_op jit(solution)/shard_map/all_to_all | solution.py:30
  30.7 7.9 %collective-permute-start = (bf16[32,256]{1,0:T(8,128)(2,1)S(1)}, bf16[32,256]{1,0:T(8,128)(2,1)S(1)}, u32[]{:S(2)}, u32[]{:S(2)}) collective-permute-start(bf16[32,256]{1,0:T(8,128)(2,1)S(1)} %copy-done.1), channel_id=1, source_target_pairs={{0,8},{8,0},{1,9},{9,1},{2,10},{10,2},{3,11},{11,3},{4,12},{12,4},... | collective-permute-start | bytes 49160 | tf_op jit(solution)/shard_map/ppermute | solution.py:48
  39.4 4.5 %collective-permute-done.other_ref = bf16[32,256]{1,0:T(8,128)(2,1)S(1)} collective-permute-done((bf16[32,256]{1,0:T(8,128)(2,1)S(1)}, bf16[32,256]{1,0:T(8,128)(2,1)S(1)}, u32[]{:S(2)}, u32[]{:S(2)}) %collective-permute-start) | collective-permute-done | bytes 16416 | tf_op jit(solution)/shard_map/ppermute | solution.py:48
  44.2 17.7 %all_to_all.55.row_ref = bf16[8,128,256]{2,1,0:T(8,128)(2,1)S(1)} all-to-all(bf16[8,128,256]{2,1,0:T(8,128)(2,1)S(1)} %shard_map.68), channel_id=1, replica_groups=mesh['row_0'=8,'row_1'=4,'col_0'=2,'col_1'=4,'col_2'=2] {'col_1','col_2'}, dimensions={0} | all-to-all | bytes 1048576 | tf_op jit(solution)/shard_map/all_to_all | solution.py:30
  62.2 12.0 %all_to_all.56.mirror_ref = bf16[4,256,256]{2,1,0:T(8,128)(2,1)S(1)} all-to-all(bf16[4,256,256]{2,1,0:T(8,128)(2,1)S(1)} %get-tuple-element.18), channel_id=1, replica_groups=mesh['row_0'=8,'row_1'=4,'col_0'=2,'col_1'=4,'col_2'=2] {'row_1'}, dimensions={0} | all-to-all | bytes 1048576 | tf_op jit(solution)/shard_map/all_to_all | solution.py:30
  74.9 4.1 %all-to-all-start.4 = ((bf16[8,32,256]{2,1,0:T(8,128)(2,1)}), bf16[8,32,256]{2,1,0:T(8,128)(2,1)S(1)}, u32[]{:S(2)}, u32[]{:S(2)}) async-start(bf16[8,32,256]{2,1,0:T(8,128)(2,1)} %shard_map.70), calls=%async_computation.4 | async-start | bytes 262144 | tf_op jit(solution)/shard_map/all_to_all | solution.py:30
  79.0 7.8 %collective-permute-start.1 = (bf16[32,256]{1,0:T(8,128)(2,1)S(1)}, bf16[32,256]{1,0:T(8,128)(2,1)S(1)}, u32[]{:S(2)}, u32[]{:S(2)}) collective-permute-start(bf16[32,256]{1,0:T(8,128)(2,1)S(1)} %get-tuple-element.17), channel_id=1, source_target_pairs={{0,8},{8,0},{1,9},{9,1},{2,10},{10,2},{3,11},{11,3},{4,12},{12,4},... | collective-permute-start | bytes 49160 | tf_op jit(solution)/shard_map/ppermute | solution.py:48
  86.9 5.3 %collective-permute-done.1.far_ref = bf16[32,256]{1,0:T(8,128)(2,1)S(1)} collective-permute-done((bf16[32,256]{1,0:T(8,128)(2,1)S(1)}, bf16[32,256]{1,0:T(8,128)(2,1)S(1)}, u32[]{:S(2)}, u32[]{:S(2)}) %collective-permute-start.1) | collective-permute-done | bytes 16416 | tf_op jit(solution)/shard_map/ppermute | solution.py:48
  93.1 9.3 %all-to-all-start.5 = ((bf16[8,40,256]{2,1,0:T(8,128)(2,1)}), bf16[8,40,256]{2,1,0:T(8,128)(2,1)S(1)}, u32[]{:S(2)}, u32[]{:S(2)}) async-start(bf16[8,40,256]{2,1,0:T(8,128)(2,1)} %get-tuple-element.19), calls=%async_computation.5 | async-start | bytes 327680 | tf_op jit(solution)/shard_map/all_to_all | solution.py:30
  102.5 10.6 %all-to-all-done.5.by_z_ref = bf16[8,40,256]{2,1,0:T(8,128)(2,1)S(1)} async-done(((bf16[8,40,256]{2,1,0:T(8,128)(2,1)}), bf16[8,40,256]{2,1,0:T(8,128)(2,1)S(1)}, u32[]{:S(2)}, u32[]{:S(2)}) %all-to-all-start.5) | async-done | bytes 163872 | tf_op jit(solution)/shard_map/all_to_all | solution.py:30
  113.9 3.4 %all-to-all-start.6 = ((bf16[4,136,256]{2,1,0:T(8,128)(2,1)}), bf16[4,136,256]{2,1,0:T(8,128)(2,1)S(1)}, u32[]{:S(2)}, u32[]{:S(2)}) async-start(bf16[4,136,256]{2,1,0:T(8,128)(2,1)} %shard_map.72), calls=%async_computation.6 | async-start | bytes 557056 | tf_op jit(solution)/shard_map/all_to_all | solution.py:30
  117.4 7.9 %collective-permute-start.2 = (bf16[32,256]{1,0:T(8,128)(2,1)S(1)}, bf16[32,256]{1,0:T(8,128)(2,1)S(1)}, u32[]{:S(2)}, u32[]{:S(2)}) collective-permute-start(bf16[32,256]{1,0:T(8,128)(2,1)S(1)} %get-tuple-element.20.own_ref.near_ref), channel_id=1, source_target_pairs={{0,8},{8,0},{1,9},{9,1},{2,10},{10,2},{3,11},{11,3},{4,12},{12,4},... | collective-permute-start | bytes 49160 | tf_op jit(solution)/shard_map/ppermute | solution.py:48
  125.3 5.4 %collective-permute-done.2.other_ref = bf16[32,256]{1,0:T(8,128)(2,1)S(1)} collective-permute-done((bf16[32,256]{1,0:T(8,128)(2,1)S(1)}, bf16[32,256]{1,0:T(8,128)(2,1)S(1)}, u32[]{:S(2)}, u32[]{:S(2)}) %collective-permute-start.2) | collective-permute-done | bytes 16416 | tf_op jit(solution)/shard_map/ppermute | solution.py:48
  131.0 19.2 %all_to_all.57.row_ref = bf16[8,136,256]{2,1,0:T(8,128)(2,1)S(1)} all-to-all(bf16[8,136,256]{2,1,0:T(8,128)(2,1)S(1)} %shard_map.73), channel_id=1, replica_groups=mesh['row_0'=8,'row_1'=4,'col_0'=2,'col_1'=4,'col_2'=2] {'col_1','col_2'}, dimensions={0} | all-to-all | bytes 1114112 | tf_op jit(solution)/shard_map/all_to_all | solution.py:30
  151.3 7.8 %collective-permute-start.3 = (bf16[48,256]{1,0:T(8,128)(2,1)S(1)}, bf16[48,256]{1,0:T(8,128)(2,1)S(1)}, u32[]{:S(2)}, u32[]{:S(2)}) collective-permute-start(bf16[48,256]{1,0:T(8,128)(2,1)S(1)} %get-tuple-element.21.sent_ref), channel_id=1, source_target_pairs={{0,8},{8,0},{1,9},{9,1},{2,10},{10,2},{3,11},{11,3},{4,12},{12,4},... | collective-permute-start | bytes 73736 | tf_op jit(solution)/shard_map/ppermute | solution.py:48
  159.2 4.5 %all-to-all-start.8 = ((bf16[4,256,256]{2,1,0:T(8,128)(2,1)}), bf16[4,256,256]{2,1,0:T(8,128)(2,1)S(1)}, u32[]{:S(2)}, u32[]{:S(2)}) async-start(bf16[4,256,256]{2,1,0:T(8,128)(2,1)} %get-tuple-element.24), calls=%async_computation.8 | async-start | bytes 1048576 | tf_op jit(solution)/shard_map/all_to_all | solution.py:30
  164.7 2.9 %cholesky.17 = f32[32,32]{1,0:T(8,128)S(1)} custom-call(f32[32,32]{1,0:T(8,128)S(1)} %fusion.3), custom_call_target="Cholesky" | custom-call | tf_op jit(solution)/shard_map/jit(cholesky)/cholesky | solution.py:325
  169.0 2.4 %custom-call.6 = f32[1,32,32]{1,2,0:T(8,128)S(1)} custom-call(f32[1,32,32]{2,1,0:T(8,128)S(1)} %fusion), custom_call_target="InvertDiagBlocksLowerTriangular" | custom-call | tf_op jit(solution)/shard_map/triangular_solve | solution.py:326
  172.5 3.4 %all-to-all-start.9 = ((bf16[8,40,256]{2,1,0:T(8,128)(2,1)}), bf16[8,40,256]{2,1,0:T(8,128)(2,1)S(1)}, u32[]{:S(2)}, u32[]{:S(2)}) async-start(bf16[8,40,256]{2,1,0:T(8,128)(2,1)} %shard_map.76), calls=%async_computation.9 | async-start | bytes 327680 | tf_op jit(solution)/shard_map/all_to_all | solution.py:30
  176.9 9.6 %all-to-all-done.9.mirror_ref = bf16[8,40,256]{2,1,0:T(8,128)(2,1)S(1)} async-done(((bf16[8,40,256]{2,1,0:T(8,128)(2,1)}), bf16[8,40,256]{2,1,0:T(8,128)(2,1)S(1)}, u32[]{:S(2)}, u32[]{:S(2)}) %all-to-all-start.9) | async-done | bytes 163872 | tf_op jit(solution)/shard_map/all_to_all | solution.py:30
  187.2 8.3 %all-to-all-start.10 = ((bf16[32,8,256]{2,1,0:T(8,128)(2,1)}), bf16[32,8,256]{2,1,0:T(8,128)(2,1)S(1)}, u32[]{:S(2)}, u32[]{:S(2)}) async-start(bf16[32,8,256]{2,1,0:T(8,128)(2,1)} %get-tuple-element.25), calls=%async_computation.10 | async-start | bytes 262144 | tf_op jit(solution)/shard_map/all_to_all | solution.py:30
  195.6 7.4 %all-to-all-done.10.bits_ref = bf16[32,8,256]{2,1,0:T(8,128)(2,1)S(1)} async-done(((bf16[32,8,256]{2,1,0:T(8,128)(2,1)}), bf16[32,8,256]{2,1,0:T(8,128)(2,1)S(1)}, u32[]{:S(2)}, u32[]{:S(2)}) %all-to-all-start.10) | async-done | bytes 131104 | tf_op jit(solution)/shard_map/all_to_all | solution.py:30
  (43 shorter events, 13.9 us)
Async XLA Ops:
  2.0 13.2 %copy-start.3 = (s32[1,1,4]{2,1,0:T(1,128)S(1)}, s32[1,1,4]{2,1,0:T(1,128)}, u32[]{:S(2)}) copy-start(s32[1,1,4]{2,1,0:T(1,128)} %param.6) | copy-start | bytes 52
  2.0 23.5 %all-to-all-start = ((bf16[8,32,256]{2,1,0:T(8,128)(2,1)}), bf16[8,32,256]{2,1,0:T(8,128)(2,1)S(1)}, u32[]{:S(2)}, u32[]{:S(2)}) async-start(bf16[8,32,256]{2,1,0:T(8,128)(2,1)} %broadcast_in_dim.12), calls=%async_computation | async-start | bytes 262144 | tf_op jit(solution)/shard_map/all_to_all | solution.py:30
  26.4 4.3 %copy-start.1 = (bf16[32,256]{1,0:T(8,128)(2,1)S(1)}, bf16[32,256]{1,0:T(8,128)(2,1)}, u32[]{:S(2)}) copy-start(bf16[32,256]{1,0:T(8,128)(2,1)} %near_ref.1) | copy-start | bytes 49156
  26.4 17.5 %copy-start = (bf16[1,1,4,256,256]{4,3,2,1,0:T(8,128)(2,1)S(1)}, bf16[1,1,4,256,256]{4,3,2,1,0:T(8,128)(2,1)}, u32[]{:S(2)}) copy-start(bf16[1,1,4,256,256]{4,3,2,1,0:T(8,128)(2,1)} %param.4) | copy-start | bytes 1572868
  26.4 17.5 %all-to-all-start.1 = ((bf16[4,264,256]{2,1,0:T(8,128)(2,1)}), bf16[4,264,256]{2,1,0:T(8,128)(2,1)S(1)}, u32[]{:S(2)}, u32[]{:S(2)}) async-start(bf16[4,264,256]{2,1,0:T(8,128)(2,1)} %shard_map.67), calls=%async_computation.1 | async-start | bytes 1081344 | tf_op jit(solution)/shard_map/all_to_all | solution.py:30
  30.7 13.2 %collective-permute-start = (bf16[32,256]{1,0:T(8,128)(2,1)S(1)}, bf16[32,256]{1,0:T(8,128)(2,1)S(1)}, u32[]{:S(2)}, u32[]{:S(2)}) collective-permute-start(bf16[32,256]{1,0:T(8,128)(2,1)S(1)} %copy-done.1), channel_id=1, source_target_pairs={{0,8},{8,0},{1,9},{9,1},{2,10},{10,2},{3,11},{11,3},{4,12},{12,4},... | collective-permute-start | bytes 49160 | tf_op jit(solution)/shard_map/ppermute | solution.py:48
  38.6 0.7 copy-start.4
  74.9 17.3 %all-to-all-start.4 = ((bf16[8,32,256]{2,1,0:T(8,128)(2,1)}), bf16[8,32,256]{2,1,0:T(8,128)(2,1)S(1)}, u32[]{:S(2)}, u32[]{:S(2)}) async-start(bf16[8,32,256]{2,1,0:T(8,128)(2,1)} %shard_map.70), calls=%async_computation.4 | async-start | bytes 262144 | tf_op jit(solution)/shard_map/all_to_all | solution.py:30
  79.0 13.2 %collective-permute-start.1 = (bf16[32,256]{1,0:T(8,128)(2,1)S(1)}, bf16[32,256]{1,0:T(8,128)(2,1)S(1)}, u32[]{:S(2)}, u32[]{:S(2)}) collective-permute-start(bf16[32,256]{1,0:T(8,128)(2,1)S(1)} %get-tuple-element.17), channel_id=1, source_target_pairs={{0,8},{8,0},{1,9},{9,1},{2,10},{10,2},{3,11},{11,3},{4,12},{12,4},... | collective-permute-start | bytes 49160 | tf_op jit(solution)/shard_map/ppermute | solution.py:48
  93.1 20.0 %all-to-all-start.5 = ((bf16[8,40,256]{2,1,0:T(8,128)(2,1)}), bf16[8,40,256]{2,1,0:T(8,128)(2,1)S(1)}, u32[]{:S(2)}, u32[]{:S(2)}) async-start(bf16[8,40,256]{2,1,0:T(8,128)(2,1)} %get-tuple-element.19), calls=%async_computation.5 | async-start | bytes 327680 | tf_op jit(solution)/shard_map/all_to_all | solution.py:30
  113.9 16.7 %all-to-all-start.6 = ((bf16[4,136,256]{2,1,0:T(8,128)(2,1)}), bf16[4,136,256]{2,1,0:T(8,128)(2,1)S(1)}, u32[]{:S(2)}, u32[]{:S(2)}) async-start(bf16[4,136,256]{2,1,0:T(8,128)(2,1)} %shard_map.72), calls=%async_computation.6 | async-start | bytes 557056 | tf_op jit(solution)/shard_map/all_to_all | solution.py:30
  117.4 13.3 %collective-permute-start.2 = (bf16[32,256]{1,0:T(8,128)(2,1)S(1)}, bf16[32,256]{1,0:T(8,128)(2,1)S(1)}, u32[]{:S(2)}, u32[]{:S(2)}) collective-permute-start(bf16[32,256]{1,0:T(8,128)(2,1)S(1)} %get-tuple-element.20.own_ref.near_ref), channel_id=1, source_target_pairs={{0,8},{8,0},{1,9},{9,1},{2,10},{10,2},{3,11},{11,3},{4,12},{12,4},... | collective-permute-start | bytes 49160 | tf_op jit(solution)/shard_map/ppermute | solution.py:48
  151.3 13.3 %collective-permute-start.3 = (bf16[48,256]{1,0:T(8,128)(2,1)S(1)}, bf16[48,256]{1,0:T(8,128)(2,1)S(1)}, u32[]{:S(2)}, u32[]{:S(2)}) collective-permute-start(bf16[48,256]{1,0:T(8,128)(2,1)S(1)} %get-tuple-element.21.sent_ref), channel_id=1, source_target_pairs={{0,8},{8,0},{1,9},{9,1},{2,10},{10,2},{3,11},{11,3},{4,12},{12,4},... | collective-permute-start | bytes 73736 | tf_op jit(solution)/shard_map/ppermute | solution.py:48
  159.2 12.6 %all-to-all-start.8 = ((bf16[4,256,256]{2,1,0:T(8,128)(2,1)}), bf16[4,256,256]{2,1,0:T(8,128)(2,1)S(1)}, u32[]{:S(2)}, u32[]{:S(2)}) async-start(bf16[4,256,256]{2,1,0:T(8,128)(2,1)} %get-tuple-element.24), calls=%async_computation.8 | async-start | bytes 1048576 | tf_op jit(solution)/shard_map/all_to_all | solution.py:30
  172.5 14.0 %all-to-all-start.9 = ((bf16[8,40,256]{2,1,0:T(8,128)(2,1)}), bf16[8,40,256]{2,1,0:T(8,128)(2,1)S(1)}, u32[]{:S(2)}, u32[]{:S(2)}) async-start(bf16[8,40,256]{2,1,0:T(8,128)(2,1)} %shard_map.76), calls=%async_computation.9 | async-start | bytes 327680 | tf_op jit(solution)/shard_map/all_to_all | solution.py:30
  176.3 0.6 copy-start.2
  187.2 15.9 %all-to-all-start.10 = ((bf16[32,8,256]{2,1,0:T(8,128)(2,1)}), bf16[32,8,256]{2,1,0:T(8,128)(2,1)S(1)}, u32[]{:S(2)}, u32[]{:S(2)}) async-start(bf16[32,8,256]{2,1,0:T(8,128)(2,1)} %get-tuple-element.25), calls=%async_computation.10 | async-start | bytes 262144 | tf_op jit(solution)/shard_map/all_to_all | solution.py:30

commit v9 on v8

--- a/solution.py
+++ b/solution.py
@@ -178,6 +178,11 @@
         store_bits(far_ref, (pl.ds(vectors + ROWS, ROWS),), pack(form))
     for k in range(y_count):
         out_ref[k] = jnp.zeros(out_ref.shape[1:], BF16)
+    if extra:
+        for t in range(tiles):
+            _, y = parted(pair_ref[0, tiles + t], y_count)
+            out_ref[y, pl.ds(t * vectors, vectors)] = sums_ref[t].astype(BF16)
+        return
     slots = []
     for t in range(tiles):
         j = pair_ref[0, tiles + t]
@@ -199,24 +204,27 @@
         store_bits(send_ref, (z, pl.ds(image.shape[0], ROWS)), gram)
 
 
-def sum_over_y(mirror_ref, send_ref, vectors):
+def first_middle_kernel(mirror_ref, send_ref):
+    vectors = send_ref.shape[1]
     for z in range(send_ref.shape[0]):
         rows = pl.ds(z * vectors, vectors)
         total = mirror_ref[0, rows].astype(F32)
         for y in range(1, mirror_ref.shape[0]):
             total = total + mirror_ref[y, rows].astype(F32)
-        send_ref[z, pl.ds(0, vectors)] = total.astype(BF16)
-
-
-def first_middle_kernel(mirror_ref, send_ref):
-    sum_over_y(mirror_ref, send_ref, send_ref.shape[1])
-
-
-def second_middle_kernel(mirror_ref, sent_ref, far_ref, send_ref, *, vectors):
-    sum_over_y(mirror_ref, send_ref, vectors)
+        send_ref[z] = total.astype(BF16)
+
+
+def second_middle_kernel(peer_ref, mirror_ref, sent_ref, far_ref, send_ref, sums_ref):
+    y_count, vectors = (mirror_ref.shape[0], sums_ref.shape[1])
+    sums_ref[...] = jnp.zeros_like(sums_ref)
+    for y in range(y_count):
+        for t in range(mirror_ref.shape[1] // vectors):
+            z, _ = parted(peer_ref[y, t], y_count)
+            sums_ref[z] = sums_ref[z] + mirror_ref[y, pl.ds(t * vectors, vectors)].astype(F32)
     rows = pl.ds(vectors + ROWS, ROWS)
     form = from_bits(sent_ref[rows]) + from_bits(far_ref[rows])
     for z in range(send_ref.shape[0]):
+        send_ref[z, pl.ds(0, vectors)] = sums_ref[z].astype(BF16)
         store_bits(send_ref, (z, pl.ds(vectors, ROWS)), form)
 
 
@@ -277,7 +285,7 @@
     arrived = exchange(send, X_CORE)
     send, own_direct, far = call(
         mirror_kernel,
-        ((y_count, z_count * vectors, size), BF16),
+        ((y_count, (count if extra else z_count) * vectors, size), BF16),
         ((vectors, size), F32),
         ((vectors + 2 * ROWS * extra, size), BF16),
         scratch=[pltpu.VMEM((count, vectors, size), F32)],
@@ -286,8 +294,8 @@
     sent, far = (far, partner(far))
     out = ((z_count, vectors + ROWS * extra, size), BF16)
     if extra:
-        middle = functools.partial(second_middle_kernel, vectors=vectors)
-        mirror = call(middle, out)(mirror, sent, far)[0]
+        scratch = [pltpu.VMEM((z_count, vectors, size), F32)]
+        mirror = call(second_middle_kernel, out, scratch=scratch)(peers, mirror, sent, far)[0]
     else:
         mirror = call(first_middle_kernel, out)(mirror)[0]
     mirror = exchange(mirror, Z_LO)

time: 205 us -> 205 us (level)
  transfers between devices with their start and end apart: 12 -> 12, of which waited for: 9 -> 8; matrix products, arithmetic and copies ran while one was open for 4% -> 4% of each run, Pallas kernels for 0% -> 0%
where the time goes in v9:
time: 205 us; the launch traced here: 204 us
  starting transfers between devices  82.3 us (40%)
  waiting for transfers between devices  54.2 us (26%)
  blocking collectives  48.9 us (24%)
  Pallas kernels  8 us (4%)
  other arithmetic  6.78 us (3%)
  local copies, waits for them, and re-layouts  2.51 us (1%)
    all_to_all x8, starting transfers between devices, exchange(): return lax.all_to_all(parts, axis, 0, 0, tiled=True)  50.8 us
    all_to_all x3, blocking collectives, exchange(): return lax.all_to_all(parts, axis, 0, 0, tiled=True)  48.9 us
    all_to_all x8, waiting for transfers between devices, exchange(): return lax.all_to_all(parts, axis, 0, 0, tiled=True)  38.1 us
    ppermute x4, starting transfers between devices, partner(): return lax.ppermute(value, Z_HI, [(0, 1), (1, 0)])  31.5 us
    ppermute x4, waiting for transfers between devices, partner(): return lax.ppermute(value, Z_HI, [(0, 1), (1, 0)])  16.2 us
    pallas_call x12, Pallas kernels, run(): pl.pallas_call(kernel, out_shape=tuple((out(shape, kind) for shape, kind...  8 us
  transfers between devices with their start and end apart: 12, of which 8 were waited for; matrix products, arithmetic and copies ran while one was open for 4% of the time, Pallas kernels for 0%

profile of v9, /device:TPU:1, one launch (start us, length us, event | category | flops | bytes accessed | tf_op | source)
XLA Modules:
  0.0 204.2 jit_solution(16224695632964184413)
XLA Ops:
  2.0 13.2 %all-to-all-start = ((bf16[8,32,256]{2,1,0:T(8,128)(2,1)}), bf16[8,32,256]{2,1,0:T(8,128)(2,1)S(1)}, u32[]{:S(2)}, u32[]{:S(2)}) async-start(bf16[8,32,256]{2,1,0:T(8,128)(2,1)} %broadcast_in_dim.12), calls=%async_computation | async-start | bytes 262144 | tf_op jit(solution)/shard_map/all_to_all | solution.py:30
  15.2 10.3 %all-to-all-done.by_z_ref = bf16[8,32,256]{2,1,0:T(8,128)(2,1)S(1)} async-done(((bf16[8,32,256]{2,1,0:T(8,128)(2,1)}), bf16[8,32,256]{2,1,0:T(8,128)(2,1)S(1)}, u32[]{:S(2)}, u32[]{:S(2)}) %all-to-all-start) | async-done | bytes 131104 | tf_op jit(solution)/shard_map/all_to_all | solution.py:30
  26.4 4.3 %all-to-all-start.1 = ((bf16[4,264,256]{2,1,0:T(8,128)(2,1)}), bf16[4,264,256]{2,1,0:T(8,128)(2,1)S(1)}, u32[]{:S(2)}, u32[]{:S(2)}) async-start(bf16[4,264,256]{2,1,0:T(8,128)(2,1)} %shard_map.67), calls=%async_computation.1 | async-start | bytes 1081344 | tf_op jit(solution)/shard_map/all_to_all | solution.py:30
  30.7 7.9 %collective-permute-start = (bf16[32,256]{1,0:T(8,128)(2,1)S(1)}, bf16[32,256]{1,0:T(8,128)(2,1)S(1)}, u32[]{:S(2)}, u32[]{:S(2)}) collective-permute-start(bf16[32,256]{1,0:T(8,128)(2,1)S(1)} %copy-done.1), channel_id=1, source_target_pairs={{0,8},{8,0},{1,9},{9,1},{2,10},{10,2},{3,11},{11,3},{4,12},{12,4},... | collective-permute-start | bytes 49160 | tf_op jit(solution)/shard_map/ppermute | solution.py:48
  39.4 4.5 %collective-permute-done.other_ref = bf16[32,256]{1,0:T(8,128)(2,1)S(1)} collective-permute-done((bf16[32,256]{1,0:T(8,128)(2,1)S(1)}, bf16[32,256]{1,0:T(8,128)(2,1)S(1)}, u32[]{:S(2)}, u32[]{:S(2)}) %collective-permute-start) | collective-permute-done | bytes 16416 | tf_op jit(solution)/shard_map/ppermute | solution.py:48
  44.2 17.7 %all_to_all.55.row_ref = bf16[8,128,256]{2,1,0:T(8,128)(2,1)S(1)} all-to-all(bf16[8,128,256]{2,1,0:T(8,128)(2,1)S(1)} %shard_map.68), channel_id=1, replica_groups=mesh['row_0'=8,'row_1'=4,'col_0'=2,'col_1'=4,'col_2'=2] {'col_1','col_2'}, dimensions={0} | all-to-all | bytes 1048576 | tf_op jit(solution)/shard_map/all_to_all | solution.py:30
  62.2 12.0 %all_to_all.56.mirror_ref = bf16[4,256,256]{2,1,0:T(8,128)(2,1)S(1)} all-to-all(bf16[4,256,256]{2,1,0:T(8,128)(2,1)S(1)} %get-tuple-element.18), channel_id=1, replica_groups=mesh['row_0'=8,'row_1'=4,'col_0'=2,'col_1'=4,'col_2'=2] {'row_1'}, dimensions={0} | all-to-all | bytes 1048576 | tf_op jit(solution)/shard_map/all_to_all | solution.py:30
  74.9 4.1 %all-to-all-start.4 = ((bf16[8,32,256]{2,1,0:T(8,128)(2,1)}), bf16[8,32,256]{2,1,0:T(8,128)(2,1)S(1)}, u32[]{:S(2)}, u32[]{:S(2)}) async-start(bf16[8,32,256]{2,1,0:T(8,128)(2,1)} %shard_map.70), calls=%async_computation.4 | async-start | bytes 262144 | tf_op jit(solution)/shard_map/all_to_all | solution.py:30
  79.0 7.8 %collective-permute-start.1 = (bf16[32,256]{1,0:T(8,128)(2,1)S(1)}, bf16[32,256]{1,0:T(8,128)(2,1)S(1)}, u32[]{:S(2)}, u32[]{:S(2)}) collective-permute-start(bf16[32,256]{1,0:T(8,128)(2,1)S(1)} %get-tuple-element.17), channel_id=1, source_target_pairs={{0,8},{8,0},{1,9},{9,1},{2,10},{10,2},{3,11},{11,3},{4,12},{12,4},... | collective-permute-start | bytes 49160 | tf_op jit(solution)/shard_map/ppermute | solution.py:48
  86.9 5.3 %collective-permute-done.1.far_ref = bf16[32,256]{1,0:T(8,128)(2,1)S(1)} collective-permute-done((bf16[32,256]{1,0:T(8,128)(2,1)S(1)}, bf16[32,256]{1,0:T(8,128)(2,1)S(1)}, u32[]{:S(2)}, u32[]{:S(2)}) %collective-permute-start.1) | collective-permute-done | bytes 16416 | tf_op jit(solution)/shard_map/ppermute | solution.py:48
  93.1 9.3 %all-to-all-start.5 = ((bf16[8,40,256]{2,1,0:T(8,128)(2,1)}), bf16[8,40,256]{2,1,0:T(8,128)(2,1)S(1)}, u32[]{:S(2)}, u32[]{:S(2)}) async-start(bf16[8,40,256]{2,1,0:T(8,128)(2,1)} %get-tuple-element.19), calls=%async_computation.5 | async-start | bytes 327680 | tf_op jit(solution)/shard_map/all_to_all | solution.py:30
  102.5 10.6 %all-to-all-done.5.by_z_ref = bf16[8,40,256]{2,1,0:T(8,128)(2,1)S(1)} async-done(((bf16[8,40,256]{2,1,0:T(8,128)(2,1)}), bf16[8,40,256]{2,1,0:T(8,128)(2,1)S(1)}, u32[]{:S(2)}, u32[]{:S(2)}) %all-to-all-start.5) | async-done | bytes 163872 | tf_op jit(solution)/shard_map/all_to_all | solution.py:30
  113.9 3.4 %all-to-all-start.6 = ((bf16[4,136,256]{2,1,0:T(8,128)(2,1)}), bf16[4,136,256]{2,1,0:T(8,128)(2,1)S(1)}, u32[]{:S(2)}, u32[]{:S(2)}) async-start(bf16[4,136,256]{2,1,0:T(8,128)(2,1)} %shard_map.72), calls=%async_computation.6 | async-start | bytes 557056 | tf_op jit(solution)/shard_map/all_to_all | solution.py:30
  117.4 7.9 %collective-permute-start.2 = (bf16[32,256]{1,0:T(8,128)(2,1)S(1)}, bf16[32,256]{1,0:T(8,128)(2,1)S(1)}, u32[]{:S(2)}, u32[]{:S(2)}) collective-permute-start(bf16[32,256]{1,0:T(8,128)(2,1)S(1)} %get-tuple-element.20.own_ref.near_ref), channel_id=1, source_target_pairs={{0,8},{8,0},{1,9},{9,1},{2,10},{10,2},{3,11},{11,3},{4,12},{12,4},... | collective-permute-start | bytes 49160 | tf_op jit(solution)/shard_map/ppermute | solution.py:48
  125.3 5.4 %collective-permute-done.2.other_ref = bf16[32,256]{1,0:T(8,128)(2,1)S(1)} collective-permute-done((bf16[32,256]{1,0:T(8,128)(2,1)S(1)}, bf16[32,256]{1,0:T(8,128)(2,1)S(1)}, u32[]{:S(2)}, u32[]{:S(2)}) %collective-permute-start.2) | collective-permute-done | bytes 16416 | tf_op jit(solution)/shard_map/ppermute | solution.py:48
  131.0 19.2 %all_to_all.57.row_ref = bf16[8,136,256]{2,1,0:T(8,128)(2,1)S(1)} all-to-all(bf16[8,136,256]{2,1,0:T(8,128)(2,1)S(1)} %shard_map.73), channel_id=1, replica_groups=mesh['row_0'=8,'row_1'=4,'col_0'=2,'col_1'=4,'col_2'=2] {'col_1','col_2'}, dimensions={0} | all-to-all | bytes 1114112 | tf_op jit(solution)/shard_map/all_to_all | solution.py:30
  151.2 7.8 %collective-permute-start.3 = (bf16[48,256]{1,0:T(8,128)(2,1)S(1)}, bf16[48,256]{1,0:T(8,128)(2,1)S(1)}, u32[]{:S(2)}, u32[]{:S(2)}) collective-permute-start(bf16[48,256]{1,0:T(8,128)(2,1)S(1)} %get-tuple-element.21.sent_ref), channel_id=1, source_target_pairs={{0,8},{8,0},{1,9},{9,1},{2,10},{10,2},{3,11},{11,3},{4,12},{12,4},... | collective-permute-start | bytes 73736 | tf_op jit(solution)/shard_map/ppermute | solution.py:48
  159.1 4.5 %all-to-all-start.8 = ((bf16[4,128,256]{2,1,0:T(8,128)(2,1)}), bf16[4,128,256]{2,1,0:T(8,128)(2,1)S(1)}, u32[]{:S(2)}, u32[]{:S(2)}) async-start(bf16[4,128,256]{2,1,0:T(8,128)(2,1)} %get-tuple-element.24), calls=%async_computation.8 | async-start | bytes 524288 | tf_op jit(solution)/shard_map/all_to_all | solution.py:30
  164.6 2.9 %cholesky.17 = f32[32,32]{1,0:T(8,128)S(1)} custom-call(f32[32,32]{1,0:T(8,128)S(1)} %fusion.3), custom_call_target="Cholesky" | custom-call | tf_op jit(solution)/shard_map/jit(cholesky)/cholesky | solution.py:333
  168.9 2.4 %custom-call.6 = f32[1,32,32]{1,2,0:T(8,128)S(1)} custom-call(f32[1,32,32]{2,1,0:T(8,128)S(1)} %fusion), custom_call_target="InvertDiagBlocksLowerTriangular" | custom-call | tf_op jit(solution)/shard_map/triangular_solve | solution.py:334
  172.2 3.4 %all-to-all-start.9 = ((bf16[8,40,256]{2,1,0:T(8,128)(2,1)}), bf16[8,40,256]{2,1,0:T(8,128)(2,1)S(1)}, u32[]{:S(2)}, u32[]{:S(2)}) async-start(bf16[8,40,256]{2,1,0:T(8,128)(2,1)} %shard_map.76), calls=%async_computation.9 | async-start | bytes 327680 | tf_op jit(solution)/shard_map/all_to_all | solution.py:30
  176.6 9.7 %all-to-all-done.9.mirror_ref = bf16[8,40,256]{2,1,0:T(8,128)(2,1)S(1)} async-done(((bf16[8,40,256]{2,1,0:T(8,128)(2,1)}), bf16[8,40,256]{2,1,0:T(8,128)(2,1)S(1)}, u32[]{:S(2)}, u32[]{:S(2)}) %all-to-all-start.9) | async-done | bytes 163872 | tf_op jit(solution)/shard_map/all_to_all | solution.py:30
  187.0 8.5 %all-to-all-start.10 = ((bf16[32,8,256]{2,1,0:T(8,128)(2,1)}), bf16[32,8,256]{2,1,0:T(8,128)(2,1)S(1)}, u32[]{:S(2)}, u32[]{:S(2)}) async-start(bf16[32,8,256]{2,1,0:T(8,128)(2,1)} %get-tuple-element.25), calls=%async_computation.10 | async-start | bytes 262144 | tf_op jit(solution)/shard_map/all_to_all | solution.py:30
  195.7 7.4 %all-to-all-done.10.bits_ref = bf16[32,8,256]{2,1,0:T(8,128)(2,1)S(1)} async-done(((bf16[32,8,256]{2,1,0:T(8,128)(2,1)}), bf16[32,8,256]{2,1,0:T(8,128)(2,1)S(1)}, u32[]{:S(2)}, u32[]{:S(2)}) %all-to-all-start.10) | async-done | bytes 131104 | tf_op jit(solution)/shard_map/all_to_all | solution.py:30
  (43 shorter events, 13.6 us)
Async XLA Ops:
  2.0 13.2 %copy-start.3 = (s32[1,1,4]{2,1,0:T(1,128)S(1)}, s32[1,1,4]{2,1,0:T(1,128)}, u32[]{:S(2)}) copy-start(s32[1,1,4]{2,1,0:T(1,128)} %param.6) | copy-start | bytes 52
  2.0 23.5 %all-to-all-start = ((bf16[8,32,256]{2,1,0:T(8,128)(2,1)}), bf16[8,32,256]{2,1,0:T(8,128)(2,1)S(1)}, u32[]{:S(2)}, u32[]{:S(2)}) async-start(bf16[8,32,256]{2,1,0:T(8,128)(2,1)} %broadcast_in_dim.12), calls=%async_computation | async-start | bytes 262144 | tf_op jit(solution)/shard_map/all_to_all | solution.py:30
  26.4 4.3 %copy-start.1 = (bf16[32,256]{1,0:T(8,128)(2,1)S(1)}, bf16[32,256]{1,0:T(8,128)(2,1)}, u32[]{:S(2)}) copy-start(bf16[32,256]{1,0:T(8,128)(2,1)} %near_ref.1) | copy-start | bytes 49156
  26.4 17.5 %copy-start = (bf16[1,1,4,256,256]{4,3,2,1,0:T(8,128)(2,1)S(1)}, bf16[1,1,4,256,256]{4,3,2,1,0:T(8,128)(2,1)}, u32[]{:S(2)}) copy-start(bf16[1,1,4,256,256]{4,3,2,1,0:T(8,128)(2,1)} %param.4) | copy-start | bytes 1572868
  26.4 17.5 %all-to-all-start.1 = ((bf16[4,264,256]{2,1,0:T(8,128)(2,1)}), bf16[4,264,256]{2,1,0:T(8,128)(2,1)S(1)}, u32[]{:S(2)}, u32[]{:S(2)}) async-start(bf16[4,264,256]{2,1,0:T(8,128)(2,1)} %shard_map.67), calls=%async_computation.1 | async-start | bytes 1081344 | tf_op jit(solution)/shard_map/all_to_all | solution.py:30
  30.7 13.2 %collective-permute-start = (bf16[32,256]{1,0:T(8,128)(2,1)S(1)}, bf16[32,256]{1,0:T(8,128)(2,1)S(1)}, u32[]{:S(2)}, u32[]{:S(2)}) collective-permute-start(bf16[32,256]{1,0:T(8,128)(2,1)S(1)} %copy-done.1), channel_id=1, source_target_pairs={{0,8},{8,0},{1,9},{9,1},{2,10},{10,2},{3,11},{11,3},{4,12},{12,4},... | collective-permute-start | bytes 49160 | tf_op jit(solution)/shard_map/ppermute | solution.py:48
  38.6 0.7 copy-start.4
  74.9 17.3 %all-to-all-start.4 = ((bf16[8,32,256]{2,1,0:T(8,128)(2,1)}), bf16[8,32,256]{2,1,0:T(8,128)(2,1)S(1)}, u32[]{:S(2)}, u32[]{:S(2)}) async-start(bf16[8,32,256]{2,1,0:T(8,128)(2,1)} %shard_map.70), calls=%async_computation.4 | async-start | bytes 262144 | tf_op jit(solution)/shard_map/all_to_all | solution.py:30
  79.0 13.2 %collective-permute-start.1 = (bf16[32,256]{1,0:T(8,128)(2,1)S(1)}, bf16[32,256]{1,0:T(8,128)(2,1)S(1)}, u32[]{:S(2)}, u32[]{:S(2)}) collective-permute-start(bf16[32,256]{1,0:T(8,128)(2,1)S(1)} %get-tuple-element.17), channel_id=1, source_target_pairs={{0,8},{8,0},{1,9},{9,1},{2,10},{10,2},{3,11},{11,3},{4,12},{12,4},... | collective-permute-start | bytes 49160 | tf_op jit(solution)/shard_map/ppermute | solution.py:48
  93.1 20.0 %all-to-all-start.5 = ((bf16[8,40,256]{2,1,0:T(8,128)(2,1)}), bf16[8,40,256]{2,1,0:T(8,128)(2,1)S(1)}, u32[]{:S(2)}, u32[]{:S(2)}) async-start(bf16[8,40,256]{2,1,0:T(8,128)(2,1)} %get-tuple-element.19), calls=%async_computation.5 | async-start | bytes 327680 | tf_op jit(solution)/shard_map/all_to_all | solution.py:30
  113.9 16.7 %all-to-all-start.6 = ((bf16[4,136,256]{2,1,0:T(8,128)(2,1)}), bf16[4,136,256]{2,1,0:T(8,128)(2,1)S(1)}, u32[]{:S(2)}, u32[]{:S(2)}) async-start(bf16[4,136,256]{2,1,0:T(8,128)(2,1)} %shard_map.72), calls=%async_computation.6 | async-start | bytes 557056 | tf_op jit(solution)/shard_map/all_to_all | solution.py:30
  117.4 13.3 %collective-permute-start.2 = (bf16[32,256]{1,0:T(8,128)(2,1)S(1)}, bf16[32,256]{1,0:T(8,128)(2,1)S(1)}, u32[]{:S(2)}, u32[]{:S(2)}) collective-permute-start(bf16[32,256]{1,0:T(8,128)(2,1)S(1)} %get-tuple-element.20.own_ref.near_ref), channel_id=1, source_target_pairs={{0,8},{8,0},{1,9},{9,1},{2,10},{10,2},{3,11},{11,3},{4,12},{12,4},... | collective-permute-start | bytes 49160 | tf_op jit(solution)/shard_map/ppermute | solution.py:48
  151.2 13.3 %collective-permute-start.3 = (bf16[48,256]{1,0:T(8,128)(2,1)S(1)}, bf16[48,256]{1,0:T(8,128)(2,1)S(1)}, u32[]{:S(2)}, u32[]{:S(2)}) collective-permute-start(bf16[48,256]{1,0:T(8,128)(2,1)S(1)} %get-tuple-element.21.sent_ref), channel_id=1, source_target_pairs={{0,8},{8,0},{1,9},{9,1},{2,10},{10,2},{3,11},{11,3},{4,12},{12,4},... | collective-permute-start | bytes 73736 | tf_op jit(solution)/shard_map/ppermute | solution.py:48
  159.1 12.3 %all-to-all-start.8 = ((bf16[4,128,256]{2,1,0:T(8,128)(2,1)}), bf16[4,128,256]{2,1,0:T(8,128)(2,1)S(1)}, u32[]{:S(2)}, u32[]{:S(2)}) async-start(bf16[4,128,256]{2,1,0:T(8,128)(2,1)} %get-tuple-element.24), calls=%async_computation.8 | async-start | bytes 524288 | tf_op jit(solution)/shard_map/all_to_all | solution.py:30
  172.2 14.1 %all-to-all-start.9 = ((bf16[8,40,256]{2,1,0:T(8,128)(2,1)}), bf16[8,40,256]{2,1,0:T(8,128)(2,1)S(1)}, u32[]{:S(2)}, u32[]{:S(2)}) async-start(bf16[8,40,256]{2,1,0:T(8,128)(2,1)} %shard_map.76), calls=%async_computation.9 | async-start | bytes 327680 | tf_op jit(solution)/shard_map/all_to_all | solution.py:30
  176.0 0.6 copy-start.2
  187.0 16.2 %all-to-all-start.10 = ((bf16[32,8,256]{2,1,0:T(8,128)(2,1)}), bf16[32,8,256]{2,1,0:T(8,128)(2,1)S(1)}, u32[]{:S(2)}, u32[]{:S(2)}) async-start(bf16[32,8,256]{2,1,0:T(8,128)(2,1)} %get-tuple-element.25), calls=%async_computation.10 | async-start | bytes 262144 | tf_op jit(solution)/shard_map/all_to_all | solution.py:30

commit v10 on v9

--- a/solution.py
+++ b/solution.py
@@ -214,48 +214,46 @@
         send_ref[z] = total.astype(BF16)
 
 
-def second_middle_kernel(peer_ref, mirror_ref, sent_ref, far_ref, send_ref, sums_ref):
+def form_kernel(sent_ref, far_ref, send_ref, gram_ref, *, rows):
+    vectors = gram_ref.shape[0]
+    place = pl.ds(vectors, ROWS)
+    gram_ref[...] = unpack(from_bits(sent_ref[place]) + from_bits(far_ref[place])) * (1.0 / rows)
+    place = pl.ds(vectors + ROWS, ROWS)
+    form = from_bits(sent_ref[place]) + from_bits(far_ref[place])
+    for k in range(send_ref.shape[0]):
+        store_bits(send_ref, (k, pl.ds(0, ROWS)), form)
+
+
+def second_middle_kernel(peer_ref, mirror_ref, bits_ref, send_ref, sums_ref):
     y_count, vectors = (mirror_ref.shape[0], sums_ref.shape[1])
     sums_ref[...] = jnp.zeros_like(sums_ref)
     for y in range(y_count):
         for t in range(mirror_ref.shape[1] // vectors):
             z, _ = parted(peer_ref[y, t], y_count)
             sums_ref[z] = sums_ref[z] + mirror_ref[y, pl.ds(t * vectors, vectors)].astype(F32)
-    rows = pl.ds(vectors + ROWS, ROWS)
-    form = from_bits(sent_ref[rows]) + from_bits(far_ref[rows])
+    form = jnp.zeros((ROWS, LANES), F32)
+    for k in range(bits_ref.shape[0]):
+        form += from_bits(bits_ref[k])
     for z in range(send_ref.shape[0]):
         send_ref[z, pl.ds(0, vectors)] = sums_ref[z].astype(BF16)
         store_bits(send_ref, (z, pl.ds(vectors, ROWS)), form)
 
 
-def gram_kernel(sent_ref, far_ref, gram_ref, *, rows):
-    place = pl.ds(gram_ref.shape[0], ROWS)
-    both = from_bits(sent_ref[place]) + from_bits(far_ref[place])
-    gram_ref[...] = unpack(both) * (1.0 / rows)
-
-
-def last_kernel(direct_ref, far_ref, mirror_ref, image_ref, send_ref):
-    vectors = image_ref.shape[0]
+def finish_kernel(
+    mirror_ref, direct_ref, far_ref, inverse_ref, turned_ref, residual_ref, projected_ref, *, rows
+):
+    vectors = inverse_ref.shape[0]
     form = jnp.zeros((ROWS, LANES), F32)
+    image = direct_ref[...] + far_ref[pl.ds(0, vectors)].astype(F32)
     for z in range(mirror_ref.shape[0]):
         form += from_bits(mirror_ref[z, pl.ds(vectors, ROWS)])
-    for k in range(send_ref.shape[0]):
-        store_bits(send_ref, (k, pl.ds(0, ROWS)), form)
-    image = direct_ref[...] + far_ref[pl.ds(0, vectors)].astype(F32)
-    for z in range(mirror_ref.shape[0]):
         image = image + mirror_ref[z, pl.ds(0, vectors)].astype(F32)
-    image_ref[...] = image
-
-
-def finish_kernel(bits_ref, inverse_ref, ritz_ref, last_ref, residual_ref, projected_ref, *, rows):
-    form = jnp.zeros((ROWS, LANES), F32)
-    for k in range(bits_ref.shape[0]):
-        form += from_bits(bits_ref[k])
     form = unpack(form)
     inverse = inverse_ref[...]
+    last_image = dot(inverse, image, 1, 0)
     half = dot(inverse, (form + form.T) * (1.0 / rows), 1, 0)
     projected_ref[...] = dot(half, inverse, 1, 1)
-    residual_ref[...] = last_ref[...] - dot(half, ritz_ref[...], 1, 0)
+    residual_ref[...] = last_image - dot(half, turned_ref[...], 1, 0)
 
 
 def product(pairs, tiles, current, send_z, note, peers):
@@ -292,14 +290,23 @@
     )(pairs, arrived, tiles, current, other)
     mirror = exchange(send, Y)
     sent, far = (far, partner(far))
-    out = ((z_count, vectors + ROWS * extra, size), BF16)
-    if extra:
-        scratch = [pltpu.VMEM((z_count, vectors, size), F32)]
-        mirror = call(second_middle_kernel, out, scratch=scratch)(peers, mirror, sent, far)[0]
+    if extra:
+        form, gram = call(
+            functools.partial(form_kernel, rows=size * lax.axis_size(COL_ROW)),
+            ((lax.axis_size(Y_X_CORE), ROWS, 2 * LANES), BF16),
+            ((vectors, vectors), F32),
+        )(sent, far)
+        form = exchange(form, Y_X_CORE)
+        mirror = call(
+            second_middle_kernel,
+            ((z_count, vectors + ROWS, size), BF16),
+            scratch=[pltpu.VMEM((z_count, vectors, size), F32)],
+        )(peers, mirror, form)[0]
     else:
-        mirror = call(first_middle_kernel, out)(mirror)[0]
+        mirror = call(first_middle_kernel, ((z_count, vectors, size), BF16))(mirror)[0]
+        gram = None
     mirror = exchange(mirror, Z_LO)
-    return own_direct, sent, far, mirror, peers
+    return own_direct, far, mirror, gram, peers
 
 
 def steps(tile_values, tile_row, tile_col, basis_init):
@@ -313,36 +320,26 @@
     note = jnp.pad(
         tile_col[0].astype(BF16), [(0, ROWS - 1), (0, size - tiles.shape[0])]
     )
-    own_direct, _, far, mirror, peers = product(pairs, tiles, basis_init, None, note, None)
+    own_direct, far, mirror, _, peers = product(pairs, tiles, basis_init, None, note, None)
     image, current, send = call(
         image_kernel,
         ((vectors, size), F32),
         ((vectors, size), BF16),
         ((mirror.shape[0], vectors + ROWS, size), BF16),
     )(own_direct, far, mirror)
-    own_direct, sent, far, mirror, _ = product(pairs, tiles, current, send, None, peers)
-    raw_image, send = call(
-        last_kernel,
-        ((vectors, size), F32),
-        ((lax.axis_size(Y_X_CORE), ROWS, 2 * LANES), BF16),
-    )(own_direct, far, mirror)
-    form = exchange(send, Y_X_CORE)
-    gram = call(
-        functools.partial(gram_kernel, rows=total_rows), ((vectors, vectors), F32)
-    )(sent, far)[0]
+    own_direct, far, mirror, gram, _ = product(pairs, tiles, current, send, None, peers)
     factor = jnp.linalg.cholesky(gram)
     inverse = lax.linalg.triangular_solve(
         factor, jnp.eye(vectors, dtype=F32), left_side=True, lower=True
     )
     ritz_basis = jnp.dot(inverse, image, precision=HIGHEST)
-    last_image = jnp.dot(inverse, raw_image, precision=HIGHEST)
     turned = jnp.dot(inverse.T, ritz_basis, precision=HIGHEST)
     residual, projected = call(
         functools.partial(finish_kernel, rows=total_rows),
         ((vectors, size), F32),
         ((vectors, vectors), F32),
         out=jax.ShapeDtypeStruct,
-    )(form, inverse, turned, last_image)
+    )(mirror, own_direct, far, inverse, turned)
     return (ritz_basis, residual, projected)
 
 

time: 205 us -> 208 us (1.015)
  waiting for transfers between devices: 54.2 us -> 58 us
  starting transfers between devices: 82.3 us -> 79.9 us
    ppermute x4, waiting for transfers between devices: 16.2 us -> 20.6 us  [partner(): return lax.ppermute(value, Z_HI, [(0, 1), (1, 0)])]
    all_to_all x8, starting transfers between devices: 50.8 us -> 48.4 us  [exchange(): return lax.all_to_all(parts, axis, 0, 0, tiled=True)]
    pallas_call x12 -> x11, Pallas kernels: 8 us -> 7.89 us  [run(): pl.pallas_call(kernel, out_shape=tuple((out(shape, kind) for shape, kind...]
  transfers between devices with their start and end apart: 12 -> 12, of which waited for: 8 -> 9; matrix products, arithmetic and copies ran while one was open for 4% -> 4% of each run, Pallas kernels for 0% -> 0%
where the time goes in v10:
time: 208 us; the launch traced here: 205 us
  starting transfers between devices  79.9 us (38%)
  waiting for transfers between devices  58 us (28%)
  blocking collectives  48.9 us (24%)
  Pallas kernels  7.89 us (4%)
  other arithmetic  6.78 us (3%)
  local copies, waits for them, and re-layouts  2.5 us (1%)
    all_to_all x3, blocking collectives, exchange(): return lax.all_to_all(parts, axis, 0, 0, tiled=True)  48.9 us
    all_to_all x8, starting transfers between devices, exchange(): return lax.all_to_all(parts, axis, 0, 0, tiled=True)  48.4 us
    all_to_all x8, waiting for transfers between devices, exchange(): return lax.all_to_all(parts, axis, 0, 0, tiled=True)  37.4 us
    ppermute x4, starting transfers between devices, partner(): return lax.ppermute(value, Z_HI, [(0, 1), (1, 0)])  31.5 us
    ppermute x4, waiting for transfers between devices, partner(): return lax.ppermute(value, Z_HI, [(0, 1), (1, 0)])  20.6 us
    pallas_call x11, Pallas kernels, run(): pl.pallas_call(kernel, out_shape=tuple((out(shape, kind) for shape, kind...  7.89 us
  transfers between devices with their start and end apart: 12, of which 9 were waited for; matrix products, arithmetic and copies ran while one was open for 4% of the time, Pallas kernels for 0%

profile of v10, /device:TPU:1, one launch (start us, length us, event | category | flops | bytes accessed | tf_op | source)
XLA Modules:
  0.0 205.4 jit_solution(13031405715438825114)
XLA Ops:
  2.0 13.2 %all-to-all-start = ((bf16[8,32,256]{2,1,0:T(8,128)(2,1)}), bf16[8,32,256]{2,1,0:T(8,128)(2,1)S(1)}, u32[]{:S(2)}, u32[]{:S(2)}) async-start(bf16[8,32,256]{2,1,0:T(8,128)(2,1)} %broadcast_in_dim.12), calls=%async_computation | async-start | bytes 262144 | tf_op jit(solution)/shard_map/all_to_all | solution.py:30
  15.2 10.3 %all-to-all-done.by_z_ref = bf16[8,32,256]{2,1,0:T(8,128)(2,1)S(1)} async-done(((bf16[8,32,256]{2,1,0:T(8,128)(2,1)}), bf16[8,32,256]{2,1,0:T(8,128)(2,1)S(1)}, u32[]{:S(2)}, u32[]{:S(2)}) %all-to-all-start) | async-done | bytes 131104 | tf_op jit(solution)/shard_map/all_to_all | solution.py:30
  26.4 4.3 %all-to-all-start.1 = ((bf16[4,264,256]{2,1,0:T(8,128)(2,1)}), bf16[4,264,256]{2,1,0:T(8,128)(2,1)S(1)}, u32[]{:S(2)}, u32[]{:S(2)}) async-start(bf16[4,264,256]{2,1,0:T(8,128)(2,1)} %shard_map.67), calls=%async_computation.1 | async-start | bytes 1081344 | tf_op jit(solution)/shard_map/all_to_all | solution.py:30
  30.7 7.9 %collective-permute-start = (bf16[32,256]{1,0:T(8,128)(2,1)S(1)}, bf16[32,256]{1,0:T(8,128)(2,1)S(1)}, u32[]{:S(2)}, u32[]{:S(2)}) collective-permute-start(bf16[32,256]{1,0:T(8,128)(2,1)S(1)} %copy-done.1), channel_id=1, source_target_pairs={{0,8},{8,0},{1,9},{9,1},{2,10},{10,2},{3,11},{11,3},{4,12},{12,4},... | collective-permute-start | bytes 49160 | tf_op jit(solution)/shard_map/ppermute | solution.py:48
  39.4 4.5 %collective-permute-done.other_ref = bf16[32,256]{1,0:T(8,128)(2,1)S(1)} collective-permute-done((bf16[32,256]{1,0:T(8,128)(2,1)S(1)}, bf16[32,256]{1,0:T(8,128)(2,1)S(1)}, u32[]{:S(2)}, u32[]{:S(2)}) %collective-permute-start) | collective-permute-done | bytes 16416 | tf_op jit(solution)/shard_map/ppermute | solution.py:48
  44.2 17.7 %all_to_all.55.row_ref = bf16[8,128,256]{2,1,0:T(8,128)(2,1)S(1)} all-to-all(bf16[8,128,256]{2,1,0:T(8,128)(2,1)S(1)} %shard_map.68), channel_id=1, replica_groups=mesh['row_0'=8,'row_1'=4,'col_0'=2,'col_1'=4,'col_2'=2] {'col_1','col_2'}, dimensions={0} | all-to-all | bytes 1048576 | tf_op jit(solution)/shard_map/all_to_all | solution.py:30
  62.2 12.0 %all_to_all.56.mirror_ref = bf16[4,256,256]{2,1,0:T(8,128)(2,1)S(1)} all-to-all(bf16[4,256,256]{2,1,0:T(8,128)(2,1)S(1)} %get-tuple-element.18), channel_id=1, replica_groups=mesh['row_0'=8,'row_1'=4,'col_0'=2,'col_1'=4,'col_2'=2] {'row_1'}, dimensions={0} | all-to-all | bytes 1048576 | tf_op jit(solution)/shard_map/all_to_all | solution.py:30
  74.9 4.1 %all-to-all-start.4 = ((bf16[8,32,256]{2,1,0:T(8,128)(2,1)}), bf16[8,32,256]{2,1,0:T(8,128)(2,1)S(1)}, u32[]{:S(2)}, u32[]{:S(2)}) async-start(bf16[8,32,256]{2,1,0:T(8,128)(2,1)} %shard_map.70), calls=%async_computation.4 | async-start | bytes 262144 | tf_op jit(solution)/shard_map/all_to_all | solution.py:30
  79.0 7.8 %collective-permute-start.1 = (bf16[32,256]{1,0:T(8,128)(2,1)S(1)}, bf16[32,256]{1,0:T(8,128)(2,1)S(1)}, u32[]{:S(2)}, u32[]{:S(2)}) collective-permute-start(bf16[32,256]{1,0:T(8,128)(2,1)S(1)} %get-tuple-element.17), channel_id=1, source_target_pairs={{0,8},{8,0},{1,9},{9,1},{2,10},{10,2},{3,11},{11,3},{4,12},{12,4},... | collective-permute-start | bytes 49160 | tf_op jit(solution)/shard_map/ppermute | solution.py:48
  86.9 5.3 %collective-permute-done.1.far_ref = bf16[32,256]{1,0:T(8,128)(2,1)S(1)} collective-permute-done((bf16[32,256]{1,0:T(8,128)(2,1)S(1)}, bf16[32,256]{1,0:T(8,128)(2,1)S(1)}, u32[]{:S(2)}, u32[]{:S(2)}) %collective-permute-start.1) | collective-permute-done | bytes 16416 | tf_op jit(solution)/shard_map/ppermute | solution.py:48
  93.1 9.3 %all-to-all-start.5 = ((bf16[8,40,256]{2,1,0:T(8,128)(2,1)}), bf16[8,40,256]{2,1,0:T(8,128)(2,1)S(1)}, u32[]{:S(2)}, u32[]{:S(2)}) async-start(bf16[8,40,256]{2,1,0:T(8,128)(2,1)} %get-tuple-element.19), calls=%async_computation.5 | async-start | bytes 327680 | tf_op jit(solution)/shard_map/all_to_all | solution.py:30
  102.5 10.6 %all-to-all-done.5.by_z_ref = bf16[8,40,256]{2,1,0:T(8,128)(2,1)S(1)} async-done(((bf16[8,40,256]{2,1,0:T(8,128)(2,1)}), bf16[8,40,256]{2,1,0:T(8,128)(2,1)S(1)}, u32[]{:S(2)}, u32[]{:S(2)}) %all-to-all-start.5) | async-done | bytes 163872 | tf_op jit(solution)/shard_map/all_to_all | solution.py:30
  113.9 3.4 %all-to-all-start.6 = ((bf16[4,136,256]{2,1,0:T(8,128)(2,1)}), bf16[4,136,256]{2,1,0:T(8,128)(2,1)S(1)}, u32[]{:S(2)}, u32[]{:S(2)}) async-start(bf16[4,136,256]{2,1,0:T(8,128)(2,1)} %shard_map.72), calls=%async_computation.6 | async-start | bytes 557056 | tf_op jit(solution)/shard_map/all_to_all | solution.py:30
  117.4 7.9 %collective-permute-start.2 = (bf16[32,256]{1,0:T(8,128)(2,1)S(1)}, bf16[32,256]{1,0:T(8,128)(2,1)S(1)}, u32[]{:S(2)}, u32[]{:S(2)}) collective-permute-start(bf16[32,256]{1,0:T(8,128)(2,1)S(1)} %get-tuple-element.20.own_ref.near_ref), channel_id=1, source_target_pairs={{0,8},{8,0},{1,9},{9,1},{2,10},{10,2},{3,11},{11,3},{4,12},{12,4},... | collective-permute-start | bytes 49160 | tf_op jit(solution)/shard_map/ppermute | solution.py:48
  125.3 5.4 %collective-permute-done.2.other_ref = bf16[32,256]{1,0:T(8,128)(2,1)S(1)} collective-permute-done((bf16[32,256]{1,0:T(8,128)(2,1)S(1)}, bf16[32,256]{1,0:T(8,128)(2,1)S(1)}, u32[]{:S(2)}, u32[]{:S(2)}) %collective-permute-start.2) | collective-permute-done | bytes 16416 | tf_op jit(solution)/shard_map/ppermute | solution.py:48
  131.0 19.2 %all_to_all.57.row_ref = bf16[8,136,256]{2,1,0:T(8,128)(2,1)S(1)} all-to-all(bf16[8,136,256]{2,1,0:T(8,128)(2,1)S(1)} %shard_map.73), channel_id=1, replica_groups=mesh['row_0'=8,'row_1'=4,'col_0'=2,'col_1'=4,'col_2'=2] {'col_1','col_2'}, dimensions={0} | all-to-all | bytes 1114112 | tf_op jit(solution)/shard_map/all_to_all | solution.py:30
  151.2 7.8 %collective-permute-start.3 = (bf16[48,256]{1,0:T(8,128)(2,1)S(1)}, bf16[48,256]{1,0:T(8,128)(2,1)S(1)}, u32[]{:S(2)}, u32[]{:S(2)}) collective-permute-start(bf16[48,256]{1,0:T(8,128)(2,1)S(1)} %get-tuple-element.21.sent_ref), channel_id=1, source_target_pairs={{0,8},{8,0},{1,9},{9,1},{2,10},{10,2},{3,11},{11,3},{4,12},{12,4},... | collective-permute-start | bytes 73736 | tf_op jit(solution)/shard_map/ppermute | solution.py:48
  159.1 5.4 %collective-permute-done.3.far_ref = bf16[48,256]{1,0:T(8,128)(2,1)S(1)} collective-permute-done((bf16[48,256]{1,0:T(8,128)(2,1)S(1)}, bf16[48,256]{1,0:T(8,128)(2,1)S(1)}, u32[]{:S(2)}, u32[]{:S(2)}) %collective-permute-start.3) | collective-permute-done | bytes 24608 | tf_op jit(solution)/shard_map/ppermute | solution.py:48
  165.2 7.2 %all-to-all-start.9 = ((bf16[32,8,256]{2,1,0:T(8,128)(2,1)}), bf16[32,8,256]{2,1,0:T(8,128)(2,1)S(1)}, u32[]{:S(2)}, u32[]{:S(2)}) async-start(bf16[32,8,256]{2,1,0:T(8,128)(2,1)} %get-tuple-element.25), calls=%async_computation.9 | async-start | bytes 262144 | tf_op jit(solution)/shard_map/all_to_all | solution.py:30
  176.1 3.9 %all-to-all-done.9.bits_ref = bf16[32,8,256]{2,1,0:T(8,128)(2,1)S(1)} async-done(((bf16[32,8,256]{2,1,0:T(8,128)(2,1)}), bf16[32,8,256]{2,1,0:T(8,128)(2,1)S(1)}, u32[]{:S(2)}, u32[]{:S(2)}) %all-to-all-start.9) | async-done | bytes 131104 | tf_op jit(solution)/shard_map/all_to_all | solution.py:30
  180.0 3.4 %all-to-all-start.8 = ((bf16[4,128,256]{2,1,0:T(8,128)(2,1)}), bf16[4,128,256]{2,1,0:T(8,128)(2,1)S(1)}, u32[]{:S(2)}, u32[]{:S(2)}) async-start(bf16[4,128,256]{2,1,0:T(8,128)(2,1)} %get-tuple-element.24), calls=%async_computation.8 | async-start | bytes 524288 | tf_op jit(solution)/shard_map/all_to_all | solution.py:30
  186.5 2.9 %all-to-all-done.8.mirror_ref = bf16[4,128,256]{2,1,0:T(8,128)(2,1)S(1)} async-done(((bf16[4,128,256]{2,1,0:T(8,128)(2,1)}), bf16[4,128,256]{2,1,0:T(8,128)(2,1)S(1)}, u32[]{:S(2)}, u32[]{:S(2)}) %all-to-all-start.8) | async-done | bytes 262176 | tf_op jit(solution)/shard_map/all_to_all | solution.py:30
  190.3 3.4 %all-to-all-start.10 = ((bf16[8,40,256]{2,1,0:T(8,128)(2,1)}), bf16[8,40,256]{2,1,0:T(8,128)(2,1)S(1)}, u32[]{:S(2)}, u32[]{:S(2)}) async-start(bf16[8,40,256]{2,1,0:T(8,128)(2,1)} %shard_map.76), calls=%async_computation.10 | async-start | bytes 327680 | tf_op jit(solution)/shard_map/all_to_all | solution.py:30
  194.7 9.6 %all-to-all-done.10.mirror_ref = bf16[8,40,256]{2,1,0:T(8,128)(2,1)S(1)} async-done(((bf16[8,40,256]{2,1,0:T(8,128)(2,1)}), bf16[8,40,256]{2,1,0:T(8,128)(2,1)S(1)}, u32[]{:S(2)}, u32[]{:S(2)}) %all-to-all-start.10) | async-done | bytes 163872 | tf_op jit(solution)/shard_map/all_to_all | solution.py:30
  (41 shorter events, 17.8 us)
Async XLA Ops:
  2.0 13.2 %copy-start.3 = (s32[1,1,4]{2,1,0:T(1,128)S(1)}, s32[1,1,4]{2,1,0:T(1,128)}, u32[]{:S(2)}) copy-start(s32[1,1,4]{2,1,0:T(1,128)} %param.6) | copy-start | bytes 52
  2.0 23.5 %all-to-all-start = ((bf16[8,32,256]{2,1,0:T(8,128)(2,1)}), bf16[8,32,256]{2,1,0:T(8,128)(2,1)S(1)}, u32[]{:S(2)}, u32[]{:S(2)}) async-start(bf16[8,32,256]{2,1,0:T(8,128)(2,1)} %broadcast_in_dim.12), calls=%async_computation | async-start | bytes 262144 | tf_op jit(solution)/shard_map/all_to_all | solution.py:30
  26.4 4.3 %copy-start.1 = (bf16[32,256]{1,0:T(8,128)(2,1)S(1)}, bf16[32,256]{1,0:T(8,128)(2,1)}, u32[]{:S(2)}) copy-start(bf16[32,256]{1,0:T(8,128)(2,1)} %near_ref.1) | copy-start | bytes 49156
  26.4 17.5 %copy-start = (bf16[1,1,4,256,256]{4,3,2,1,0:T(8,128)(2,1)S(1)}, bf16[1,1,4,256,256]{4,3,2,1,0:T(8,128)(2,1)}, u32[]{:S(2)}) copy-start(bf16[1,1,4,256,256]{4,3,2,1,0:T(8,128)(2,1)} %param.4) | copy-start | bytes 1572868
  26.4 17.5 %all-to-all-start.1 = ((bf16[4,264,256]{2,1,0:T(8,128)(2,1)}), bf16[4,264,256]{2,1,0:T(8,128)(2,1)S(1)}, u32[]{:S(2)}, u32[]{:S(2)}) async-start(bf16[4,264,256]{2,1,0:T(8,128)(2,1)} %shard_map.67), calls=%async_computation.1 | async-start | bytes 1081344 | tf_op jit(solution)/shard_map/all_to_all | solution.py:30
  30.7 13.2 %collective-permute-start = (bf16[32,256]{1,0:T(8,128)(2,1)S(1)}, bf16[32,256]{1,0:T(8,128)(2,1)S(1)}, u32[]{:S(2)}, u32[]{:S(2)}) collective-permute-start(bf16[32,256]{1,0:T(8,128)(2,1)S(1)} %copy-done.1), channel_id=1, source_target_pairs={{0,8},{8,0},{1,9},{9,1},{2,10},{10,2},{3,11},{11,3},{4,12},{12,4},... | collective-permute-start | bytes 49160 | tf_op jit(solution)/shard_map/ppermute | solution.py:48
  38.6 0.7 copy-start.4
  74.9 17.3 %all-to-all-start.4 = ((bf16[8,32,256]{2,1,0:T(8,128)(2,1)}), bf16[8,32,256]{2,1,0:T(8,128)(2,1)S(1)}, u32[]{:S(2)}, u32[]{:S(2)}) async-start(bf16[8,32,256]{2,1,0:T(8,128)(2,1)} %shard_map.70), calls=%async_computation.4 | async-start | bytes 262144 | tf_op jit(solution)/shard_map/all_to_all | solution.py:30
  79.0 13.2 %collective-permute-start.1 = (bf16[32,256]{1,0:T(8,128)(2,1)S(1)}, bf16[32,256]{1,0:T(8,128)(2,1)S(1)}, u32[]{:S(2)}, u32[]{:S(2)}) collective-permute-start(bf16[32,256]{1,0:T(8,128)(2,1)S(1)} %get-tuple-element.17), channel_id=1, source_target_pairs={{0,8},{8,0},{1,9},{9,1},{2,10},{10,2},{3,11},{11,3},{4,12},{12,4},... | collective-permute-start | bytes 49160 | tf_op jit(solution)/shard_map/ppermute | solution.py:48
  93.1 20.0 %all-to-all-start.5 = ((bf16[8,40,256]{2,1,0:T(8,128)(2,1)}), bf16[8,40,256]{2,1,0:T(8,128)(2,1)S(1)}, u32[]{:S(2)}, u32[]{:S(2)}) async-start(bf16[8,40,256]{2,1,0:T(8,128)(2,1)} %get-tuple-element.19), calls=%async_computation.5 | async-start | bytes 327680 | tf_op jit(solution)/shard_map/all_to_all | solution.py:30
  113.9 16.7 %all-to-all-start.6 = ((bf16[4,136,256]{2,1,0:T(8,128)(2,1)}), bf16[4,136,256]{2,1,0:T(8,128)(2,1)S(1)}, u32[]{:S(2)}, u32[]{:S(2)}) async-start(bf16[4,136,256]{2,1,0:T(8,128)(2,1)} %shard_map.72), calls=%async_computation.6 | async-start | bytes 557056 | tf_op jit(solution)/shard_map/all_to_all | solution.py:30
  117.4 13.3 %collective-permute-start.2 = (bf16[32,256]{1,0:T(8,128)(2,1)S(1)}, bf16[32,256]{1,0:T(8,128)(2,1)S(1)}, u32[]{:S(2)}, u32[]{:S(2)}) collective-permute-start(bf16[32,256]{1,0:T(8,128)(2,1)S(1)} %get-tuple-element.20.own_ref.near_ref), channel_id=1, source_target_pairs={{0,8},{8,0},{1,9},{9,1},{2,10},{10,2},{3,11},{11,3},{4,12},{12,4},... | collective-permute-start | bytes 49160 | tf_op jit(solution)/shard_map/ppermute | solution.py:48
  151.2 13.3 %collective-permute-start.3 = (bf16[48,256]{1,0:T(8,128)(2,1)S(1)}, bf16[48,256]{1,0:T(8,128)(2,1)S(1)}, u32[]{:S(2)}, u32[]{:S(2)}) collective-permute-start(bf16[48,256]{1,0:T(8,128)(2,1)S(1)} %get-tuple-element.21.sent_ref), channel_id=1, source_target_pairs={{0,8},{8,0},{1,9},{9,1},{2,10},{10,2},{3,11},{11,3},{4,12},{12,4},... | collective-permute-start | bytes 73736 | tf_op jit(solution)/shard_map/ppermute | solution.py:48
  165.2 14.9 %all-to-all-start.9 = ((bf16[32,8,256]{2,1,0:T(8,128)(2,1)}), bf16[32,8,256]{2,1,0:T(8,128)(2,1)S(1)}, u32[]{:S(2)}, u32[]{:S(2)}) async-start(bf16[32,8,256]{2,1,0:T(8,128)(2,1)} %get-tuple-element.25), calls=%async_computation.9 | async-start | bytes 262144 | tf_op jit(solution)/shard_map/all_to_all | solution.py:30
  180.0 9.4 %all-to-all-start.8 = ((bf16[4,128,256]{2,1,0:T(8,128)(2,1)}), bf16[4,128,256]{2,1,0:T(8,128)(2,1)S(1)}, u32[]{:S(2)}, u32[]{:S(2)}) async-start(bf16[4,128,256]{2,1,0:T(8,128)(2,1)} %get-tuple-element.24), calls=%async_computation.8 | async-start | bytes 524288 | tf_op jit(solution)/shard_map/all_to_all | solution.py:30
  190.3 14.0 %all-to-all-start.10 = ((bf16[8,40,256]{2,1,0:T(8,128)(2,1)}), bf16[8,40,256]{2,1,0:T(8,128)(2,1)S(1)}, u32[]{:S(2)}, u32[]{:S(2)}) async-start(bf16[8,40,256]{2,1,0:T(8,128)(2,1)} %shard_map.76), calls=%async_computation.10 | async-start | bytes 327680 | tf_op jit(solution)/shard_map/all_to_all | solution.py:30
  194.1 0.6 copy-start.2

commit v11 on v10

--- a/solution.py
+++ b/solution.py
@@ -102,7 +102,14 @@
         out_ref[y, pl.ds(by_z_ref.shape[0] * length, ROWS)] = note_ref[...]
 
 
-def select_kernel(peer_ref, by_z_ref, out_ref, *, vectors):
+def read_table(noted_ref, table_ref):
+    for y in range(noted_ref.shape[0]):
+        note = noted_ref[y, pl.ds(noted_ref.shape[1] - ROWS, ROWS), pl.ds(0, LANES)]
+        table_ref[y] = note.astype(F32).astype(jnp.int32)
+
+
+def select_kernel(noted_ref, by_z_ref, out_ref, table_ref, *, vectors):
+    read_table(noted_ref, table_ref)
     y_count = out_ref.shape[0]
     tiles = (out_ref.shape[1] - ROWS) // vectors
     total = jnp.zeros((ROWS, LANES), F32)
@@ -110,7 +117,7 @@
         total += from_bits(by_z_ref[z, pl.ds(vectors, ROWS)])
     for y in range(y_count):
         for t in range(tiles):
-            place, _ = parted(peer_ref[y, t], y_count)
+            place, _ = parted(table_ref[y, 0, t], y_count)
             out_ref[y, pl.ds(t * vectors, vectors)] = by_z_ref[place, pl.ds(0, vectors)]
         store_bits(out_ref, (y, pl.ds(tiles * vectors, ROWS)), total)
 
@@ -178,17 +185,9 @@
         store_bits(far_ref, (pl.ds(vectors + ROWS, ROWS),), pack(form))
     for k in range(y_count):
         out_ref[k] = jnp.zeros(out_ref.shape[1:], BF16)
-    if extra:
-        for t in range(tiles):
-            _, y = parted(pair_ref[0, tiles + t], y_count)
-            out_ref[y, pl.ds(t * vectors, vectors)] = sums_ref[t].astype(BF16)
-        return
-    slots = []
     for t in range(tiles):
-        j = pair_ref[0, tiles + t]
-        z, y = parted(j, y_count)
-        slots.append((j, (y, span(z, vectors))))
-    store_sums(out_ref, slots, sums_ref)
+        _, y = parted(pair_ref[0, tiles + t], y_count)
+        out_ref[y, pl.ds(t * vectors, vectors)] = sums_ref[t].astype(BF16)
 
 
 def image_kernel(direct_ref, far_ref, mirror_ref, image_ref, current_ref, send_ref):
@@ -204,14 +203,19 @@
         store_bits(send_ref, (z, pl.ds(image.shape[0], ROWS)), gram)
 
 
-def first_middle_kernel(mirror_ref, send_ref):
-    vectors = send_ref.shape[1]
-    for z in range(send_ref.shape[0]):
-        rows = pl.ds(z * vectors, vectors)
-        total = mirror_ref[0, rows].astype(F32)
-        for y in range(1, mirror_ref.shape[0]):
-            total = total + mirror_ref[y, rows].astype(F32)
-        send_ref[z] = total.astype(BF16)
+def sum_over_y(noted_ref, mirror_ref, sums_ref, table_ref):
+    read_table(noted_ref, table_ref)
+    y_count, vectors = (mirror_ref.shape[0], sums_ref.shape[1])
+    sums_ref[...] = jnp.zeros_like(sums_ref)
+    for y in range(y_count):
+        for t in range(mirror_ref.shape[1] // vectors):
+            z, _ = parted(table_ref[y, 0, t], y_count)
+            sums_ref[z] = sums_ref[z] + mirror_ref[y, pl.ds(t * vectors, vectors)].astype(F32)
+
+
+def first_middle_kernel(noted_ref, mirror_ref, send_ref, sums_ref, table_ref):
+    sum_over_y(noted_ref, mirror_ref, sums_ref, table_ref)
+    send_ref[...] = sums_ref[...].astype(BF16)
 
 
 def form_kernel(sent_ref, far_ref, send_ref, gram_ref, *, rows):
@@ -224,13 +228,9 @@
         store_bits(send_ref, (k, pl.ds(0, ROWS)), form)
 
 
-def second_middle_kernel(peer_ref, mirror_ref, bits_ref, send_ref, sums_ref):
-    y_count, vectors = (mirror_ref.shape[0], sums_ref.shape[1])
-    sums_ref[...] = jnp.zeros_like(sums_ref)
-    for y in range(y_count):
-        for t in range(mirror_ref.shape[1] // vectors):
-            z, _ = parted(peer_ref[y, t], y_count)
-            sums_ref[z] = sums_ref[z] + mirror_ref[y, pl.ds(t * vectors, vectors)].astype(F32)
+def second_middle_kernel(noted_ref, mirror_ref, bits_ref, send_ref, sums_ref, table_ref):
+    sum_over_y(noted_ref, mirror_ref, sums_ref, table_ref)
+    vectors = sums_ref.shape[1]
     form = jnp.zeros((ROWS, LANES), F32)
     for k in range(bits_ref.shape[0]):
         form += from_bits(bits_ref[k])
@@ -256,11 +256,12 @@
     residual_ref[...] = last_image - dot(half, turned_ref[...], 1, 0)
 
 
-def product(pairs, tiles, current, send_z, note, peers):
+def product(pairs, tiles, current, send_z, note, noted):
     vectors, size = current.shape
     count = tiles.shape[0]
     y_count, z_count, xc_count = (lax.axis_size(Y), lax.axis_size(Z_LO), lax.axis_size(X_CORE))
     extra = send_z is not None
+    table = pltpu.VMEM((y_count, ROWS, LANES), jnp.int32)
     if not extra:
         send_z = jnp.broadcast_to(current[None], (z_count, vectors, size))
     by_z = exchange(send_z, Z_LO)
@@ -268,13 +269,13 @@
     if extra:
         select = functools.partial(select_kernel, vectors=vectors)
         out = ((y_count, count * vectors + ROWS, size), BF16)
-        send = call(select, out)(peers, by_z)[0]
+        send = call(select, out, scratch=[table])(noted, by_z)[0]
     else:
         out = ((y_count, z_count * vectors + ROWS, size), BF16)
         send = call(spread_kernel, out)(by_z, note)[0]
     column_block = exchange(send, Y)
     if not extra:
-        peers = column_block[:, z_count * vectors, :LANES].astype(jnp.int32)
+        noted = column_block
     send = call(
         functools.partial(direct_kernel, extra=extra),
         ((xc_count, 4 * vectors + ROWS * extra, size), BF16),
@@ -283,13 +284,14 @@
     arrived = exchange(send, X_CORE)
     send, own_direct, far = call(
         mirror_kernel,
-        ((y_count, (count if extra else z_count) * vectors, size), BF16),
+        ((y_count, count * vectors, size), BF16),
         ((vectors, size), F32),
         ((vectors + 2 * ROWS * extra, size), BF16),
         scratch=[pltpu.VMEM((count, vectors, size), F32)],
     )(pairs, arrived, tiles, current, other)
     mirror = exchange(send, Y)
     sent, far = (far, partner(far))
+    sums = pltpu.VMEM((z_count, vectors, size), F32)
     if extra:
         form, gram = call(
             functools.partial(form_kernel, rows=size * lax.axis_size(COL_ROW)),
@@ -300,13 +302,14 @@
         mirror = call(
             second_middle_kernel,
             ((z_count, vectors + ROWS, size), BF16),
-            scratch=[pltpu.VMEM((z_count, vectors, size), F32)],
-        )(peers, mirror, form)[0]
+            scratch=[sums, table],
+        )(noted, mirror, form)[0]
     else:
-        mirror = call(first_middle_kernel, ((z_count, vectors, size), BF16))(mirror)[0]
+        out = ((z_count, vectors, size), BF16)
+        mirror = call(first_middle_kernel, out, scratch=[sums, table])(noted, mirror)[0]
         gram = None
     mirror = exchange(mirror, Z_LO)
-    return own_direct, far, mirror, gram, peers
+    return own_direct, far, mirror, gram, noted
 
 
 def steps(tile_values, tile_row, tile_col, basis_init):
@@ -320,14 +323,14 @@
     note = jnp.pad(
         tile_col[0].astype(BF16), [(0, ROWS - 1), (0, size - tiles.shape[0])]
     )
-    own_direct, far, mirror, _, peers = product(pairs, tiles, basis_init, None, note, None)
+    own_direct, far, mirror, _, noted = product(pairs, tiles, basis_init, None, note, None)
     image, current, send = call(
         image_kernel,
         ((vectors, size), F32),
         ((vectors, size), BF16),
         ((mirror.shape[0], vectors + ROWS, size), BF16),
     )(own_direct, far, mirror)
-    own_direct, far, mirror, gram, _ = product(pairs, tiles, current, send, None, peers)
+    own_direct, far, mirror, gram, _ = product(pairs, tiles, current, send, None, noted)
     factor = jnp.linalg.cholesky(gram)
     inverse = lax.linalg.triangular_solve(
         factor, jnp.eye(vectors, dtype=F32), left_side=True, lower=True

time: 208 us -> 204 us (0.981)
  blocking collectives: 48.9 us -> 66.3 us
  waiting for transfers between devices: 58 us -> 47.4 us
  starting transfers between devices: 79.9 us -> 70.6 us
    all_to_all x3 -> x4, blocking collectives: 48.9 us -> 66.3 us  [exchange(): return lax.all_to_all(parts, axis, 0, 0, tiled=True)]
    all_to_all x8 -> x7, waiting for transfers between devices: 37.4 us -> 26.8 us  [exchange(): return lax.all_to_all(parts, axis, 0, 0, tiled=True)]
    all_to_all x8 -> x7, starting transfers between devices: 48.4 us -> 39.1 us  [exchange(): return lax.all_to_all(parts, axis, 0, 0, tiled=True)]
  transfers between devices with their start and end apart: 12 -> 11, of which waited for: 9 -> 8; matrix products, arithmetic and copies ran while one was open for 4% -> 4% of each run, Pallas kernels for 0% -> 0%
where the time goes in v11:
time: 204 us; the launch traced here: 202 us
  starting transfers between devices  70.6 us (35%)
  blocking collectives  66.3 us (32%)
  waiting for transfers between devices  47.4 us (23%)
  Pallas kernels  7.3 us (4%)
  other arithmetic  6.77 us (3%)
  local copies, waits for them, and re-layouts  2.51 us (1%)
    all_to_all x4, blocking collectives, exchange(): return lax.all_to_all(parts, axis, 0, 0, tiled=True)  66.3 us
    all_to_all x7, starting transfers between devices, exchange(): return lax.all_to_all(parts, axis, 0, 0, tiled=True)  39.1 us
    ppermute x4, starting transfers between devices, partner(): return lax.ppermute(value, Z_HI, [(0, 1), (1, 0)])  31.5 us
    all_to_all x7, waiting for transfers between devices, exchange(): return lax.all_to_all(parts, axis, 0, 0, tiled=True)  26.8 us
    ppermute x4, waiting for transfers between devices, partner(): return lax.ppermute(value, Z_HI, [(0, 1), (1, 0)])  20.6 us
    pallas_call x11, Pallas kernels, run(): pl.pallas_call(kernel, out_shape=tuple((out(shape, kind) for shape, kind...  7.3 us
  transfers between devices with their start and end apart: 11, of which 8 were waited for; matrix products, arithmetic and copies ran while one was open for 4% of the time, Pallas kernels for 0%

profile of v11, /device:TPU:1, one launch (start us, length us, event | category | flops | bytes accessed | tf_op | source)
XLA Modules:
  0.0 202.2 jit_solution(15277332430908917993)
XLA Ops:
  2.0 13.2 %all-to-all-start = ((bf16[8,32,256]{2,1,0:T(8,128)(2,1)}), bf16[8,32,256]{2,1,0:T(8,128)(2,1)S(1)}, u32[]{:S(2)}, u32[]{:S(2)}) async-start(bf16[8,32,256]{2,1,0:T(8,128)(2,1)} %broadcast_in_dim.12), calls=%async_computation | async-start | bytes 262144 | tf_op jit(solution)/shard_map/all_to_all | solution.py:30
  15.2 10.3 %all-to-all-done.by_z_ref = bf16[8,32,256]{2,1,0:T(8,128)(2,1)S(1)} async-done(((bf16[8,32,256]{2,1,0:T(8,128)(2,1)}), bf16[8,32,256]{2,1,0:T(8,128)(2,1)S(1)}, u32[]{:S(2)}, u32[]{:S(2)}) %all-to-all-start) | async-done | bytes 131104 | tf_op jit(solution)/shard_map/all_to_all | solution.py:30
  26.4 4.3 %all-to-all-start.1 = ((bf16[4,264,256]{2,1,0:T(8,128)(2,1)}), bf16[4,264,256]{2,1,0:T(8,128)(2,1)S(1)}, u32[]{:S(2)}, u32[]{:S(2)}) async-start(bf16[4,264,256]{2,1,0:T(8,128)(2,1)} %shard_map.67), calls=%async_computation.1 | async-start | bytes 1081344 | tf_op jit(solution)/shard_map/all_to_all | solution.py:30
  30.7 7.9 %collective-permute-start = (bf16[32,256]{1,0:T(8,128)(2,1)S(1)}, bf16[32,256]{1,0:T(8,128)(2,1)S(1)}, u32[]{:S(2)}, u32[]{:S(2)}) collective-permute-start(bf16[32,256]{1,0:T(8,128)(2,1)S(1)} %copy-done.1), channel_id=1, source_target_pairs={{0,8},{8,0},{1,9},{9,1},{2,10},{10,2},{3,11},{11,3},{4,12},{12,4},... | collective-permute-start | bytes 49160 | tf_op jit(solution)/shard_map/ppermute | solution.py:48
  39.4 4.5 %collective-permute-done.other_ref = bf16[32,256]{1,0:T(8,128)(2,1)S(1)} collective-permute-done((bf16[32,256]{1,0:T(8,128)(2,1)S(1)}, bf16[32,256]{1,0:T(8,128)(2,1)S(1)}, u32[]{:S(2)}, u32[]{:S(2)}) %collective-permute-start) | collective-permute-done | bytes 16416 | tf_op jit(solution)/shard_map/ppermute | solution.py:48
  44.2 17.7 %all_to_all.55.row_ref = bf16[8,128,256]{2,1,0:T(8,128)(2,1)S(1)} all-to-all(bf16[8,128,256]{2,1,0:T(8,128)(2,1)S(1)} %shard_map.68), channel_id=1, replica_groups=mesh['row_0'=8,'row_1'=4,'col_0'=2,'col_1'=4,'col_2'=2] {'col_1','col_2'}, dimensions={0} | all-to-all | bytes 1048576 | tf_op jit(solution)/shard_map/all_to_all | solution.py:30
  62.2 9.6 %all_to_all.56.mirror_ref = bf16[4,128,256]{2,1,0:T(8,128)(2,1)S(1)} all-to-all(bf16[4,128,256]{2,1,0:T(8,128)(2,1)S(1)} %get-tuple-element.18), channel_id=1, replica_groups=mesh['row_0'=8,'row_1'=4,'col_0'=2,'col_1'=4,'col_2'=2] {'row_1'}, dimensions={0} | all-to-all | bytes 524288 | tf_op jit(solution)/shard_map/all_to_all | solution.py:30
  72.6 4.1 %all-to-all-start.4 = ((bf16[8,32,256]{2,1,0:T(8,128)(2,1)}), bf16[8,32,256]{2,1,0:T(8,128)(2,1)S(1)}, u32[]{:S(2)}, u32[]{:S(2)}) async-start(bf16[8,32,256]{2,1,0:T(8,128)(2,1)} %shard_map.70), calls=%async_computation.4 | async-start | bytes 262144 | tf_op jit(solution)/shard_map/all_to_all | solution.py:30
  76.7 7.8 %collective-permute-start.1 = (bf16[32,256]{1,0:T(8,128)(2,1)S(1)}, bf16[32,256]{1,0:T(8,128)(2,1)S(1)}, u32[]{:S(2)}, u32[]{:S(2)}) collective-permute-start(bf16[32,256]{1,0:T(8,128)(2,1)S(1)} %get-tuple-element.17), channel_id=1, source_target_pairs={{0,8},{8,0},{1,9},{9,1},{2,10},{10,2},{3,11},{11,3},{4,12},{12,4},... | collective-permute-start | bytes 49160 | tf_op jit(solution)/shard_map/ppermute | solution.py:48
  84.5 5.3 %collective-permute-done.1.far_ref = bf16[32,256]{1,0:T(8,128)(2,1)S(1)} collective-permute-done((bf16[32,256]{1,0:T(8,128)(2,1)S(1)}, bf16[32,256]{1,0:T(8,128)(2,1)S(1)}, u32[]{:S(2)}, u32[]{:S(2)}) %collective-permute-start.1) | collective-permute-done | bytes 16416 | tf_op jit(solution)/shard_map/ppermute | solution.py:48
  90.1 19.8 %all_to_all.57.by_z_ref = bf16[8,40,256]{2,1,0:T(8,128)(2,1)S(1)} all-to-all(bf16[8,40,256]{2,1,0:T(8,128)(2,1)S(1)} %get-tuple-element.19), channel_id=1, replica_groups=mesh['row_0'=8,'row_1'=4,'col_0'=2,'col_1'=4,'col_2'=2] {'row_0'}, dimensions={0} | all-to-all | bytes 327680 | tf_op jit(solution)/shard_map/all_to_all | solution.py:30
  110.7 3.4 %all-to-all-start.6 = ((bf16[4,136,256]{2,1,0:T(8,128)(2,1)}), bf16[4,136,256]{2,1,0:T(8,128)(2,1)S(1)}, u32[]{:S(2)}, u32[]{:S(2)}) async-start(bf16[4,136,256]{2,1,0:T(8,128)(2,1)} %shard_map.72), calls=%async_computation.6 | async-start | bytes 557056 | tf_op jit(solution)/shard_map/all_to_all | solution.py:30
  114.2 7.9 %collective-permute-start.2 = (bf16[32,256]{1,0:T(8,128)(2,1)S(1)}, bf16[32,256]{1,0:T(8,128)(2,1)S(1)}, u32[]{:S(2)}, u32[]{:S(2)}) collective-permute-start(bf16[32,256]{1,0:T(8,128)(2,1)S(1)} %get-tuple-element.20.own_ref.near_ref), channel_id=1, source_target_pairs={{0,8},{8,0},{1,9},{9,1},{2,10},{10,2},{3,11},{11,3},{4,12},{12,4},... | collective-permute-start | bytes 49160 | tf_op jit(solution)/shard_map/ppermute | solution.py:48
  122.1 5.4 %collective-permute-done.2.other_ref = bf16[32,256]{1,0:T(8,128)(2,1)S(1)} collective-permute-done((bf16[32,256]{1,0:T(8,128)(2,1)S(1)}, bf16[32,256]{1,0:T(8,128)(2,1)S(1)}, u32[]{:S(2)}, u32[]{:S(2)}) %collective-permute-start.2) | collective-permute-done | bytes 16416 | tf_op jit(solution)/shard_map/ppermute | solution.py:48
  127.8 19.2 %all_to_all.58.row_ref = bf16[8,136,256]{2,1,0:T(8,128)(2,1)S(1)} all-to-all(bf16[8,136,256]{2,1,0:T(8,128)(2,1)S(1)} %shard_map.73), channel_id=1, replica_groups=mesh['row_0'=8,'row_1'=4,'col_0'=2,'col_1'=4,'col_2'=2] {'col_1','col_2'}, dimensions={0} | all-to-all | bytes 1114112 | tf_op jit(solution)/shard_map/all_to_all | solution.py:30
  148.0 7.8 %collective-permute-start.3 = (bf16[48,256]{1,0:T(8,128)(2,1)S(1)}, bf16[48,256]{1,0:T(8,128)(2,1)S(1)}, u32[]{:S(2)}, u32[]{:S(2)}) collective-permute-start(bf16[48,256]{1,0:T(8,128)(2,1)S(1)} %get-tuple-element.21.sent_ref), channel_id=1, source_target_pairs={{0,8},{8,0},{1,9},{9,1},{2,10},{10,2},{3,11},{11,3},{4,12},{12,4},... | collective-permute-start | bytes 73736 | tf_op jit(solution)/shard_map/ppermute | solution.py:48
  155.9 5.4 %collective-permute-done.3.far_ref = bf16[48,256]{1,0:T(8,128)(2,1)S(1)} collective-permute-done((bf16[48,256]{1,0:T(8,128)(2,1)S(1)}, bf16[48,256]{1,0:T(8,128)(2,1)S(1)}, u32[]{:S(2)}, u32[]{:S(2)}) %collective-permute-start.3) | collective-permute-done | bytes 24608 | tf_op jit(solution)/shard_map/ppermute | solution.py:48
  161.9 7.2 %all-to-all-start.9 = ((bf16[32,8,256]{2,1,0:T(8,128)(2,1)}), bf16[32,8,256]{2,1,0:T(8,128)(2,1)S(1)}, u32[]{:S(2)}, u32[]{:S(2)}) async-start(bf16[32,8,256]{2,1,0:T(8,128)(2,1)} %get-tuple-element.25), calls=%async_computation.9 | async-start | bytes 262144 | tf_op jit(solution)/shard_map/all_to_all | solution.py:30
  169.3 2.9 %cholesky.17 = f32[32,32]{1,0:T(8,128)S(1)} custom-call(f32[32,32]{1,0:T(8,128)S(1)} %fusion.3), custom_call_target="Cholesky" | custom-call | tf_op jit(solution)/shard_map/jit(cholesky)/cholesky | solution.py:334
  172.9 3.9 %all-to-all-done.9.bits_ref = bf16[32,8,256]{2,1,0:T(8,128)(2,1)S(1)} async-done(((bf16[32,8,256]{2,1,0:T(8,128)(2,1)}), bf16[32,8,256]{2,1,0:T(8,128)(2,1)S(1)}, u32[]{:S(2)}, u32[]{:S(2)}) %all-to-all-start.9) | async-done | bytes 131104 | tf_op jit(solution)/shard_map/all_to_all | solution.py:30
  176.8 3.4 %all-to-all-start.8 = ((bf16[4,128,256]{2,1,0:T(8,128)(2,1)}), bf16[4,128,256]{2,1,0:T(8,128)(2,1)S(1)}, u32[]{:S(2)}, u32[]{:S(2)}) async-start(bf16[4,128,256]{2,1,0:T(8,128)(2,1)} %get-tuple-element.24), calls=%async_computation.8 | async-start | bytes 524288 | tf_op jit(solution)/shard_map/all_to_all | solution.py:30
  183.3 2.9 %all-to-all-done.8.mirror_ref = bf16[4,128,256]{2,1,0:T(8,128)(2,1)S(1)} async-done(((bf16[4,128,256]{2,1,0:T(8,128)(2,1)}), bf16[4,128,256]{2,1,0:T(8,128)(2,1)S(1)}, u32[]{:S(2)}, u32[]{:S(2)}) %all-to-all-start.8) | async-done | bytes 262176 | tf_op jit(solution)/shard_map/all_to_all | solution.py:30
  187.1 3.4 %all-to-all-start.10 = ((bf16[8,40,256]{2,1,0:T(8,128)(2,1)}), bf16[8,40,256]{2,1,0:T(8,128)(2,1)S(1)}, u32[]{:S(2)}, u32[]{:S(2)}) async-start(bf16[8,40,256]{2,1,0:T(8,128)(2,1)} %shard_map.76), calls=%async_computation.10 | async-start | bytes 327680 | tf_op jit(solution)/shard_map/all_to_all | solution.py:30
  191.5 9.6 %all-to-all-done.10.mirror_ref = bf16[8,40,256]{2,1,0:T(8,128)(2,1)S(1)} async-done(((bf16[8,40,256]{2,1,0:T(8,128)(2,1)}), bf16[8,40,256]{2,1,0:T(8,128)(2,1)S(1)}, u32[]{:S(2)}, u32[]{:S(2)}) %all-to-all-start.10) | async-done | bytes 163872 | tf_op jit(solution)/shard_map/all_to_all | solution.py:30
  (38 shorter events, 14.3 us)
Async XLA Ops:
  2.0 13.2 %copy-start.3 = (s32[1,1,4]{2,1,0:T(1,128)S(1)}, s32[1,1,4]{2,1,0:T(1,128)}, u32[]{:S(2)}) copy-start(s32[1,1,4]{2,1,0:T(1,128)} %param.6) | copy-start | bytes 52
  2.0 23.5 %all-to-all-start = ((bf16[8,32,256]{2,1,0:T(8,128)(2,1)}), bf16[8,32,256]{2,1,0:T(8,128)(2,1)S(1)}, u32[]{:S(2)}, u32[]{:S(2)}) async-start(bf16[8,32,256]{2,1,0:T(8,128)(2,1)} %broadcast_in_dim.12), calls=%async_computation | async-start | bytes 262144 | tf_op jit(solution)/shard_map/all_to_all | solution.py:30
  26.4 4.3 %copy-start.1 = (bf16[32,256]{1,0:T(8,128)(2,1)S(1)}, bf16[32,256]{1,0:T(8,128)(2,1)}, u32[]{:S(2)}) copy-start(bf16[32,256]{1,0:T(8,128)(2,1)} %near_ref.1) | copy-start | bytes 49156
  26.4 17.5 %copy-start = (bf16[1,1,4,256,256]{4,3,2,1,0:T(8,128)(2,1)S(1)}, bf16[1,1,4,256,256]{4,3,2,1,0:T(8,128)(2,1)}, u32[]{:S(2)}) copy-start(bf16[1,1,4,256,256]{4,3,2,1,0:T(8,128)(2,1)} %param.4) | copy-start | bytes 1572868
  26.4 17.5 %all-to-all-start.1 = ((bf16[4,264,256]{2,1,0:T(8,128)(2,1)}), bf16[4,264,256]{2,1,0:T(8,128)(2,1)S(1)}, u32[]{:S(2)}, u32[]{:S(2)}) async-start(bf16[4,264,256]{2,1,0:T(8,128)(2,1)} %shard_map.67), calls=%async_computation.1 | async-start | bytes 1081344 | tf_op jit(solution)/shard_map/all_to_all | solution.py:30
  30.7 13.2 %collective-permute-start = (bf16[32,256]{1,0:T(8,128)(2,1)S(1)}, bf16[32,256]{1,0:T(8,128)(2,1)S(1)}, u32[]{:S(2)}, u32[]{:S(2)}) collective-permute-start(bf16[32,256]{1,0:T(8,128)(2,1)S(1)} %copy-done.1), channel_id=1, source_target_pairs={{0,8},{8,0},{1,9},{9,1},{2,10},{10,2},{3,11},{11,3},{4,12},{12,4},... | collective-permute-start | bytes 49160 | tf_op jit(solution)/shard_map/ppermute | solution.py:48
  38.6 0.7 copy-start.4
  72.6 17.3 %all-to-all-start.4 = ((bf16[8,32,256]{2,1,0:T(8,128)(2,1)}), bf16[8,32,256]{2,1,0:T(8,128)(2,1)S(1)}, u32[]{:S(2)}, u32[]{:S(2)}) async-start(bf16[8,32,256]{2,1,0:T(8,128)(2,1)} %shard_map.70), calls=%async_computation.4 | async-start | bytes 262144 | tf_op jit(solution)/shard_map/all_to_all | solution.py:30
  76.7 13.2 %collective-permute-start.1 = (bf16[32,256]{1,0:T(8,128)(2,1)S(1)}, bf16[32,256]{1,0:T(8,128)(2,1)S(1)}, u32[]{:S(2)}, u32[]{:S(2)}) collective-permute-start(bf16[32,256]{1,0:T(8,128)(2,1)S(1)} %get-tuple-element.17), channel_id=1, source_target_pairs={{0,8},{8,0},{1,9},{9,1},{2,10},{10,2},{3,11},{11,3},{4,12},{12,4},... | collective-permute-start | bytes 49160 | tf_op jit(solution)/shard_map/ppermute | solution.py:48
  110.7 16.7 %all-to-all-start.6 = ((bf16[4,136,256]{2,1,0:T(8,128)(2,1)}), bf16[4,136,256]{2,1,0:T(8,128)(2,1)S(1)}, u32[]{:S(2)}, u32[]{:S(2)}) async-start(bf16[4,136,256]{2,1,0:T(8,128)(2,1)} %shard_map.72), calls=%async_computation.6 | async-start | bytes 557056 | tf_op jit(solution)/shard_map/all_to_all | solution.py:30
  114.2 13.2 %collective-permute-start.2 = (bf16[32,256]{1,0:T(8,128)(2,1)S(1)}, bf16[32,256]{1,0:T(8,128)(2,1)S(1)}, u32[]{:S(2)}, u32[]{:S(2)}) collective-permute-start(bf16[32,256]{1,0:T(8,128)(2,1)S(1)} %get-tuple-element.20.own_ref.near_ref), channel_id=1, source_target_pairs={{0,8},{8,0},{1,9},{9,1},{2,10},{10,2},{3,11},{11,3},{4,12},{12,4},... | collective-permute-start | bytes 49160 | tf_op jit(solution)/shard_map/ppermute | solution.py:48
  148.0 13.3 %collective-permute-start.3 = (bf16[48,256]{1,0:T(8,128)(2,1)S(1)}, bf16[48,256]{1,0:T(8,128)(2,1)S(1)}, u32[]{:S(2)}, u32[]{:S(2)}) collective-permute-start(bf16[48,256]{1,0:T(8,128)(2,1)S(1)} %get-tuple-element.21.sent_ref), channel_id=1, source_target_pairs={{0,8},{8,0},{1,9},{9,1},{2,10},{10,2},{3,11},{11,3},{4,12},{12,4},... | collective-permute-start | bytes 73736 | tf_op jit(solution)/shard_map/ppermute | solution.py:48
  161.9 14.9 %all-to-all-start.9 = ((bf16[32,8,256]{2,1,0:T(8,128)(2,1)}), bf16[32,8,256]{2,1,0:T(8,128)(2,1)S(1)}, u32[]{:S(2)}, u32[]{:S(2)}) async-start(bf16[32,8,256]{2,1,0:T(8,128)(2,1)} %get-tuple-element.25), calls=%async_computation.9 | async-start | bytes 262144 | tf_op jit(solution)/shard_map/all_to_all | solution.py:30
  176.8 9.4 %all-to-all-start.8 = ((bf16[4,128,256]{2,1,0:T(8,128)(2,1)}), bf16[4,128,256]{2,1,0:T(8,128)(2,1)S(1)}, u32[]{:S(2)}, u32[]{:S(2)}) async-start(bf16[4,128,256]{2,1,0:T(8,128)(2,1)} %get-tuple-element.24), calls=%async_computation.8 | async-start | bytes 524288 | tf_op jit(solution)/shard_map/all_to_all | solution.py:30
  187.1 14.0 %all-to-all-start.10 = ((bf16[8,40,256]{2,1,0:T(8,128)(2,1)}), bf16[8,40,256]{2,1,0:T(8,128)(2,1)S(1)}, u32[]{:S(2)}, u32[]{:S(2)}) async-start(bf16[8,40,256]{2,1,0:T(8,128)(2,1)} %shard_map.76), calls=%async_computation.10 | async-start | bytes 327680 | tf_op jit(solution)/shard_map/all_to_all | solution.py:30
  190.9 0.6 copy-start.2

commit v12 on v11

--- a/solution.py
+++ b/solution.py
@@ -96,10 +96,13 @@
 
 def spread_kernel(by_z_ref, note_ref, out_ref):
     length = by_z_ref.shape[1]
+    end = by_z_ref.shape[0] * length
+    note = note_ref[...].astype(F32).astype(BF16)
     for y in range(out_ref.shape[0]):
         for z in range(by_z_ref.shape[0]):
             out_ref[y, pl.ds(z * length, length)] = by_z_ref[z]
-        out_ref[y, pl.ds(by_z_ref.shape[0] * length, ROWS)] = note_ref[...]
+        out_ref[y, pl.ds(end, ROWS)] = jnp.zeros((ROWS, out_ref.shape[2]), BF16)
+        out_ref[y, pl.ds(end, 1), pl.ds(0, note.shape[1])] = note
 
 
 def read_table(noted_ref, table_ref):
@@ -320,10 +323,7 @@
     vectors, size = basis_init.shape
     total_rows = size * lax.axis_size(COL_ROW)
 
-    note = jnp.pad(
-        tile_col[0].astype(BF16), [(0, ROWS - 1), (0, size - tiles.shape[0])]
-    )
-    own_direct, far, mirror, _, noted = product(pairs, tiles, basis_init, None, note, None)
+    own_direct, far, mirror, _, noted = product(pairs, tiles, basis_init, None, tile_col[0], None)
     image, current, send = call(
         image_kernel,
         ((vectors, size), F32),

time: 204 us -> 204 us (level)
  blocking collectives: 66.3 us -> 89.5 us
  starting transfers between devices: 70.6 us -> 57.4 us
  waiting for transfers between devices: 47.4 us -> 37.1 us
    all_to_all x4 -> x5, blocking collectives: 66.3 us -> 89.5 us  [exchange(): return lax.all_to_all(parts, axis, 0, 0, tiled=True)]
    all_to_all x7 -> x6, starting transfers between devices: 39.1 us -> 25.9 us  [exchange(): return lax.all_to_all(parts, axis, 0, 0, tiled=True)]
    all_to_all x7 -> x6, waiting for transfers between devices: 26.8 us -> 16.5 us  [exchange(): return lax.all_to_all(parts, axis, 0, 0, tiled=True)]
  transfers between devices with their start and end apart: 11 -> 10, of which waited for: 8 -> 7; matrix products, arithmetic and copies ran while one was open for 4% -> 4% of each run, Pallas kernels for 0% -> 0%
where the time goes in v12:
time: 204 us; the launch traced here: 202 us
  blocking collectives  89.5 us (44%)
  starting transfers between devices  57.4 us (28%)
  waiting for transfers between devices  37.1 us (18%)
  Pallas kernels  7.31 us (4%)
  other arithmetic  6.77 us (3%)
  local copies, waits for them, and re-layouts  2.5 us (1%)
    all_to_all x5, blocking collectives, exchange(): return lax.all_to_all(parts, axis, 0, 0, tiled=True)  89.5 us
    ppermute x4, starting transfers between devices, partner(): return lax.ppermute(value, Z_HI, [(0, 1), (1, 0)])  31.5 us
    all_to_all x6, starting transfers between devices, exchange(): return lax.all_to_all(parts, axis, 0, 0, tiled=True)  25.9 us
    ppermute x4, waiting for transfers between devices, partner(): return lax.ppermute(value, Z_HI, [(0, 1), (1, 0)])  20.6 us
    all_to_all x6, waiting for transfers between devices, exchange(): return lax.all_to_all(parts, axis, 0, 0, tiled=True)  16.5 us
    pallas_call x11, Pallas kernels, run(): pl.pallas_call(kernel, out_shape=tuple((out(shape, kind) for shape, kind...  7.31 us
  transfers between devices with their start and end apart: 10, of which 7 were waited for; matrix products, arithmetic and copies ran while one was open for 4% of the time, Pallas kernels for 0%

profile of v12, /device:TPU:1, one launch (start us, length us, event | category | flops | bytes accessed | tf_op | source)
XLA Modules:
  0.0 201.9 jit_solution(12854197384247337662)
XLA Ops:
  1.4 23.2 %all_to_all.55.by_z_ref = bf16[8,32,256]{2,1,0:T(8,128)(2,1)S(1)} all-to-all(bf16[8,32,256]{2,1,0:T(8,128)(2,1)S(1)} %broadcast_in_dim.12), channel_id=1, replica_groups=mesh['row_0'=8,'row_1'=4,'col_0'=2,'col_1'=4,'col_2'=2] {'row_0'}, dimensions={0} | all-to-all | bytes 262144 | tf_op jit(solution)/shard_map/all_to_all | solution.py:30
  26.1 4.3 %all-to-all-start.1 = ((bf16[4,264,256]{2,1,0:T(8,128)(2,1)}), bf16[4,264,256]{2,1,0:T(8,128)(2,1)S(1)}, u32[]{:S(2)}, u32[]{:S(2)}) async-start(bf16[4,264,256]{2,1,0:T(8,128)(2,1)} %shard_map.67), calls=%async_computation.1 | async-start | bytes 1081344 | tf_op jit(solution)/shard_map/all_to_all | solution.py:30
  30.4 7.9 %collective-permute-start = (bf16[32,256]{1,0:T(8,128)(2,1)S(1)}, bf16[32,256]{1,0:T(8,128)(2,1)S(1)}, u32[]{:S(2)}, u32[]{:S(2)}) collective-permute-start(bf16[32,256]{1,0:T(8,128)(2,1)S(1)} %copy-done.1), channel_id=1, source_target_pairs={{0,8},{8,0},{1,9},{9,1},{2,10},{10,2},{3,11},{11,3},{4,12},{12,4},... | collective-permute-start | bytes 49160 | tf_op jit(solution)/shard_map/ppermute | solution.py:48
  39.1 4.5 %collective-permute-done.other_ref = bf16[32,256]{1,0:T(8,128)(2,1)S(1)} collective-permute-done((bf16[32,256]{1,0:T(8,128)(2,1)S(1)}, bf16[32,256]{1,0:T(8,128)(2,1)S(1)}, u32[]{:S(2)}, u32[]{:S(2)}) %collective-permute-start) | collective-permute-done | bytes 16416 | tf_op jit(solution)/shard_map/ppermute | solution.py:48
  43.9 17.7 %all_to_all.56.row_ref = bf16[8,128,256]{2,1,0:T(8,128)(2,1)S(1)} all-to-all(bf16[8,128,256]{2,1,0:T(8,128)(2,1)S(1)} %shard_map.68), channel_id=1, replica_groups=mesh['row_0'=8,'row_1'=4,'col_0'=2,'col_1'=4,'col_2'=2] {'col_1','col_2'}, dimensions={0} | all-to-all | bytes 1048576 | tf_op jit(solution)/shard_map/all_to_all | solution.py:30
  61.9 9.6 %all_to_all.57.mirror_ref = bf16[4,128,256]{2,1,0:T(8,128)(2,1)S(1)} all-to-all(bf16[4,128,256]{2,1,0:T(8,128)(2,1)S(1)} %get-tuple-element.18), channel_id=1, replica_groups=mesh['row_0'=8,'row_1'=4,'col_0'=2,'col_1'=4,'col_2'=2] {'row_1'}, dimensions={0} | all-to-all | bytes 524288 | tf_op jit(solution)/shard_map/all_to_all | solution.py:30
  72.3 4.1 %all-to-all-start.4 = ((bf16[8,32,256]{2,1,0:T(8,128)(2,1)}), bf16[8,32,256]{2,1,0:T(8,128)(2,1)S(1)}, u32[]{:S(2)}, u32[]{:S(2)}) async-start(bf16[8,32,256]{2,1,0:T(8,128)(2,1)} %shard_map.70), calls=%async_computation.4 | async-start | bytes 262144 | tf_op jit(solution)/shard_map/all_to_all | solution.py:30
  76.4 7.8 %collective-permute-start.1 = (bf16[32,256]{1,0:T(8,128)(2,1)S(1)}, bf16[32,256]{1,0:T(8,128)(2,1)S(1)}, u32[]{:S(2)}, u32[]{:S(2)}) collective-permute-start(bf16[32,256]{1,0:T(8,128)(2,1)S(1)} %get-tuple-element.17), channel_id=1, source_target_pairs={{0,8},{8,0},{1,9},{9,1},{2,10},{10,2},{3,11},{11,3},{4,12},{12,4},... | collective-permute-start | bytes 49160 | tf_op jit(solution)/shard_map/ppermute | solution.py:48
  84.2 5.3 %collective-permute-done.1.far_ref = bf16[32,256]{1,0:T(8,128)(2,1)S(1)} collective-permute-done((bf16[32,256]{1,0:T(8,128)(2,1)S(1)}, bf16[32,256]{1,0:T(8,128)(2,1)S(1)}, u32[]{:S(2)}, u32[]{:S(2)}) %collective-permute-start.1) | collective-permute-done | bytes 16416 | tf_op jit(solution)/shard_map/ppermute | solution.py:48
  89.8 19.8 %all_to_all.58.by_z_ref = bf16[8,40,256]{2,1,0:T(8,128)(2,1)S(1)} all-to-all(bf16[8,40,256]{2,1,0:T(8,128)(2,1)S(1)} %get-tuple-element.19), channel_id=1, replica_groups=mesh['row_0'=8,'row_1'=4,'col_0'=2,'col_1'=4,'col_2'=2] {'row_0'}, dimensions={0} | all-to-all | bytes 327680 | tf_op jit(solution)/shard_map/all_to_all | solution.py:30
  110.4 3.4 %all-to-all-start.6 = ((bf16[4,136,256]{2,1,0:T(8,128)(2,1)}), bf16[4,136,256]{2,1,0:T(8,128)(2,1)S(1)}, u32[]{:S(2)}, u32[]{:S(2)}) async-start(bf16[4,136,256]{2,1,0:T(8,128)(2,1)} %shard_map.72), calls=%async_computation.6 | async-start | bytes 557056 | tf_op jit(solution)/shard_map/all_to_all | solution.py:30
  113.9 7.9 %collective-permute-start.2 = (bf16[32,256]{1,0:T(8,128)(2,1)S(1)}, bf16[32,256]{1,0:T(8,128)(2,1)S(1)}, u32[]{:S(2)}, u32[]{:S(2)}) collective-permute-start(bf16[32,256]{1,0:T(8,128)(2,1)S(1)} %get-tuple-element.20.own_ref.near_ref), channel_id=1, source_target_pairs={{0,8},{8,0},{1,9},{9,1},{2,10},{10,2},{3,11},{11,3},{4,12},{12,4},... | collective-permute-start | bytes 49160 | tf_op jit(solution)/shard_map/ppermute | solution.py:48
  121.7 5.4 %collective-permute-done.2.other_ref = bf16[32,256]{1,0:T(8,128)(2,1)S(1)} collective-permute-done((bf16[32,256]{1,0:T(8,128)(2,1)S(1)}, bf16[32,256]{1,0:T(8,128)(2,1)S(1)}, u32[]{:S(2)}, u32[]{:S(2)}) %collective-permute-start.2) | collective-permute-done | bytes 16416 | tf_op jit(solution)/shard_map/ppermute | solution.py:48
  127.4 19.2 %all_to_all.59.row_ref = bf16[8,136,256]{2,1,0:T(8,128)(2,1)S(1)} all-to-all(bf16[8,136,256]{2,1,0:T(8,128)(2,1)S(1)} %shard_map.73), channel_id=1, replica_groups=mesh['row_0'=8,'row_1'=4,'col_0'=2,'col_1'=4,'col_2'=2] {'col_1','col_2'}, dimensions={0} | all-to-all | bytes 1114112 | tf_op jit(solution)/shard_map/all_to_all | solution.py:30
  147.7 7.8 %collective-permute-start.3 = (bf16[48,256]{1,0:T(8,128)(2,1)S(1)}, bf16[48,256]{1,0:T(8,128)(2,1)S(1)}, u32[]{:S(2)}, u32[]{:S(2)}) collective-permute-start(bf16[48,256]{1,0:T(8,128)(2,1)S(1)} %get-tuple-element.21.sent_ref), channel_id=1, source_target_pairs={{0,8},{8,0},{1,9},{9,1},{2,10},{10,2},{3,11},{11,3},{4,12},{12,4},... | collective-permute-start | bytes 73736 | tf_op jit(solution)/shard_map/ppermute | solution.py:48
  155.5 5.4 %collective-permute-done.3.far_ref = bf16[48,256]{1,0:T(8,128)(2,1)S(1)} collective-permute-done((bf16[48,256]{1,0:T(8,128)(2,1)S(1)}, bf16[48,256]{1,0:T(8,128)(2,1)S(1)}, u32[]{:S(2)}, u32[]{:S(2)}) %collective-permute-start.3) | collective-permute-done | bytes 24608 | tf_op jit(solution)/shard_map/ppermute | solution.py:48
  161.6 7.2 %all-to-all-start.9 = ((bf16[32,8,256]{2,1,0:T(8,128)(2,1)}), bf16[32,8,256]{2,1,0:T(8,128)(2,1)S(1)}, u32[]{:S(2)}, u32[]{:S(2)}) async-start(bf16[32,8,256]{2,1,0:T(8,128)(2,1)} %get-tuple-element.25), calls=%async_computation.9 | async-start | bytes 262144 | tf_op jit(solution)/shard_map/all_to_all | solution.py:30
  169.0 2.9 %cholesky.17 = f32[32,32]{1,0:T(8,128)S(1)} custom-call(f32[32,32]{1,0:T(8,128)S(1)} %fusion.3), custom_call_target="Cholesky" | custom-call | tf_op jit(solution)/shard_map/jit(cholesky)/cholesky | solution.py:334
  172.6 3.9 %all-to-all-done.9.bits_ref = bf16[32,8,256]{2,1,0:T(8,128)(2,1)S(1)} async-done(((bf16[32,8,256]{2,1,0:T(8,128)(2,1)}), bf16[32,8,256]{2,1,0:T(8,128)(2,1)S(1)}, u32[]{:S(2)}, u32[]{:S(2)}) %all-to-all-start.9) | async-done | bytes 131104 | tf_op jit(solution)/shard_map/all_to_all | solution.py:30
  176.5 3.4 %all-to-all-start.8 = ((bf16[4,128,256]{2,1,0:T(8,128)(2,1)}), bf16[4,128,256]{2,1,0:T(8,128)(2,1)S(1)}, u32[]{:S(2)}, u32[]{:S(2)}) async-start(bf16[4,128,256]{2,1,0:T(8,128)(2,1)} %get-tuple-element.24), calls=%async_computation.8 | async-start | bytes 524288 | tf_op jit(solution)/shard_map/all_to_all | solution.py:30
  180.6 2.4 %custom-call.6 = f32[1,32,32]{1,2,0:T(8,128)S(1)} custom-call(f32[1,32,32]{2,1,0:T(8,128)S(1)} %fusion), custom_call_target="InvertDiagBlocksLowerTriangular" | custom-call | tf_op jit(solution)/shard_map/triangular_solve | solution.py:335
  183.0 2.9 %all-to-all-done.8.mirror_ref = bf16[4,128,256]{2,1,0:T(8,128)(2,1)S(1)} async-done(((bf16[4,128,256]{2,1,0:T(8,128)(2,1)}), bf16[4,128,256]{2,1,0:T(8,128)(2,1)S(1)}, u32[]{:S(2)}, u32[]{:S(2)}) %all-to-all-start.8) | async-done | bytes 262176 | tf_op jit(solution)/shard_map/all_to_all | solution.py:30
  186.8 3.4 %all-to-all-start.10 = ((bf16[8,40,256]{2,1,0:T(8,128)(2,1)}), bf16[8,40,256]{2,1,0:T(8,128)(2,1)S(1)}, u32[]{:S(2)}, u32[]{:S(2)}) async-start(bf16[8,40,256]{2,1,0:T(8,128)(2,1)} %shard_map.76), calls=%async_computation.10 | async-start | bytes 327680 | tf_op jit(solution)/shard_map/all_to_all | solution.py:30
  191.2 9.6 %all-to-all-done.10.mirror_ref = bf16[8,40,256]{2,1,0:T(8,128)(2,1)S(1)} async-done(((bf16[8,40,256]{2,1,0:T(8,128)(2,1)}), bf16[8,40,256]{2,1,0:T(8,128)(2,1)S(1)}, u32[]{:S(2)}, u32[]{:S(2)}) %all-to-all-start.10) | async-done | bytes 163872 | tf_op jit(solution)/shard_map/all_to_all | solution.py:30
  (35 shorter events, 11.8 us)
Async XLA Ops:
  24.6 0.7 copy-start.2
  26.1 4.3 %copy-start.1 = (bf16[32,256]{1,0:T(8,128)(2,1)S(1)}, bf16[32,256]{1,0:T(8,128)(2,1)}, u32[]{:S(2)}) copy-start(bf16[32,256]{1,0:T(8,128)(2,1)} %near_ref.1) | copy-start | bytes 49156
  26.1 17.5 %copy-start = (bf16[1,1,4,256,256]{4,3,2,1,0:T(8,128)(2,1)S(1)}, bf16[1,1,4,256,256]{4,3,2,1,0:T(8,128)(2,1)}, u32[]{:S(2)}) copy-start(bf16[1,1,4,256,256]{4,3,2,1,0:T(8,128)(2,1)} %param.4) | copy-start | bytes 1572868
  26.1 17.5 %all-to-all-start.1 = ((bf16[4,264,256]{2,1,0:T(8,128)(2,1)}), bf16[4,264,256]{2,1,0:T(8,128)(2,1)S(1)}, u32[]{:S(2)}, u32[]{:S(2)}) async-start(bf16[4,264,256]{2,1,0:T(8,128)(2,1)} %shard_map.67), calls=%async_computation.1 | async-start | bytes 1081344 | tf_op jit(solution)/shard_map/all_to_all | solution.py:30
  30.4 13.2 %collective-permute-start = (bf16[32,256]{1,0:T(8,128)(2,1)S(1)}, bf16[32,256]{1,0:T(8,128)(2,1)S(1)}, u32[]{:S(2)}, u32[]{:S(2)}) collective-permute-start(bf16[32,256]{1,0:T(8,128)(2,1)S(1)} %copy-done.1), channel_id=1, source_target_pairs={{0,8},{8,0},{1,9},{9,1},{2,10},{10,2},{3,11},{11,3},{4,12},{12,4},... | collective-permute-start | bytes 49160 | tf_op jit(solution)/shard_map/ppermute | solution.py:48
  38.3 0.7 copy-start.4
  72.3 17.3 %all-to-all-start.4 = ((bf16[8,32,256]{2,1,0:T(8,128)(2,1)}), bf16[8,32,256]{2,1,0:T(8,128)(2,1)S(1)}, u32[]{:S(2)}, u32[]{:S(2)}) async-start(bf16[8,32,256]{2,1,0:T(8,128)(2,1)} %shard_map.70), calls=%async_computation.4 | async-start | bytes 262144 | tf_op jit(solution)/shard_map/all_to_all | solution.py:30
  76.4 13.2 %collective-permute-start.1 = (bf16[32,256]{1,0:T(8,128)(2,1)S(1)}, bf16[32,256]{1,0:T(8,128)(2,1)S(1)}, u32[]{:S(2)}, u32[]{:S(2)}) collective-permute-start(bf16[32,256]{1,0:T(8,128)(2,1)S(1)} %get-tuple-element.17), channel_id=1, source_target_pairs={{0,8},{8,0},{1,9},{9,1},{2,10},{10,2},{3,11},{11,3},{4,12},{12,4},... | collective-permute-start | bytes 49160 | tf_op jit(solution)/shard_map/ppermute | solution.py:48
  110.4 16.7 %all-to-all-start.6 = ((bf16[4,136,256]{2,1,0:T(8,128)(2,1)}), bf16[4,136,256]{2,1,0:T(8,128)(2,1)S(1)}, u32[]{:S(2)}, u32[]{:S(2)}) async-start(bf16[4,136,256]{2,1,0:T(8,128)(2,1)} %shard_map.72), calls=%async_computation.6 | async-start | bytes 557056 | tf_op jit(solution)/shard_map/all_to_all | solution.py:30
  113.9 13.2 %collective-permute-start.2 = (bf16[32,256]{1,0:T(8,128)(2,1)S(1)}, bf16[32,256]{1,0:T(8,128)(2,1)S(1)}, u32[]{:S(2)}, u32[]{:S(2)}) collective-permute-start(bf16[32,256]{1,0:T(8,128)(2,1)S(1)} %get-tuple-element.20.own_ref.near_ref), channel_id=1, source_target_pairs={{0,8},{8,0},{1,9},{9,1},{2,10},{10,2},{3,11},{11,3},{4,12},{12,4},... | collective-permute-start | bytes 49160 | tf_op jit(solution)/shard_map/ppermute | solution.py:48
  147.7 13.3 %collective-permute-start.3 = (bf16[48,256]{1,0:T(8,128)(2,1)S(1)}, bf16[48,256]{1,0:T(8,128)(2,1)S(1)}, u32[]{:S(2)}, u32[]{:S(2)}) collective-permute-start(bf16[48,256]{1,0:T(8,128)(2,1)S(1)} %get-tuple-element.21.sent_ref), channel_id=1, source_target_pairs={{0,8},{8,0},{1,9},{9,1},{2,10},{10,2},{3,11},{11,3},{4,12},{12,4},... | collective-permute-start | bytes 73736 | tf_op jit(solution)/shard_map/ppermute | solution.py:48
  161.6 14.9 %all-to-all-start.9 = ((bf16[32,8,256]{2,1,0:T(8,128)(2,1)}), bf16[32,8,256]{2,1,0:T(8,128)(2,1)S(1)}, u32[]{:S(2)}, u32[]{:S(2)}) async-start(bf16[32,8,256]{2,1,0:T(8,128)(2,1)} %get-tuple-element.25), calls=%async_computation.9 | async-start | bytes 262144 | tf_op jit(solution)/shard_map/all_to_all | solution.py:30
  176.5 9.4 %all-to-all-start.8 = ((bf16[4,128,256]{2,1,0:T(8,128)(2,1)}), bf16[4,128,256]{2,1,0:T(8,128)(2,1)S(1)}, u32[]{:S(2)}, u32[]{:S(2)}) async-start(bf16[4,128,256]{2,1,0:T(8,128)(2,1)} %get-tuple-element.24), calls=%async_computation.8 | async-start | bytes 524288 | tf_op jit(solution)/shard_map/all_to_all | solution.py:30
  186.8 14.0 %all-to-all-start.10 = ((bf16[8,40,256]{2,1,0:T(8,128)(2,1)}), bf16[8,40,256]{2,1,0:T(8,128)(2,1)S(1)}, u32[]{:S(2)}, u32[]{:S(2)}) async-start(bf16[8,40,256]{2,1,0:T(8,128)(2,1)} %shard_map.76), calls=%async_computation.10 | async-start | bytes 327680 | tf_op jit(solution)/shard_map/all_to_all | solution.py:30
  190.5 0.6 copy-start.3

commit v13 on v12

--- a/solution.py
+++ b/solution.py
@@ -92,6 +92,12 @@
     if isinstance(slot, int):
         return pl.ds(start + slot * length, length)
     return pl.ds(pl.multiple_of(start + slot * length, length), length)
+
+
+def start_kernel(block_ref, send_ref, own_ref):
+    own_ref[...] = block_ref[...]
+    for z in range(send_ref.shape[0]):
+        send_ref[z] = block_ref[...]
 
 
 def spread_kernel(by_z_ref, note_ref, out_ref):
@@ -266,7 +272,15 @@
     extra = send_z is not None
     table = pltpu.VMEM((y_count, ROWS, LANES), jnp.int32)
     if not extra:
-        send_z = jnp.broadcast_to(current[None], (z_count, vectors, size))
+        send_z, current = pl.pallas_call(
+            start_kernel,
+            out_shape=(
+                jax.ShapeDtypeStruct((z_count, vectors, size), BF16),
+                pltpu.VMEM((vectors, size), BF16),
+            ),
+            in_specs=[VMEM],
+            out_specs=(VMEM, VMEM),
+        )(current)
     by_z = exchange(send_z, Z_LO)
     other = partner(current)
     if extra:

time: 204 us -> 205 us (level)
  no operation moved by 1% of the time
where the time goes in v13:
time: 205 us; the launch traced here: 203 us
  blocking collectives  89.7 us (44%)
  starting transfers between devices  57.4 us (28%)
  waiting for transfers between devices  37.1 us (18%)
  Pallas kernels  8.69 us (4%)
  other arithmetic  6.77 us (3%)
    all_to_all x5, blocking collectives, exchange(): return lax.all_to_all(parts, axis, 0, 0, tiled=True)  89.7 us
    ppermute x4, starting transfers between devices, partner(): return lax.ppermute(value, Z_HI, [(0, 1), (1, 0)])  31.5 us
    all_to_all x6, starting transfers between devices, exchange(): return lax.all_to_all(parts, axis, 0, 0, tiled=True)  25.9 us
    ppermute x4, waiting for transfers between devices, partner(): return lax.ppermute(value, Z_HI, [(0, 1), (1, 0)])  20.6 us
    all_to_all x6, waiting for transfers between devices, exchange(): return lax.all_to_all(parts, axis, 0, 0, tiled=True)  16.5 us
    pallas_call x11, Pallas kernels, run(): pl.pallas_call(kernel, out_shape=tuple((out(shape, kind) for shape, kind...  7.31 us
  transfers between devices with their start and end apart: 10, of which 7 were waited for; matrix products, arithmetic and copies ran while one was open for 4% of the time, Pallas kernels for 0%

profile of v13, /device:TPU:1, one launch (start us, length us, event | category | flops | bytes accessed | tf_op | source)
XLA Modules:
  0.0 202.7 jit_solution(10742446358695025744)
XLA Ops:
  2.0 23.4 %all_to_all.55.by_z_ref = bf16[8,32,256]{2,1,0:T(8,128)(2,1)S(1)} all-to-all(bf16[8,32,256]{2,1,0:T(8,128)(2,1)} %get-tuple-element.18), channel_id=1, replica_groups=mesh['row_0'=8,'row_1'=4,'col_0'=2,'col_1'=4,'col_2'=2] {'row_0'}, dimensions={0} | all-to-all | bytes 262144 | tf_op jit(solution)/shard_map/all_to_all | solution.py:30
  26.9 4.3 %all-to-all-start.1 = ((bf16[4,264,256]{2,1,0:T(8,128)(2,1)}), bf16[4,264,256]{2,1,0:T(8,128)(2,1)S(1)}, u32[]{:S(2)}, u32[]{:S(2)}) async-start(bf16[4,264,256]{2,1,0:T(8,128)(2,1)} %shard_map.68), calls=%async_computation.1 | async-start | bytes 1081344 | tf_op jit(solution)/shard_map/all_to_all | solution.py:30
  31.2 7.9 %collective-permute-start = (bf16[32,256]{1,0:T(8,128)(2,1)S(1)}, bf16[32,256]{1,0:T(8,128)(2,1)S(1)}, u32[]{:S(2)}, u32[]{:S(2)}) collective-permute-start(bf16[32,256]{1,0:T(8,128)(2,1)S(1)} %get-tuple-element.19.own_ref.near_ref), channel_id=1, source_target_pairs={{0,8},{8,0},{1,9},{9,1},{2,10},{10,2},{3,11},{11,3},{4,12},{12,4},... | collective-permute-start | bytes 49160 | tf_op jit(solution)/shard_map/ppermute | solution.py:48
  39.9 4.5 %collective-permute-done.other_ref = bf16[32,256]{1,0:T(8,128)(2,1)S(1)} collective-permute-done((bf16[32,256]{1,0:T(8,128)(2,1)S(1)}, bf16[32,256]{1,0:T(8,128)(2,1)S(1)}, u32[]{:S(2)}, u32[]{:S(2)}) %collective-permute-start) | collective-permute-done | bytes 16416 | tf_op jit(solution)/shard_map/ppermute | solution.py:48
  44.7 17.7 %all_to_all.56.row_ref = bf16[8,128,256]{2,1,0:T(8,128)(2,1)S(1)} all-to-all(bf16[8,128,256]{2,1,0:T(8,128)(2,1)S(1)} %shard_map.69), channel_id=1, replica_groups=mesh['row_0'=8,'row_1'=4,'col_0'=2,'col_1'=4,'col_2'=2] {'col_1','col_2'}, dimensions={0} | all-to-all | bytes 1048576 | tf_op jit(solution)/shard_map/all_to_all | solution.py:30
  62.7 9.6 %all_to_all.57.mirror_ref = bf16[4,128,256]{2,1,0:T(8,128)(2,1)S(1)} all-to-all(bf16[4,128,256]{2,1,0:T(8,128)(2,1)S(1)} %get-tuple-element.22), channel_id=1, replica_groups=mesh['row_0'=8,'row_1'=4,'col_0'=2,'col_1'=4,'col_2'=2] {'row_1'}, dimensions={0} | all-to-all | bytes 524288 | tf_op jit(solution)/shard_map/all_to_all | solution.py:30
  73.1 4.1 %all-to-all-start.4 = ((bf16[8,32,256]{2,1,0:T(8,128)(2,1)}), bf16[8,32,256]{2,1,0:T(8,128)(2,1)S(1)}, u32[]{:S(2)}, u32[]{:S(2)}) async-start(bf16[8,32,256]{2,1,0:T(8,128)(2,1)} %shard_map.71), calls=%async_computation.4 | async-start | bytes 262144 | tf_op jit(solution)/shard_map/all_to_all | solution.py:30
  77.2 7.8 %collective-permute-start.1 = (bf16[32,256]{1,0:T(8,128)(2,1)S(1)}, bf16[32,256]{1,0:T(8,128)(2,1)S(1)}, u32[]{:S(2)}, u32[]{:S(2)}) collective-permute-start(bf16[32,256]{1,0:T(8,128)(2,1)S(1)} %get-tuple-element.21), channel_id=1, source_target_pairs={{0,8},{8,0},{1,9},{9,1},{2,10},{10,2},{3,11},{11,3},{4,12},{12,4},... | collective-permute-start | bytes 49160 | tf_op jit(solution)/shard_map/ppermute | solution.py:48
  85.1 5.3 %collective-permute-done.1.far_ref = bf16[32,256]{1,0:T(8,128)(2,1)S(1)} collective-permute-done((bf16[32,256]{1,0:T(8,128)(2,1)S(1)}, bf16[32,256]{1,0:T(8,128)(2,1)S(1)}, u32[]{:S(2)}, u32[]{:S(2)}) %collective-permute-start.1) | collective-permute-done | bytes 16416 | tf_op jit(solution)/shard_map/ppermute | solution.py:48
  90.6 19.8 %all_to_all.58.by_z_ref = bf16[8,40,256]{2,1,0:T(8,128)(2,1)S(1)} all-to-all(bf16[8,40,256]{2,1,0:T(8,128)(2,1)S(1)} %get-tuple-element.23), channel_id=1, replica_groups=mesh['row_0'=8,'row_1'=4,'col_0'=2,'col_1'=4,'col_2'=2] {'row_0'}, dimensions={0} | all-to-all | bytes 327680 | tf_op jit(solution)/shard_map/all_to_all | solution.py:30
  111.2 3.4 %all-to-all-start.6 = ((bf16[4,136,256]{2,1,0:T(8,128)(2,1)}), bf16[4,136,256]{2,1,0:T(8,128)(2,1)S(1)}, u32[]{:S(2)}, u32[]{:S(2)}) async-start(bf16[4,136,256]{2,1,0:T(8,128)(2,1)} %shard_map.73), calls=%async_computation.6 | async-start | bytes 557056 | tf_op jit(solution)/shard_map/all_to_all | solution.py:30
  114.7 7.9 %collective-permute-start.2 = (bf16[32,256]{1,0:T(8,128)(2,1)S(1)}, bf16[32,256]{1,0:T(8,128)(2,1)S(1)}, u32[]{:S(2)}, u32[]{:S(2)}) collective-permute-start(bf16[32,256]{1,0:T(8,128)(2,1)S(1)} %get-tuple-element.24.own_ref.near_ref), channel_id=1, source_target_pairs={{0,8},{8,0},{1,9},{9,1},{2,10},{10,2},{3,11},{11,3},{4,12},{12,4},... | collective-permute-start | bytes 49160 | tf_op jit(solution)/shard_map/ppermute | solution.py:48
  122.6 5.4 %collective-permute-done.2.other_ref = bf16[32,256]{1,0:T(8,128)(2,1)S(1)} collective-permute-done((bf16[32,256]{1,0:T(8,128)(2,1)S(1)}, bf16[32,256]{1,0:T(8,128)(2,1)S(1)}, u32[]{:S(2)}, u32[]{:S(2)}) %collective-permute-start.2) | collective-permute-done | bytes 16416 | tf_op jit(solution)/shard_map/ppermute | solution.py:48
  128.3 19.2 %all_to_all.59.row_ref = bf16[8,136,256]{2,1,0:T(8,128)(2,1)S(1)} all-to-all(bf16[8,136,256]{2,1,0:T(8,128)(2,1)S(1)} %shard_map.74), channel_id=1, replica_groups=mesh['row_0'=8,'row_1'=4,'col_0'=2,'col_1'=4,'col_2'=2] {'col_1','col_2'}, dimensions={0} | all-to-all | bytes 1114112 | tf_op jit(solution)/shard_map/all_to_all | solution.py:30
  148.5 7.8 %collective-permute-start.3 = (bf16[48,256]{1,0:T(8,128)(2,1)S(1)}, bf16[48,256]{1,0:T(8,128)(2,1)S(1)}, u32[]{:S(2)}, u32[]{:S(2)}) collective-permute-start(bf16[48,256]{1,0:T(8,128)(2,1)S(1)} %get-tuple-element.25.sent_ref), channel_id=1, source_target_pairs={{0,8},{8,0},{1,9},{9,1},{2,10},{10,2},{3,11},{11,3},{4,12},{12,4},... | collective-permute-start | bytes 73736 | tf_op jit(solution)/shard_map/ppermute | solution.py:48
  156.4 5.4 %collective-permute-done.3.far_ref = bf16[48,256]{1,0:T(8,128)(2,1)S(1)} collective-permute-done((bf16[48,256]{1,0:T(8,128)(2,1)S(1)}, bf16[48,256]{1,0:T(8,128)(2,1)S(1)}, u32[]{:S(2)}, u32[]{:S(2)}) %collective-permute-start.3) | collective-permute-done | bytes 24608 | tf_op jit(solution)/shard_map/ppermute | solution.py:48
  162.5 7.3 %all-to-all-start.9 = ((bf16[32,8,256]{2,1,0:T(8,128)(2,1)}), bf16[32,8,256]{2,1,0:T(8,128)(2,1)S(1)}, u32[]{:S(2)}, u32[]{:S(2)}) async-start(bf16[32,8,256]{2,1,0:T(8,128)(2,1)} %get-tuple-element.29), calls=%async_computation.9 | async-start | bytes 262144 | tf_op jit(solution)/shard_map/all_to_all | solution.py:30
  169.8 2.9 %cholesky.17 = f32[32,32]{1,0:T(8,128)S(1)} custom-call(f32[32,32]{1,0:T(8,128)S(1)} %fusion.3), custom_call_target="Cholesky" | custom-call | tf_op jit(solution)/shard_map/jit(cholesky)/cholesky | solution.py:348
  173.4 3.9 %all-to-all-done.9.bits_ref = bf16[32,8,256]{2,1,0:T(8,128)(2,1)S(1)} async-done(((bf16[32,8,256]{2,1,0:T(8,128)(2,1)}), bf16[32,8,256]{2,1,0:T(8,128)(2,1)S(1)}, u32[]{:S(2)}, u32[]{:S(2)}) %all-to-all-start.9) | async-done | bytes 131104 | tf_op jit(solution)/shard_map/all_to_all | solution.py:30
  177.3 3.4 %all-to-all-start.8 = ((bf16[4,128,256]{2,1,0:T(8,128)(2,1)}), bf16[4,128,256]{2,1,0:T(8,128)(2,1)S(1)}, u32[]{:S(2)}, u32[]{:S(2)}) async-start(bf16[4,128,256]{2,1,0:T(8,128)(2,1)} %get-tuple-element.28), calls=%async_computation.8 | async-start | bytes 524288 | tf_op jit(solution)/shard_map/all_to_all | solution.py:30
  181.4 2.4 %custom-call.6 = f32[1,32,32]{1,2,0:T(8,128)S(1)} custom-call(f32[1,32,32]{2,1,0:T(8,128)S(1)} %fusion), custom_call_target="InvertDiagBlocksLowerTriangular" | custom-call | tf_op jit(solution)/shard_map/triangular_solve | solution.py:349
  183.8 2.9 %all-to-all-done.8.mirror_ref = bf16[4,128,256]{2,1,0:T(8,128)(2,1)S(1)} async-done(((bf16[4,128,256]{2,1,0:T(8,128)(2,1)}), bf16[4,128,256]{2,1,0:T(8,128)(2,1)S(1)}, u32[]{:S(2)}, u32[]{:S(2)}) %all-to-all-start.8) | async-done | bytes 262176 | tf_op jit(solution)/shard_map/all_to_all | solution.py:30
  187.6 3.4 %all-to-all-start.10 = ((bf16[8,40,256]{2,1,0:T(8,128)(2,1)}), bf16[8,40,256]{2,1,0:T(8,128)(2,1)S(1)}, u32[]{:S(2)}, u32[]{:S(2)}) async-start(bf16[8,40,256]{2,1,0:T(8,128)(2,1)} %shard_map.77), calls=%async_computation.10 | async-start | bytes 327680 | tf_op jit(solution)/shard_map/all_to_all | solution.py:30
  192.0 9.6 %all-to-all-done.10.mirror_ref = bf16[8,40,256]{2,1,0:T(8,128)(2,1)S(1)} async-done(((bf16[8,40,256]{2,1,0:T(8,128)(2,1)}), bf16[8,40,256]{2,1,0:T(8,128)(2,1)S(1)}, u32[]{:S(2)}, u32[]{:S(2)}) %all-to-all-start.10) | async-done | bytes 163872 | tf_op jit(solution)/shard_map/all_to_all | solution.py:30
  (33 shorter events, 12.5 us)
Async XLA Ops:
  25.4 0.7 copy-start.1
  26.9 17.5 %copy-start = (bf16[1,1,4,256,256]{4,3,2,1,0:T(8,128)(2,1)S(1)}, bf16[1,1,4,256,256]{4,3,2,1,0:T(8,128)(2,1)}, u32[]{:S(2)}) copy-start(bf16[1,1,4,256,256]{4,3,2,1,0:T(8,128)(2,1)} %param.4) | copy-start | bytes 1572868
  26.9 17.5 %all-to-all-start.1 = ((bf16[4,264,256]{2,1,0:T(8,128)(2,1)}), bf16[4,264,256]{2,1,0:T(8,128)(2,1)S(1)}, u32[]{:S(2)}, u32[]{:S(2)}) async-start(bf16[4,264,256]{2,1,0:T(8,128)(2,1)} %shard_map.68), calls=%async_computation.1 | async-start | bytes 1081344 | tf_op jit(solution)/shard_map/all_to_all | solution.py:30
  31.2 13.2 %collective-permute-start = (bf16[32,256]{1,0:T(8,128)(2,1)S(1)}, bf16[32,256]{1,0:T(8,128)(2,1)S(1)}, u32[]{:S(2)}, u32[]{:S(2)}) collective-permute-start(bf16[32,256]{1,0:T(8,128)(2,1)S(1)} %get-tuple-element.19.own_ref.near_ref), channel_id=1, source_target_pairs={{0,8},{8,0},{1,9},{9,1},{2,10},{10,2},{3,11},{11,3},{4,12},{12,4},... | collective-permute-start | bytes 49160 | tf_op jit(solution)/shard_map/ppermute | solution.py:48
  39.2 0.7 copy-start.3
  73.1 17.3 %all-to-all-start.4 = ((bf16[8,32,256]{2,1,0:T(8,128)(2,1)}), bf16[8,32,256]{2,1,0:T(8,128)(2,1)S(1)}, u32[]{:S(2)}, u32[]{:S(2)}) async-start(bf16[8,32,256]{2,1,0:T(8,128)(2,1)} %shard_map.71), calls=%async_computation.4 | async-start | bytes 262144 | tf_op jit(solution)/shard_map/all_to_all | solution.py:30
  77.2 13.2 %collective-permute-start.1 = (bf16[32,256]{1,0:T(8,128)(2,1)S(1)}, bf16[32,256]{1,0:T(8,128)(2,1)S(1)}, u32[]{:S(2)}, u32[]{:S(2)}) collective-permute-start(bf16[32,256]{1,0:T(8,128)(2,1)S(1)} %get-tuple-element.21), channel_id=1, source_target_pairs={{0,8},{8,0},{1,9},{9,1},{2,10},{10,2},{3,11},{11,3},{4,12},{12,4},... | collective-permute-start | bytes 49160 | tf_op jit(solution)/shard_map/ppermute | solution.py:48
  111.2 16.7 %all-to-all-start.6 = ((bf16[4,136,256]{2,1,0:T(8,128)(2,1)}), bf16[4,136,256]{2,1,0:T(8,128)(2,1)S(1)}, u32[]{:S(2)}, u32[]{:S(2)}) async-start(bf16[4,136,256]{2,1,0:T(8,128)(2,1)} %shard_map.73), calls=%async_computation.6 | async-start | bytes 557056 | tf_op jit(solution)/shard_map/all_to_all | solution.py:30
  114.7 13.2 %collective-permute-start.2 = (bf16[32,256]{1,0:T(8,128)(2,1)S(1)}, bf16[32,256]{1,0:T(8,128)(2,1)S(1)}, u32[]{:S(2)}, u32[]{:S(2)}) collective-permute-start(bf16[32,256]{1,0:T(8,128)(2,1)S(1)} %get-tuple-element.24.own_ref.near_ref), channel_id=1, source_target_pairs={{0,8},{8,0},{1,9},{9,1},{2,10},{10,2},{3,11},{11,3},{4,12},{12,4},... | collective-permute-start | bytes 49160 | tf_op jit(solution)/shard_map/ppermute | solution.py:48
  148.5 13.3 %collective-permute-start.3 = (bf16[48,256]{1,0:T(8,128)(2,1)S(1)}, bf16[48,256]{1,0:T(8,128)(2,1)S(1)}, u32[]{:S(2)}, u32[]{:S(2)}) collective-permute-start(bf16[48,256]{1,0:T(8,128)(2,1)S(1)} %get-tuple-element.25.sent_ref), channel_id=1, source_target_pairs={{0,8},{8,0},{1,9},{9,1},{2,10},{10,2},{3,11},{11,3},{4,12},{12,4},... | collective-permute-start | bytes 73736 | tf_op jit(solution)/shard_map/ppermute | solution.py:48
  162.5 14.9 %all-to-all-start.9 = ((bf16[32,8,256]{2,1,0:T(8,128)(2,1)}), bf16[32,8,256]{2,1,0:T(8,128)(2,1)S(1)}, u32[]{:S(2)}, u32[]{:S(2)}) async-start(bf16[32,8,256]{2,1,0:T(8,128)(2,1)} %get-tuple-element.29), calls=%async_computation.9 | async-start | bytes 262144 | tf_op jit(solution)/shard_map/all_to_all | solution.py:30
  177.3 9.4 %all-to-all-start.8 = ((bf16[4,128,256]{2,1,0:T(8,128)(2,1)}), bf16[4,128,256]{2,1,0:T(8,128)(2,1)S(1)}, u32[]{:S(2)}, u32[]{:S(2)}) async-start(bf16[4,128,256]{2,1,0:T(8,128)(2,1)} %get-tuple-element.28), calls=%async_computation.8 | async-start | bytes 524288 | tf_op jit(solution)/shard_map/all_to_all | solution.py:30
  187.6 14.0 %all-to-all-start.10 = ((bf16[8,40,256]{2,1,0:T(8,128)(2,1)}), bf16[8,40,256]{2,1,0:T(8,128)(2,1)S(1)}, u32[]{:S(2)}, u32[]{:S(2)}) async-start(bf16[8,40,256]{2,1,0:T(8,128)(2,1)} %shard_map.77), calls=%async_computation.10 | async-start | bytes 327680 | tf_op jit(solution)/shard_map/all_to_all | solution.py:30
  191.4 0.6 copy-start.2
